TPU v7x, 32 devices: a whole 2x2x4 slice. The times are simulated.
32 devices in a mesh: wide: 8 (over z, y), narrow: 4 (over x, core).
Axes of the slice: x: 2, y: 2, z: 4, core: 2. Of those that a mesh axis runs over, the one named last changes fastest.
Arguments:
- mobility: float32 [128, 64, 256], P('wide', 'narrow'), may hold values from 0.2 to 5
- sav_vector: float32 [128, 64, 256], P('wide', 'narrow'), may hold values from -8 to 8
- cotangent: float32 [128, 64, 256], P('wide', 'narrow'), may hold values from -8 to 8
Outputs:
- adjoint: float32 [128, 64, 256], P('wide', 'narrow')
All inputs are finite; a program needn't handle non-finite values.
Results may differ from a plain program's by a relative error of at most 0.0019.
Values sent between devices are 32-bit elements; how exact they have to be, the bound alone decides.
A program may use at most 128 MiB of HBM per device.

v0:
```python
import functools
import jax
import jax.numpy as jnp
from jax import lax
from jax.experimental import pallas as pl
from jax.experimental.pallas import tpu as pltpu
from jax.sharding import PartitionSpec as P

DAMPING = 0.8
KEEP = 1.0 - DAMPING
BASE_TAU = 16.0
H0 = 4
H1 = 5
PAD = 2
MESH = pl.DeviceIdType.MESH
F32 = jnp.float32
SIDES = [(-1, 0), (1, 0), (0, -1), (0, 1), (-1, -1), (-1, 1), (1, -1), (1, 1)]
OPPOSITE = [1, 0, 3, 2, 7, 6, 5, 4]


def iota(shape, dim):
    return lax.broadcasted_iota(jnp.int32, shape, dim)


def shift(value, amount, axis):
    return pltpu.roll(value, amount % value.shape[axis], axis)


def squeeze_matrix(rows, cols, offset=0):
    i, j = iota((rows, cols), 0), iota((rows, cols), 1)
    k = i - 2 * (j - offset)
    return jnp.where((k == 0) | (k == 1), 1.0, 0.0).astype(F32)


def spread_matrix(rows, cols):
    i, j = iota((rows, cols), 0), iota((rows, cols), 1)
    k = j - 2 * i
    return jnp.where((k == 0) | (k == 1), 1.0, 0.0).astype(F32)


def mm(a, b):
    return jnp.dot(a, b, precision=lax.Precision.HIGHEST, preferred_element_type=F32)


def rounded(x):
    return x.astype(jnp.bfloat16).astype(F32)


def slabs(lo, hi, chunk, body):
    def step(i, _):
        for k in range(chunk):
            body(lo + i * chunk + k)
        return 0

    lax.fori_loop(0, (hi - lo) // chunk, step, 0)


def build(m, cx, cy, cz, rd, d, lo, hi, tau, seg, chunk):
    shape = m.shape[1:]
    row = iota(shape, 0)
    lane = lax.rem(iota(shape, 1), seg)
    last_row, first_row = row == shape[0] - 1, row == 0
    last_lane, first_lane = lane == seg - 1, lane == 0
    half = 0.5 * tau

    def body(a):
        own = m[a]
        xp, xm = m[a + 1], m[a - 1]
        yp = jnp.where(last_row, 0.0, shift(own, -1, 0))
        ym = jnp.where(first_row, 0.0, shift(own, 1, 0))
        zp = jnp.where(last_lane, 0.0, shift(own, -1, 1))
        zm = jnp.where(first_lane, 0.0, shift(own, 1, 1))
        total = 1.0
        for other, ref in ((xp, cx), (xm, None), (yp, cy), (ym, None), (zp, cz), (zm, None)):
            face = rounded(half * (own + other))
            total = total + face
            if ref is not None:
                ref[a] = jnp.where(jnp.minimum(own, other) > 0.0, face, 0.0)
        rd[a] = DAMPING / total
        if d is not None:
            d[a] = total

    slabs(lo, hi, chunk, body)


def pairs(lo, hi):
    return 2 - (hi - lo) % 2


def neighbours(v, a, cx, cy, cz):
    own = v[a]
    cya, cza = cy[a], cz[a]
    total = cx[a] * v[a + 1] + cx[a - 1] * v[a - 1]
    total = total + (cya * shift(own, -1, 0) + shift(cya * own, 1, 0))
    total = total + (cza * shift(own, -1, 1) + shift(cza * own, 1, 1))
    return own, total


def sweep(vin, vout, r, ops, lo, hi, chunk):
    cx, cy, cz, rd, d = ops

    def body(a):
        for vi, vo, ri in zip(vin, vout, r):
            own, t = neighbours(vi, a, cx, cy, cz)
            vo[a] = KEEP * own + rd[a] * (ri[a] + t)

    slabs(lo, hi, chunk, body)


def residual(vi, ri, a, ops):
    cx, cy, cz, rd, d = ops
    own, t = neighbours(vi, a, cx, cy, cz)
    diag = d[a] if d is not None else DAMPING / rd[a]
    return own, ri[a] + t - diag * own


def fold(x):
    total = None
    for i in range(x.shape[0] // 8):
        for j in range(x.shape[1] // 128):
            part = x[8 * i : 8 * i + 8, 128 * j : 128 * j + 128]
            total = part if total is None else total + part
    return total


def kernel(nw, nn, bx, by, nz, m_ref, s_ref, c_ref, out_ref,
           m0, cx0, cy0, cz0, rd0, d0, rs0, rc0, us0, uc0, vs0, vc0,
           rx, yp, ry, cp, rcn,
           m1, cx1, cy1, cz1, rd1, d1, r1, u1, v1, w1,
           cx2, cy2, cz2, rd2, r2, u2, v2,
           cx3, cy3, cz3, rd3, r3, u3, v3,
           cx4, cy4, cz4, rd4, r4, u4, v4,
           t0, t0y, t1, t1y, sm2, sr2, sp2, gm, gr, gp, pb, pbs, t2, t2y, f1, f1p, f0a, f0b,
           e0s, e0r, m1s, m1r, e1s, e1r,
           ams, amr, bms, bmr, ars, arr, aps, apr, brs, brr, bps, bpr):
    iw, ino = lax.axis_index("wide"), lax.axis_index("narrow")
    b1x, b1y, z1 = bx // 2, by // 2, nz // 2
    b2x, b2y, z2 = bx // 4, by // 4, nz // 4
    x2, x3, x4 = nw * b2x, nw * b2x // 2, nw * b2x // 4
    xs0 = bx + 2 * H0
    there = []
    for dx, dy in SIDES:
        ok = None
        for cond, on in ((iw > 0, dx < 0), (iw < nw - 1, dx > 0), (ino > 0, dy < 0), (ino < nn - 1, dy > 0)):
            if on:
                ok = cond if ok is None else jnp.logical_and(ok, cond)
        there.append(ok)

    def peer(side):
        return (iw + SIDES[side][0], ino + SIDES[side][1])

    barrier = pltpu.get_barrier_semaphore()

    def greet(j, _):
        pl.semaphore_signal(barrier, inc=1, device_id=(lax.rem(iw + j, nw), ino), device_id_type=MESH)
        return 0

    lax.fori_loop(1, nw, greet, 0)
    for j in range(1, nn):
        pl.semaphore_signal(barrier, inc=1, device_id=(iw, lax.rem(ino + j, nn)), device_id_type=MESH)
    for k in range(4, 8):
        @pl.when(there[k])
        def _():
            pl.semaphore_signal(barrier, inc=1, device_id=peer(k), device_id_type=MESH)

    for side, (m_lo, r_lo) in enumerate(((0, 0), (by - 4, by - 3))):
        for k in range(4):
            yp[side, k] = m_ref[:, m_lo + k, :]
        for k in range(3):
            yp[side, 4 + k] = s_ref[:, r_lo + k, :]
            yp[side, 7 + k] = c_ref[:, r_lo + k, :]
    for k in range(4, 8):
        dx, dy = SIDES[k]
        m_x, m_y = (0 if dx < 0 else bx - 3), (0 if dy < 0 else by - 3)
        r_x, r_y = (0 if dx < 0 else bx - 2), (0 if dy < 0 else by - 2)
        for i in range(3):
            cp[k - 4, 3 * i : 3 * i + 3, :] = m_ref[m_x + i, m_y : m_y + 3, :]
        for i in range(2):
            cp[k - 4, 9 + 2 * i : 11 + 2 * i, :] = s_ref[r_x + i, r_y : r_y + 2, :]
            cp[k - 4, 13 + 2 * i : 15 + 2 * i, :] = c_ref[r_x + i, r_y : r_y + 2, :]

    beside_x = jnp.minimum(iw, 1) + jnp.minimum(nw - 1 - iw, 1)
    beside_y = jnp.minimum(ino, 1) + jnp.minimum(nn - 1 - ino, 1)
    pl.semaphore_wait(barrier, nw + nn - 2 + beside_x * beside_y)

    def remote(src, dst, ssem, rsem, dev):
        return pltpu.make_async_remote_copy(src_ref=src, dst_ref=dst, send_sem=ssem, recv_sem=rsem,
                                            device_id=dev, device_id_type=MESH)

    def e0_copies(side, recv, wave=0):
        other = OPPOSITE[side]
        land = side if recv else other
        dev = peer(side)
        if side < 2:
            out = []
            at = 0
            for n, (ref, width) in enumerate(((m_ref, 4), (s_ref, 3), (c_ref, 3))):
                lo = 0 if side == 0 else bx - width
                skip = width - 1 if side == 0 else 0
                first = 0 if side == 0 else 1
                if wave == 1:
                    out.append(remote(ref.at[lo + skip : lo + skip + 1], rx.at[land, at + skip : at + skip + 1],
                                      e0s.at[side, 3 + n], e0r.at[land, 3 + n], dev))
                else:
                    out.append(remote(ref.at[lo + first : lo + first + width - 1],
                                      rx.at[land, at + first : at + first + width - 1],
                                      e0s.at[side, n], e0r.at[land, n], dev))
                at += width
            return out
        if side < 4:
            return [remote(yp.at[side - 2], ry.at[land - 2], e0s.at[side, 0], e0r.at[land, 0], dev)]
        return [remote(cp.at[side - 4], rcn.at[land - 4], e0s.at[side, 0], e0r.at[land, 0], dev)]

    def box1(side, sending, width):
        dx, dy = SIDES[side]
        own = H1
        if sending:
            xlo, w = (own, width) if dx < 0 else ((own + b1x - width, width) if dx > 0 else (own, b1x))
            ylo = b1y
        else:
            xlo, w = (own - width, width) if dx < 0 else ((own + b1x, width) if dx > 0 else (own, b1x))
            ylo = b1y * (1 + dy)
        return xlo, w, ylo

    def level1_copies(ref, ssem, rsem, side, recv, width):
        land = side if recv else OPPOSITE[side]
        sx, w, sy = box1(side, True, width)
        tx, _, ty = box1(land, False, width)
        return [remote(ref.at[v, sx : sx + w, sy : sy + b1y], ref.at[v, tx : tx + w, ty : ty + b1y],
                       ssem.at[side, v], rsem.at[land, v], peer(side)) for v in range(ref.shape[0])]

    def each(fn, act, sides=range(8)):
        for side in sides:
            @pl.when(there[side])
            def _():
                for copy in fn(side):
                    act(copy)

    def start(copy):
        copy.start()

    each(lambda k: e0_copies(k, False), start, (0, 1, 4, 5, 6, 7, 2, 3))

    zc0 = squeeze_matrix(nz, z1)
    zc1 = squeeze_matrix(z1, z1)
    zc1b = squeeze_matrix(z1, z1, z2)
    zr = spread_matrix(z1, z1)

    def pair_rows(flat, half_rows):
        return flat[pl.ds(0, half_rows, stride=2), :] + flat[pl.ds(1, half_rows, stride=2), :]

    for i in range(b1x):
        t0[0, i * by : (i + 1) * by, :] = m_ref[2 * i] + m_ref[2 * i + 1]
    t0y[...] = mm(t0[0], zc0)
    mob1 = 0.125 * pair_rows(t0y, b1x * b1y)
    for i in range(b1x):
        m1[0, H1 + i, b1y : 2 * b1y, :] = mob1[i * b1y : (i + 1) * b1y]

    def clear1(ref, width):
        for side in range(8):
            xlo, w, ylo = box1(side, False, width)
            @pl.when(jnp.logical_not(there[side]))
            def _():
                ref[:, xlo : xlo + w, ylo : ylo + b1y, :] = jnp.zeros((ref.shape[0], w, b1y, z1), F32)

    clear1(m1, 5)
    clear1(r1, 4)
    each(lambda k: level1_copies(m1, m1s, m1r, k, False, 5), start)
    for i in range(b2x):
        t1[0, i * b1y : (i + 1) * b1y, :] = mob1[2 * i * b1y : (2 * i + 1) * b1y] + mob1[(2 * i + 1) * b1y : (2 * i + 2) * b1y]
    t1y[...] = mm(t1[0], zc1 + zc1b)
    mob2 = 0.125 * pair_rows(t1y, b2x * b2y)
    sm2[...] = mob2
    gm[ino, iw] = mob2

    def wide_copy(src, dst_ref, ssem, rsem, j, recv):
        to = lax.rem(iw + j, nw)
        if recv:
            return remote(src, dst_ref(to), ssem.at[j], rsem.at[to], (to, ino))
        return remote(src, dst_ref(iw), ssem.at[j], rsem.at[iw], (to, ino))

    def over_wide(src, dst_ref, ssem, rsem, what):
        def step(j, _):
            copy = wide_copy(src, dst_ref, ssem, rsem, j, what == "recv")
            if what == "start":
                copy.start()
            elif what == "recv":
                copy.wait_recv()
            else:
                copy.wait_send()
            return 0

        lax.fori_loop(1, nw, step, 0)

    def over_narrow(src, dst_ref, ssem, rsem, what):
        for j in range(1, nn):
            to = lax.rem(ino + j, nn)
            if what == "recv":
                remote(src, dst_ref(to), ssem.at[j], rsem.at[to], (iw, to)).wait_recv()
            else:
                copy = remote(src, dst_ref(ino), ssem.at[j], rsem.at[ino], (iw, to))
                if what == "start":
                    copy.start()
                else:
                    copy.wait_send()

    gather_m = (sm2, lambda w: gm.at[ino, w], ams, amr)
    spread_m = (gm.at[ino], lambda n: gm.at[n], bms, bmr)
    gather_r = (sr2, lambda w: gr.at[ino, w], ars, arr)
    gather_p = (sp2, lambda w: gp.at[w], aps, apr)
    spread_r = (gr.at[ino], lambda n: gr.at[n], brs, brr)
    spread_p = (pb, lambda n: pbs.at[n], bps, bpr)
    each(lambda k: e0_copies(k, False, 1), start, (0, 1))
    over_wide(*gather_m, "start")

    blank = jnp.zeros((H0, m0.shape[1], nz), F32)
    for ref, src in ((m0, m_ref), (rs0, s_ref), (rc0, c_ref)):
        ref[0:H0] = blank
        ref[H0 + bx :] = blank

        def put(i, _):
            ref[H0 + i, H0 : H0 + by, :] = src[i]
            return 0

        lax.fori_loop(0, bx, put, 0)
    for ref in (u2, v2, u3, v3, u4, v4):
        zero = jnp.zeros(ref.shape[1:], F32)
        for a in (0, 1, ref.shape[0] - 2, ref.shape[0] - 1):
            ref[a] = zero
    for ref in (cx2, cx3, cx4):
        ref[PAD - 1] = jnp.zeros(ref.shape[1:], F32)
    for k in range(2):
        @pl.when(jnp.logical_not(there[k]))
        def _():
            rx[k] = jnp.zeros(rx.shape[1:], F32)

        @pl.when(jnp.logical_not(there[2 + k]))
        def _():
            ry[k] = jnp.zeros(ry.shape[1:], F32)
    for k in range(4):
        @pl.when(jnp.logical_not(there[4 + k]))
        def _():
            rcn[k] = jnp.zeros(rcn.shape[1:], F32)

    def landed(copy):
        copy.wait_recv()

    each(lambda k: e0_copies(k, True), landed, (2, 3))
    fields = ((m0, 0, 4), (rs0, 4, 3), (rc0, 7, 3))
    for ref, at, width in fields:
        for i in range(width):
            ref[H0 : H0 + bx, H0 - width + i, :] = ry[0, at + i]
            ref[H0 : H0 + bx, H0 + by + i, :] = ry[1, at + i]

    ops0 = (cx0, cy0, cz0, rd0, d0)

    def first0(a):
        us0[a] = rd0[a] * rs0[a]
        uc0[a] = rd0[a] * rc0[a]

    def start0(lo, hi, v_lo, v_hi):
        build(m0, cx0, cy0, cz0, rd0, d0, lo, hi, BASE_TAU, nz, pairs(lo, hi))
        slabs(lo, hi, 1, first0)
        if v_hi > v_lo:
            sweep((us0, uc0), (vs0, vc0), (rs0, rc0), ops0, v_lo, v_hi, pairs(v_lo, v_hi))

    start0(H0 + 1, H0 + bx - 1, H0 + 2, H0 + bx - 2)

    def down0(i, carry):
        num, den = carry
        sums = []
        for k in range(2):
            a = H0 + 2 * i + k
            vs, es = residual(vs0, rs0, a, ops0)
            vc, ec = residual(vc0, rc0, a, ops0)
            rs = rs0[a]
            num = num + fold((ec * vs + vc * rs)[H0 : H0 + by])
            den = den + fold((es * vs + vs * rs)[H0 : H0 + by])
            sums.append((es, ec))
        at = pl.ds(pl.multiple_of(i * by, by), by)
        t0[0, at, :] = (sums[0][0] + sums[1][0])[H0 : H0 + by]
        t0[1, at, :] = (sums[0][1] + sums[1][1])[H0 : H0 + by]
        return num, den

    zero8 = jnp.zeros((8, 128), F32)
    part0 = lax.fori_loop(2, b1x - 2, down0, (zero8, zero8))

    each(lambda k: e0_copies(k, True), landed, (0, 1, 4, 5, 6, 7))
    for ref, at, width in fields:
        for i in range(width - 1):
            ref[H0 - width + 1 + i, H0 : H0 + by, :] = rx[0, at + 1 + i]
            ref[H0 + bx + i, H0 : H0 + by, :] = rx[1, at + i]
    for k in range(4):
        dx, dy = SIDES[4 + k]
        m_x, m_y = (H0 - 3 if dx < 0 else H0 + bx), (H0 - 3 if dy < 0 else H0 + by)
        r_x, r_y = (H0 - 2 if dx < 0 else H0 + bx), (H0 - 2 if dy < 0 else H0 + by)
        for i in range(3):
            m0[m_x + i, m_y : m_y + 3, :] = rcn[k, 3 * i : 3 * i + 3, :]
        for i in range(2):
            rs0[r_x + i, r_y : r_y + 2, :] = rcn[k, 9 + 2 * i : 11 + 2 * i, :]
            rc0[r_x + i, r_y : r_y + 2, :] = rcn[k, 13 + 2 * i : 15 + 2 * i, :]
    for lo, hi, v_lo, v_hi in ((2, H0 + 1, 3, H0 + 2), (H0 + bx - 1, xs0 - 2, H0 + bx - 2, xs0 - 3)):
        build(m0, cx0, cy0, cz0, rd0, d0, lo, hi, BASE_TAU, nz, pairs(lo, hi))
        slabs(lo, hi, 1, first0)
        sweep((us0, uc0), (vs0, vc0), (rs0, rc0), ops0, v_lo, v_hi, pairs(v_lo, v_hi))
    part0 = lax.fori_loop(0, 2, down0, part0)
    num0, den0 = lax.fori_loop(b1x - 2, b1x, down0, part0)
    for v in range(2):
        t0y[...] = mm(t0[v], zc0)
        coarse = 0.125 * pair_rows(t0y, b1x * b1y)
        for i in range(b1x):
            r1[v, H1 + i, b1y : 2 * b1y, :] = coarse[i * b1y : (i + 1) * b1y]
    each(lambda k: level1_copies(r1, e1s, e1r, k, False, 4), start)

    each(lambda k: e0_copies(k, True, 1), landed, (0, 1))
    for ref, at, width in fields:
        ref[H0 - width, H0 : H0 + by, :] = rx[0, at]
        ref[H0 + bx + width - 1, H0 : H0 + by, :] = rx[1, at + width - 1]
    for lo, v_lo in ((1, 2), (xs0 - 2, xs0 - 3)):
        start0(lo, lo + 1, v_lo, v_lo + 1)
    each(lambda k: level1_copies(m1, m1s, m1r, k, True, 5), lambda c: c.wait_recv())
    ops1 = (cx1, cy1, cz1, rd1, d1)
    build(m1.at[0], cx1, cy1, cz1, rd1, d1, 1, b1x + 2 * H1 - 1, BASE_TAU / 4, z1, 2)
    over_wide(*gather_m, "recv")
    over_narrow(*spread_m, "start")

    each(lambda k: level1_copies(r1, e1s, e1r, k, True, 4), lambda c: c.wait_recv())
    rr1 = (r1.at[0], r1.at[1])
    uu1 = (u1.at[0], u1.at[1])
    vv1 = (v1.at[0], v1.at[1])

    def first1(a):
        for v in range(2):
            u1[v, a] = rd1[a] * r1[v, a]

    slabs(1, b1x + 2 * H1 - 1, 2, first1)
    sweep(uu1, vv1, rr1, ops1, 2, b1x + 2 * H1 - 2, 2)
    num1, den1 = zero8, zero8
    own_y = slice(b1y, 2 * b1y)
    for i in range(b2x):
        pair = []
        for k in range(2):
            a = H1 + 2 * i + k
            vs, es = residual(vv1[0], rr1[0], a, ops1)
            vc, ec = residual(vv1[1], rr1[1], a, ops1)
            rs = r1[0, a]
            num1 = num1 + fold((ec * vs + vc * rs)[own_y])
            den1 = den1 + fold((es * vs + vs * rs)[own_y])
            pair.append((es, ec))
        for v in range(2):
            t1[v, i * b1y : (i + 1) * b1y, :] = (pair[0][v] + pair[1][v])[own_y]
    t1y[...] = mm(t1[0], zc1) + mm(t1[1], zc1b)
    own2 = 0.125 * pair_rows(t1y, b2x * b2y)
    sr2[...] = own2
    gr[ino, iw] = own2
    num_row = jnp.sum(num0 + 8.0 * num1, axis=0, keepdims=True)
    den_row = jnp.sum(den0 + 8.0 * den1, axis=0, keepdims=True)
    row8 = iota((8, 128), 0)
    part = jnp.where(row8 == 0, num_row, jnp.where(row8 == 1, den_row, 0.0))
    sp2[...] = part
    gp[iw] = part
    over_wide(*gather_r, "start")
    over_wide(*gather_p, "start")

    over_narrow(*spread_m, "recv")

    def unpack(src, dst):
        def step(w, _):
            for n in range(nn):
                for i in range(b2x):
                    dst[PAD + w * b2x + i, n * b2y : (n + 1) * b2y, :] = src[n, w, i * b2y : (i + 1) * b2y, :]
            return 0

        lax.fori_loop(0, nw, step, 0)

    unpack(gm, v2)
    build(v2, cx2, cy2, cz2, rd2, None, PAD, PAD + x2, BASE_TAU / 16, z2, 8)

    def coarsen_pairs(get, xc, rows, dst):
        half = rows // 2

        def step(g, _):
            for k in range(4):
                a = PAD + 2 * (4 * g + k)
                t2[k * rows : (k + 1) * rows, :] = get(a) + get(a + 1)
            t2y[0 : 4 * rows, :] = mm(t2[0 : 4 * rows, :], zc1)
            flat = 0.125 * (t2y[pl.ds(0, 4 * half, stride=2), :] + t2y[pl.ds(1, 4 * half, stride=2), :])
            for k in range(4):
                dst[PAD + 4 * g + k, 0:half, :] = flat[k * half : (k + 1) * half]
            return 0

        lax.fori_loop(0, xc // 4, step, 0)

    v4[...] = jnp.zeros(v4.shape, F32)
    r4[...] = jnp.zeros(r4.shape, F32)
    coarsen_pairs(lambda a: v2[a], x3, v2.shape[1], v3)
    build(v3, cx3, cy3, cz3, rd3, None, PAD, PAD + x3, BASE_TAU / 64, z2 // 2, 4)
    coarsen_pairs(lambda a: v3[a], x4, v3.shape[1], v4)
    build(v4, cx4, cy4, cz4, rd4, None, PAD, PAD + x4, BASE_TAU / 256, z2 // 4, 4)

    over_wide(*gather_r, "recv")
    over_narrow(*spread_r, "start")
    over_wide(*gather_p, "recv")
    total = gp[0]
    if nw <= 16:
        for w in range(1, nw):
            total = total + gp[w]
    else:
        total = lax.fori_loop(1, nw, lambda w, acc: acc + gp[w], total)
    pb[...] = total
    over_narrow(*spread_p, "start")
    over_narrow(*spread_r, "recv")
    unpack(gr, r2)

    ops2 = (cx2, cy2, cz2, rd2, None)
    ops3 = (cx3, cy3, cz3, rd3, None)
    ops4 = (cx4, cy4, cz4, rd4, None)

    def down(u, v, r, ops, xc):
        def first(a):
            u[a] = ops[3][a] * r[a]

        slabs(PAD, PAD + xc, 4, first)
        sweep((u,), (v,), (r,), ops, PAD, PAD + xc, 8)

    def up(v, coarse, xc, rows):
        half = rows // 2

        def step(g, _):
            for k in range(4):
                t2[8 * k : 8 * k + 8, :] = coarse[PAD + 4 * g + k]
            wide_rows = mm(t2[0:32, :], zr)
            t2y[pl.ds(0, 32, stride=2), :] = wide_rows
            t2y[pl.ds(1, 32, stride=2), :] = wide_rows
            for k in range(4):
                add = t2y[16 * k : 16 * k + rows, :]
                a = PAD + 2 * (4 * g + k)
                v[a] = v[a] + add
                v[a + 1] = v[a + 1] + add
            return 0

        lax.fori_loop(0, xc // 4, step, 0)

    down(u2, v2, r2, ops2, x2)
    coarsen_pairs(lambda a: residual(v2, r2, a, ops2)[1], x3, v2.shape[1], r3)
    down(u3, v3, r3, ops3, x3)
    coarsen_pairs(lambda a: residual(v3, r3, a, ops3)[1], x4, v3.shape[1], r4)
    down(u4, v4, r4, ops4, x4)
    up(v3, v4, x4, v3.shape[1])
    sweep((v3,), (u3,), (r3,), ops3, PAD, PAD + x3, 8)
    sweep((u3,), (v3,), (r3,), ops3, PAD, PAD + x3, 8)
    up(v2, v3, x3, v2.shape[1])
    sweep((v2,), (u2,), (r2,), ops2, PAD, PAD + x2, 8)
    sweep((u2,), (v2,), (r2,), ops2, PAD, PAD + x2, 8)

    low = iota(v2.shape[1:], 1) < z2

    def dots(i, carry):
        num, den = carry
        for k in range(4):
            a = PAD + 4 * i + k
            both = jnp.where(low, v2[a], 0.0)
            den = den + fold(both * r2[a])
            num = num + fold(both * shift(r2[a], z2, 1))
        return num, den

    num2, den2 = lax.fori_loop(0, x2 // 4, dots, (zero8, zero8))
    over_narrow(*spread_p, "recv")
    whole = total
    for j in range(1, nn):
        whole = whole + pbs[lax.rem(ino + j, nn)]
    num = jnp.sum(jnp.where(row8 == 0, whole, 0.0) + 64.0 * num2)
    den = jnp.sum(jnp.where(row8 == 1, whole, 0.0) + 64.0 * den2)
    ratio = (jnp.full((8, 128), num) / (1.0 + jnp.full((8, 128), den)))[0:1, :]

    rows2 = v2.shape[1]
    full_y = 2 * rows2
    for i in range(b2x + 4):
        e = v2[PAD + iw * b2x - 2 + i]
        f1[i * rows2 : (i + 1) * rows2, :] = shift(e, z2, 1) - ratio * e
    fine = mm(f1[...], zr)
    for i in range(b2x + 4):
        part = fine[i * rows2 : (i + 1) * rows2]
        f1p[i, 0:b1y, :] = jnp.zeros((b1y, z1), F32)
        f1p[i, b1y + full_y : 2 * b1y + full_y, :] = jnp.zeros((b1y, z1), F32)
        f1p[i, pl.ds(b1y, rows2, stride=2), :] = part
        f1p[i, pl.ds(b1y + 1, rows2, stride=2), :] = part
    window = pl.ds(pl.multiple_of(ino * b1y, 8), 3 * b1y)
    for a in range(2, b1x + 2 * H1 - 2):
        i = (a - H1) // 2 + 2
        u1[0, a] = v1[1, a] - ratio * v1[0, a] + f1p[i, window, :]
        w1[a] = r1[1, a] - ratio * r1[0, a]
    sweep((u1.at[0],), (u1.at[1],), (w1,), ops1, 3, b1x + 2 * H1 - 3, 2)
    sweep((u1.at[1],), (u1.at[0],), (w1,), ops1, 4, b1x + 2 * H1 - 4, 2)

    rows1 = 3 * b1y
    zr0 = spread_matrix(z1, nz)
    ratio0 = jnp.concatenate([ratio] * (nz // 128), axis=1)
    for i in range(b1x + 2):
        part = mm(u1[0, H1 - 1 + i], zr0)
        for ref, lanes in ((f0a, slice(0, 128)), (f0b, slice(128, 256))):
            ref[i, pl.ds(0, rows1, stride=2), :] = part[:, lanes]
            ref[i, pl.ds(1, rows1, stride=2), :] = part[:, lanes]
    y_at = 2 * b1y - H0

    def up0(i, _):
        add = jnp.concatenate([f0a[i, y_at : y_at + m0.shape[1], :], f0b[i, y_at : y_at + m0.shape[1], :]], axis=1)
        for k in range(2):
            a = H0 - 2 + 2 * i + k
            us0[a] = vc0[a] - ratio0 * vs0[a] + add
            rc0[a] = rc0[a] - ratio0 * rs0[a]
        return 0

    lax.fori_loop(0, b1x + 2, up0, 0)
    sweep((us0,), (uc0,), (rc0,), ops0, 3, xs0 - 3, 2)

    def last(a):
        own, t = neighbours(uc0, a, cx0, cy0, cz0)
        out_ref[a - H0] = (KEEP * own + rd0[a] * (rc0[a] + t))[H0 : H0 + by]

    slabs(H0, H0 + bx, 2, last)

    each(lambda k: e0_copies(k, False), lambda c: c.wait_send())
    each(lambda k: e0_copies(k, False, 1), lambda c: c.wait_send(), (0, 1))
    each(lambda k: level1_copies(m1, m1s, m1r, k, False, 5), lambda c: c.wait_send())
    each(lambda k: level1_copies(r1, e1s, e1r, k, False, 4), lambda c: c.wait_send())
    over_wide(*gather_m, "send")
    over_wide(*gather_r, "send")
    over_wide(*gather_p, "send")
    over_narrow(*spread_m, "send")
    over_narrow(*spread_r, "send")
    over_narrow(*spread_p, "send")


def solution(mesh):
    nw, nn = mesh.shape["wide"], mesh.shape["narrow"]

    def per_device(mobility, sav_vector, cotangent):
        bx, by, nz = mobility.shape
        b1x, b1y, z1 = bx // 2, by // 2, nz // 2
        x2, y2 = nw * bx // 4, nn * by // 4
        vm = lambda *s: pltpu.VMEM(s, F32)
        dma = lambda *s: pltpu.SemaphoreType.DMA(s)
        l0 = (bx + 2 * H0, by + 2 * H0, nz)
        l1 = (b1x + 2 * H1, 3 * b1y, z1)
        l2 = (x2 + 2 * PAD, y2, z1)
        l3 = (x2 // 2 + 2 * PAD, y2 // 2, z1)
        l4 = (x2 // 4 + 2 * PAD, 8, z1)
        own2 = (bx // 4 * (by // 4), z1)
        scratch = (
            [vm(*l0)] * 12
            + [vm(2, 10, bx, nz), vm(2, 10, bx, nz), vm(2, 10, bx, nz), vm(4, 24, nz), vm(4, 24, nz)]
            + [vm(1, *l1)] + [vm(*l1)] * 5 + [vm(2, *l1)] * 3 + [vm(*l1)]
            + [vm(*l2)] * 7 + [vm(*l3)] * 7 + [vm(*l4)] * 7
            + [vm(2, b1x * by, nz), vm(b1x * by, z1), vm(2, bx // 4 * b1y, z1), vm(bx // 4 * b1y, z1)]
            + [vm(*own2), vm(*own2), vm(8, 128), vm(nn, nw, *own2), vm(nn, nw, *own2), vm(nw, 8, 128),
               vm(8, 128), vm(nn, 8, 128)]
            + [vm(64, z1), vm(64, z1)]
            + [vm((bx // 4 + 4) * y2, z1), vm(bx // 4 + 4, 2 * y2 + 2 * b1y, z1)]
            + [vm(b1x + 2, 6 * b1y, 128)] * 2
            + [dma(8, 6), dma(8, 6), dma(8, 1), dma(8, 1), dma(8, 2), dma(8, 2)]
            + [dma(nw), dma(nw), dma(nn), dma(nn)] + [dma(nw)] * 4 + [dma(nn)] * 4
        )
        return pl.pallas_call(
            functools.partial(kernel, nw, nn, bx, by, nz),
            out_shape=jax.ShapeDtypeStruct((bx, by, nz), F32),
            in_specs=[pl.BlockSpec(memory_space=pltpu.VMEM)] * 3,
            out_specs=pl.BlockSpec(memory_space=pltpu.VMEM),
            scratch_shapes=scratch,
            compiler_params=pltpu.CompilerParams(
                collective_id=0, has_side_effects=True, vmem_limit_bytes=67043328
            ),
        )(mobility, sav_vector, cotangent)

    spec = P("wide", "narrow", None)
    return jax.shard_map(per_device, mesh=mesh, in_specs=(spec,) * 3, out_specs=spec, check_vma=False)
```

profile of v0, /device:TPU:1, one launch (start us, length us, event | category | flops | bytes accessed | tf_op | source)
XLA Modules:
  0.0 47.4 jit_solution(1040264018355425948)
XLA Ops:
  0.0 45.7 %shard_map.37 = f32[16,16,256]{2,1,0:T(8,128)} custom-call(f32[16,16,256]{2,1,0:T(8,128)} %m_ref.1, f32[16,16,256]{2,1,0:T(8,128)} %s_ref.1, f32[16,16,256]{2,1,0:T(8,128)} %c_ref.1), custom_call_target="tpu_custom_call" | custom-call | tf_op jit(solution)/shard_map/pallas_call | solution.py:664
  45.7 1.7 %copy.5 = f32[16,16,256]{2,1,0:T(8,128)} copy(f32[16,16,256]{2,1,0:T(8,128)} %shard_map.37) | data formatting | bytes 524288
where the time goes:
time: 47.5 us; the launch traced here: 47.4 us
  Pallas kernels  45.7 us (96%)
  local copies, waits for them, and re-layouts  1.67 us (4%)
    pallas_call x1, Pallas kernels, per_device(): pl.pallas_call(functools.partial(kernel, nw, nn, bx, by, nz), out_shape=j...  45.7 us
    unnamed x1, local copies, waits for them, and re-layouts  1.67 us

commit v1 on v0

v1 whole, which is shorter than its diff:
```python
import functools
import jax
import jax.numpy as jnp
from jax import lax
from jax.experimental import pallas as pl
from jax.experimental.pallas import tpu as pltpu
from jax.sharding import PartitionSpec as P

DAMPING = 0.8
KEEP = 1.0 - DAMPING
BASE_TAU = 16.0
H0 = 4
H1 = 4
PAD = 2
PAD2 = 4
MESH = pl.DeviceIdType.MESH
F32 = jnp.float32
SIDES = [(-1, 0), (1, 0), (0, -1), (0, 1), (-1, -1), (-1, 1), (1, -1), (1, 1)]
OPPOSITE = [1, 0, 3, 2, 7, 6, 5, 4]
TILE = (8, 128)


def iota(shape, dim):
    return lax.broadcasted_iota(jnp.int32, shape, dim)


def shift(value, amount, axis):
    return pltpu.roll(value, amount % value.shape[axis], axis)


def take(value, index, axis):
    return jnp.take_along_axis(value, index, axis=axis)


def z_pairs(tile):
    return take(tile + shift(tile, -1, 1), lax.rem(2 * iota(TILE, 1), 128), 1)


def put_halves(ref, v, at, value):
    for h in range(2):
        ref[v, h, at, :] = value[:, 128 * h : 128 * h + 128]


def yz_pairs(ref, v, at):
    halves = []
    for h in range(2):
        halves.append(z_pairs(ref[v, h, pl.ds(at, 8, stride=2), :] + ref[v, h, pl.ds(at + 1, 8, stride=2), :]))
    return jnp.where(iota(TILE, 1) < 64, halves[0], halves[1])


def z_repeat(tile, start=0):
    return take(tile, start + iota(TILE, 1) // 2, 1)


def y_pairs(tile):
    return take(tile + shift(tile, -1, 0), lax.rem(2 * iota(TILE, 0), 8), 0)


def y_repeat(tile, start=0):
    return take(tile, jnp.clip(start + iota(TILE, 0) // 2, 0, 7), 0)


def top_bottom(top, bottom):
    return jnp.where(iota(TILE, 0) < 4, top, bottom)


def rounded(x):
    return x.astype(jnp.bfloat16).astype(F32)


def slabs(lo, count, chunk, body):
    if count == chunk:
        for k in range(chunk):
            body(lo + k)
        return

    def step(i, _):
        for k in range(chunk):
            body(lo + i * chunk + k)
        return 0

    lax.fori_loop(0, count // chunk, step, 0)


def build(m, cx, cy, cz, rd, d, lo, count, tau, seg, chunk, firsts=()):
    shape = m.shape[1:]
    row = iota(shape, 0)
    lane = lax.rem(iota(shape, 1), seg)
    last_row, first_row = row == shape[0] - 1, row == 0
    last_lane, first_lane = lane == seg - 1, lane == 0
    half = 0.5 * tau

    def body(a):
        own = m[a]
        xp, xm = m[a + 1], m[a - 1]
        yp = jnp.where(last_row, 0.0, shift(own, -1, 0))
        ym = jnp.where(first_row, 0.0, shift(own, 1, 0))
        zp = jnp.where(last_lane, 0.0, shift(own, -1, 1))
        zm = jnp.where(first_lane, 0.0, shift(own, 1, 1))
        total = 1.0
        for other, ref in ((xp, cx), (xm, None), (yp, cy), (ym, None), (zp, cz), (zm, None)):
            face = rounded(half * (own + other))
            total = total + face
            if ref is not None:
                ref[a] = jnp.where(jnp.minimum(own, other) > 0.0, face, 0.0)
        inverse = DAMPING / total
        rd[a] = inverse
        if d is not None:
            d[a] = total
        for r, u in firsts:
            u[a] = inverse * r[a]

    slabs(lo, count, chunk, body)


def neighbours(v, a, cx, cy, cz):
    own = v[a]
    cya, cza = cy[a], cz[a]
    total = cx[a] * v[a + 1] + cx[a - 1] * v[a - 1]
    total = total + (cya * shift(own, -1, 0) + shift(cya * own, 1, 0))
    total = total + (cza * shift(own, -1, 1) + shift(cza * own, 1, 1))
    return own, total


def sweep(vin, vout, r, ops, lo, count, chunk):
    cx, cy, cz, rd, d = ops

    def body(a):
        for vi, vo, ri in zip(vin, vout, r):
            own, t = neighbours(vi, a, cx, cy, cz)
            vo[a] = KEEP * own + rd[a] * (ri[a] + t)

    slabs(lo, count, chunk, body)


def residual(vi, ri, a, ops):
    cx, cy, cz, rd, d = ops
    own, t = neighbours(vi, a, cx, cy, cz)
    diag = d[a] if d is not None else DAMPING / rd[a]
    return own, ri[a] + t - diag * own


def fold(x):
    total = None
    for i in range(x.shape[0] // 8):
        for j in range(x.shape[1] // 128):
            part = x[8 * i : 8 * i + 8, 128 * j : 128 * j + 128]
            total = part if total is None else total + part
    return total


def fold_own(x):
    total = None
    for j in range(x.shape[1] // 128):
        lanes = slice(128 * j, 128 * j + 128)
        part = x[8:16, lanes] + top_bottom(x[16:24, lanes], x[0:8, lanes])
        total = part if total is None else total + part
    return total


def kernel(nw, nn, bx, by, nz, m_hbm, s_hbm, c_hbm, out_ref,
           m_ref, s_ref, c_ref,
           m0, cx0, cy0, cz0, rd0, d0, rs0, rc0, us0, uc0, vs0, vc0,
           rx, yp, ry, cp, rcn, xv, hx, yv, hy,
           m1, cx1, cy1, cz1, rd1, d1, r1, u1, v1, w1, h1,
           cx2, cy2, cz2, rd2, r2, u2, v2,
           cx3, cy3, cz3, rd3, r3, u3, v3,
           cx4, cy4, cz4, rd4, r4, u4, v4,
           t0, sm2, sr2, sp2, gm, gr, gp, pb, pbs, f1p, tok,
           ins, ss, gs, gq, e0r, m1r, r1r, v0r, v1r):
    iw, ino = lax.axis_index("wide"), lax.axis_index("narrow")
    b1x, b1y, z1 = bx // 2, by // 2, nz // 2
    b2x, b2y, z2 = bx // 4, by // 4, nz // 4
    x2, x3, x4 = nw * b2x, nw * b2x // 2, nw * b2x // 4
    there = []
    for dx, dy in SIDES:
        ok = None
        for cond, on in ((iw > 0, dx < 0), (iw < nw - 1, dx > 0), (ino > 0, dy < 0), (ino < nn - 1, dy > 0)):
            if on:
                ok = cond if ok is None else jnp.logical_and(ok, cond)
        there.append(ok)

    def peer(side):
        return (iw + SIDES[side][0], ino + SIDES[side][1])

    inputs = [pltpu.make_async_copy(src, dst, ins.at[i])
              for i, (src, dst) in enumerate(((m_hbm, m_ref), (s_hbm, s_ref), (c_hbm, c_ref)))]
    for copy in inputs:
        copy.start()

    def clear(ref, index):
        ref[index] = jnp.zeros(ref[index].shape, F32)

    for k in range(2):
        for ref in (rx, ry, hx, hy):
            for i in range(ref.shape[1]):
                clear(ref, (k, i))
    for k in range(4):
        clear(rcn, k)
    for k in range(2):
        for i in range(h1.shape[1]):
            clear(h1, (k, i))
    side_rows = (slice(0, b1y), slice(2 * b1y, 3 * b1y))
    for a in (0, 1, 2, 3, H1 + b1x, H1 + b1x + 1, H1 + b1x + 2, H1 + b1x + 3):
        clear(m1, (0, a))
    for a in (H1 - 2, H1 - 1, H1 + b1x, H1 + b1x + 1):
        for v in range(2):
            clear(r1, (v, a))
    for a in range(H1, H1 + b1x):
        for rows in side_rows:
            clear(m1, (0, a, rows))
            for v in range(2):
                clear(r1, (v, a, rows))

    barrier = pltpu.get_barrier_semaphore()

    def greet(j, _):
        pl.semaphore_signal(barrier, inc=1, device_id=(lax.rem(iw + j, nw), ino), device_id_type=MESH)
        return 0

    lax.fori_loop(1, nw, greet, 0)
    for j in range(1, nn):
        pl.semaphore_signal(barrier, inc=1, device_id=(iw, lax.rem(ino + j, nn)), device_id_type=MESH)
    for k in range(4, 8):
        @pl.when(there[k])
        def _():
            pl.semaphore_signal(barrier, inc=1, device_id=peer(k), device_id_type=MESH)

    for copy in inputs:
        copy.wait()
    for side, (m_lo, r_lo) in enumerate(((0, 0), (by - 3, by - 2))):
        for k in range(3):
            yp[side, k] = m_ref[:, m_lo + k, :]
        for k in range(2):
            yp[side, 3 + k] = s_ref[:, r_lo + k, :]
            yp[side, 5 + k] = c_ref[:, r_lo + k, :]
    for k in range(4, 8):
        dx, dy = SIDES[k]
        xa, xb = (0, 1) if dx < 0 else (bx - 1, bx - 2)
        ya, yb = (0, 1) if dy < 0 else (by - 1, by - 2)
        for i, (ref, x, y) in enumerate(((m_ref, xa, ya), (m_ref, xa, yb), (m_ref, xb, ya),
                                         (s_ref, xa, ya), (c_ref, xa, ya))):
            cp[k - 4, i : i + 1, :] = ref[x, y : y + 1, :]

    beside_x = jnp.minimum(iw, 1) + jnp.minimum(nw - 1 - iw, 1)
    beside_y = jnp.minimum(ino, 1) + jnp.minimum(nn - 1 - ino, 1)
    pl.semaphore_wait(barrier, nw + nn - 2 + beside_x * beside_y)

    def remote(src, dst, ssem, rsem, dev):
        return pltpu.make_async_remote_copy(src_ref=src, dst_ref=dst, send_sem=ssem, recv_sem=rsem,
                                            device_id=dev, device_id_type=MESH)

    def to_side(side, pairs, rsem):
        return [remote(src, dst, ss.at[side], rsem.at[OPPOSITE[side]], peer(side)) for src, dst in pairs]

    def e0_sends(side):
        land = OPPOSITE[side]
        if side < 2:
            pairs = []
            at = 0
            for ref, width in ((m_ref, 3), (s_ref, 2), (c_ref, 2)):
                lo = 0 if side == 0 else bx - width
                pairs.append((ref.at[lo : lo + width], rx.at[land, at : at + width]))
                at += width
            return to_side(side, pairs, e0r)
        if side < 4:
            return to_side(side, [(yp.at[side - 2], ry.at[land - 2])], e0r)
        return to_side(side, [(cp.at[side - 4], rcn.at[land - 4])], e0r)

    def box1(side, sending, width, corner):
        dx, dy = SIDES[side]
        w = corner if dx and dy else width
        if sending:
            xlo, w = (H1, w) if dx < 0 else ((H1 + b1x - w, w) if dx > 0 else (H1, b1x))
            ylo = b1y
        else:
            xlo, w = (H1 - w, w) if dx < 0 else ((H1 + b1x, w) if dx > 0 else (H1, b1x))
            ylo = b1y * (1 + dy)
        return xlo, w, ylo

    def level1_sends(ref, rsem, side, width, corner):
        sx, w, sy = box1(side, True, width, corner)
        tx, _, ty = box1(OPPOSITE[side], False, width, corner)
        return to_side(side, [(ref.at[:, sx : sx + w, sy : sy + b1y], ref.at[:, tx : tx + w, ty : ty + b1y])], rsem)

    def level1_landed(ref, rsem, width, corner):
        def fn(side):
            tx, w, ty = box1(side, False, width, corner)
            view = ref.at[:, tx : tx + w, ty : ty + b1y]
            pltpu.make_async_copy(view, view, rsem.at[side]).wait()
        return fn

    def each(fn, sides=range(8)):
        for side in sides:
            @pl.when(there[side])
            def _():
                fn(side)

    def start(copies):
        for copy in copies:
            copy.start()

    def e0_landed(side):
        view = rx.at[side] if side < 2 else (ry.at[side - 2] if side < 4 else rcn.at[side - 4])
        pltpu.make_async_copy(view, view, e0r.at[side]).wait()

    each(lambda k: start(e0_sends(k)), (0, 1, 2, 3, 4, 5, 6, 7))

    own_y = slice(b1y, 2 * b1y)
    for i in range(b1x):
        put_halves(t0, 0, slice(i * by, (i + 1) * by), m_ref[2 * i] + m_ref[2 * i + 1])
    for i in range(b1x):
        m1[0, H1 + i, own_y, :] = 0.125 * yz_pairs(t0, 0, i * by)
    for i in range(0, b2x, 2):
        quads = [y_pairs(m1[0, H1 + 2 * k, own_y, :] + m1[0, H1 + 2 * k + 1, own_y, :]) for k in (i, i + 1)]
        mob2 = 0.125 * z_pairs(top_bottom(quads[0], quads[1]))
        sm2[i * b2y : (i + 2) * b2y, :] = mob2
        gm[ino, iw, i * b2y : (i + 2) * b2y, :] = mob2

    def over_wide(src, dst, kind):
        def step(j, _):
            to = lax.rem(iw + j, nw)
            remote(src, dst(iw), gs.at[kind], gq.at[kind], (to, ino)).start()
            return 0

        lax.fori_loop(1, nw, step, 0)

    def over_narrow(src, dst, kind):
        for j in range(1, nn):
            to = lax.rem(ino + j, nn)
            remote(src, dst(ino), gs.at[kind], gq.at[kind], (iw, to)).start()

    def landed(view, kind):
        pltpu.make_async_copy(view, view, gq.at[kind]).wait()

    wide_m = lambda: landed(gm.at[0, 0 : nw - 1], 0)
    narrow_m = lambda: landed(gm.at[0 : nn - 1], 1)
    wide_r = lambda: landed(gr.at[0, 0 : nw - 1], 2)
    narrow_r = lambda: landed(gr.at[0 : nn - 1], 3)
    wide_p = lambda: landed(gp.at[0 : nw - 1], 4)
    narrow_p = lambda: landed(pbs.at[0 : nn - 1], 5)

    for ref, src, width in ((m0, m_ref, 3), (rs0, s_ref, 2), (rc0, c_ref, 2)):
        blank = jnp.zeros(m0.shape[1:], F32)
        for i in range(width):
            ref[H0 - 1 - i] = blank
            ref[H0 + bx + i] = blank

        def put(i, _):
            ref[H0 + i, H0 : H0 + by, :] = src[i]
            return 0

        lax.fori_loop(0, bx, put, 0)
    for ref in (u3, v3, u4, v4):
        zero = jnp.zeros(ref.shape[1:], F32)
        for a in (0, 1, ref.shape[0] - 2, ref.shape[0] - 1):
            ref[a] = zero
    for ref in (u2, v2, r2, cx2, cy2, cz2, rd2):
        zero = jnp.zeros(ref.shape[1:], F32)
        for a in range(PAD2):
            ref[a] = zero
            ref[ref.shape[0] - 1 - a] = zero
    for ref in (cx3, cx4):
        ref[PAD - 1] = jnp.zeros(ref.shape[1:], F32)

    each(e0_landed, (2, 3))
    fields = ((m0, 0, 3), (rs0, 3, 2), (rc0, 5, 2))
    for ref, at, width in fields:
        for i in range(width):
            ref[H0 : H0 + bx, H0 - width + i, :] = ry[0, at + i]
            ref[H0 : H0 + bx, H0 + by + i, :] = ry[1, at + i]

    ops0 = (cx0, cy0, cz0, rd0, d0)
    firsts0 = ((rs0, us0), (rc0, uc0))

    build(m0, cx0, cy0, cz0, rd0, d0, H0 + 1, bx - 2, BASE_TAU, nz, 2, firsts0)
    sweep((us0, uc0), (vs0, vc0), (rs0, rc0), ops0, H0 + 2, bx - 4, 2)
    each(lambda k: start(level1_sends(m1, m1r, k, 3, 3)))
    over_wide(sm2, lambda w: gm.at[ino, w], 0)

    def down0(i, carry):
        num, den = carry
        sums = []
        for k in range(2):
            a = H0 + 2 * i + k
            vs, es = residual(vs0, rs0, a, ops0)
            vc, ec = residual(vc0, rc0, a, ops0)
            both = es + rs0[a]
            num = num + fold_own(both * vc)
            den = den + fold_own(both * vs)
            sums.append((es, ec))
        at = pl.ds(pl.multiple_of(i * m0.shape[1], 8), m0.shape[1])
        put_halves(t0, 0, at, sums[0][0] + sums[1][0])
        put_halves(t0, 1, at, sums[0][1] + sums[1][1])
        return num, den

    zero8 = jnp.zeros(TILE, F32)
    part0 = lax.fori_loop(2, b1x - 2, down0, (zero8, zero8))

    each(e0_landed, (0, 1, 4, 5, 6, 7))
    for ref, at, width in fields:
        for i in range(width):
            ref[H0 - width + i, H0 : H0 + by, :] = rx[0, at + i]
            ref[H0 + bx + i, H0 : H0 + by, :] = rx[1, at + i]
    for k in range(4):
        dx, dy = SIDES[4 + k]
        xa, xb = (H0 - 1, H0 - 2) if dx < 0 else (H0 + bx, H0 + bx + 1)
        ya, yb = (H0 - 1, H0 - 2) if dy < 0 else (H0 + by, H0 + by + 1)
        for i, (ref, x, y) in enumerate(((m0, xa, ya), (m0, xa, yb), (m0, xb, ya), (rs0, xa, ya), (rc0, xa, ya))):
            ref[x, y : y + 1, :] = rcn[k, i : i + 1, :]
    for lo, v_lo in ((H0 - 2, H0 - 1), (H0 + bx - 1, H0 + bx - 2)):
        build(m0, cx0, cy0, cz0, rd0, d0, lo, 3, BASE_TAU, nz, 1, firsts0)
        sweep((us0, uc0), (vs0, vc0), (rs0, rc0), ops0, v_lo, 3, 1)
    part0 = lax.fori_loop(0, 2, down0, part0)
    num0, den0 = lax.fori_loop(b1x - 2, b1x, down0, part0)
    for v in range(2):
        for i in range(b1x):
            r1[v, H1 + i, own_y, :] = 0.125 * yz_pairs(t0, v, i * m0.shape[1] + H0)
    each(lambda k: start(level1_sends(r1, r1r, k, 2, 1)))
    wide_m()
    over_narrow(gm.at[ino], lambda n: gm.at[n], 1)
    for side, (x_far, x_near) in enumerate(((H0 + 1, H0), (H0 + bx - 2, H0 + bx - 1))):
        for v, ref in enumerate((vs0, vc0)):
            xv[side, v, 0:by, :] = ref[x_far, H0 : H0 + by, :]
            xv[side, v, by : by + 1, :] = ref[x_near, H0 - 1 : H0, :]
            xv[side, v, by + 1 : by + 2, :] = ref[x_near, H0 + by : H0 + by + 1, :]
    for side, col in enumerate((H0 + 1, H0 + by - 2)):
        for v, ref in enumerate((vs0, vc0)):
            yv[side, v] = ref[H0 : H0 + bx, col, :]

    def v0_sends(side):
        land = OPPOSITE[side]
        src, dst = (xv.at[side], hx.at[land]) if side < 2 else (yv.at[side - 2], hy.at[land - 2])
        return to_side(side, [(src, dst)], v0r)

    each(lambda k: start(v0_sends(k)), range(4))
    each(level1_landed(m1, m1r, 3, 3))
    ops1 = (cx1, cy1, cz1, rd1, d1)
    build(m1.at[0], cx1, cy1, cz1, rd1, d1, H1 - 3, b1x + 6, BASE_TAU / 4, z1, 2)
    each(level1_landed(r1, r1r, 2, 1))
    rr1 = (r1.at[0], r1.at[1])
    uu1 = (u1.at[0], u1.at[1])
    vv1 = (v1.at[0], v1.at[1])

    def first1(a):
        for v in range(2):
            u1[v, a] = rd1[a] * r1[v, a]

    slabs(H1 - 2, b1x + 4, 2, first1)
    sweep(uu1, vv1, rr1, ops1, H1 - 1, b1x + 2, 2)
    num1, den1 = zero8, zero8
    quads = []
    for i in range(b2x):
        pair = []
        for k in range(2):
            a = H1 + 2 * i + k
            vs, es = residual(vv1[0], rr1[0], a, ops1)
            vc, ec = residual(vv1[1], rr1[1], a, ops1)
            both = (es + r1[0, a])[own_y]
            num1 = num1 + both * vc[own_y]
            den1 = den1 + both * vs[own_y]
            pair.append((es[own_y], ec[own_y]))
        quads.append([y_pairs(pair[0][v] + pair[1][v]) for v in range(2)])
        if i % 2:
            packed = [z_pairs(top_bottom(quads[i - 1][v], quads[i][v])) for v in range(2)]
            own2 = 0.125 * jnp.where(iota(TILE, 1) < z2, packed[0], packed[1])
            sr2[(i - 1) * b2y : (i + 1) * b2y, :] = own2
            gr[ino, iw, (i - 1) * b2y : (i + 1) * b2y, :] = own2
    over_wide(sr2, lambda w: gr.at[ino, w], 2)
    num_row = jnp.sum(num0 + 8.0 * num1, axis=0, keepdims=True)
    den_row = jnp.sum(den0 + 8.0 * den1, axis=0, keepdims=True)
    row8 = iota(TILE, 0)
    part = jnp.where(row8 == 0, num_row, jnp.where(row8 == 1, den_row, 0.0))
    sp2[...] = part
    gp[iw] = part
    over_wide(sp2, lambda w: gp.at[w], 4)

    narrow_m()

    def unpack(src, dst):
        def step(w, _):
            for n in range(nn):
                for i in range(b2x):
                    dst[PAD2 + w * b2x + i, n * b2y : (n + 1) * b2y, :] = src[n, w, i * b2y : (i + 1) * b2y, :]
            return 0

        lax.fori_loop(0, nw, step, 0)

    unpack(gm, v2)
    build(v2, cx2, cy2, cz2, rd2, None, PAD2, x2, BASE_TAU / 16, z2, 8)

    def coarsen(x):
        if x.shape[0] == 16:
            return 0.125 * z_pairs(top_bottom(y_pairs(x[0:8]), y_pairs(x[8:16])))
        return 0.125 * z_pairs(top_bottom(y_pairs(x), 0.0))

    def coarsen_pairs(get, xc, pad, dst):
        def step(g, _):
            for k in range(4):
                a = pad + 2 * (4 * g + k)
                dst[PAD + 4 * g + k] = coarsen(get(a) + get(a + 1))
            return 0

        lax.fori_loop(0, xc // 4, step, 0)

    coarsen_pairs(lambda a: v2[a], x3, PAD2, v3)
    build(v3, cx3, cy3, cz3, rd3, None, PAD, x3, BASE_TAU / 64, z2 // 2, 4)
    coarsen_pairs(lambda a: v3[a], x4, PAD, v4)
    build(v4, cx4, cy4, cz4, rd4, None, PAD, x4, BASE_TAU / 256, z2 // 4, 4)

    wide_r()
    over_narrow(gr.at[ino], lambda n: gr.at[n], 3)

    def v1_sends(side):
        land = OPPOSITE[side]
        pairs = []
        for v in range(2):
            lo = H1 if side == 0 else H1 + b1x - 3
            pairs.append((v1.at[v, lo : lo + 3], h1.at[land, 3 * v : 3 * v + 3]))
        for v in range(2):
            lo = H1 if side == 0 else H1 + b1x - 2
            pairs.append((r1.at[v, lo : lo + 2], h1.at[land, 6 + 2 * v : 8 + 2 * v]))
        return to_side(side, pairs, v1r)

    each(lambda k: start(v1_sends(k)), range(2))

    def v0_landed(side):
        view = hx.at[side] if side < 2 else hy.at[side - 2]
        pltpu.make_async_copy(view, view, v0r.at[side]).wait()

    each(v0_landed, range(4))
    for side, (x_far, x_near) in enumerate(((H0 - 2, H0 - 1), (H0 + bx + 1, H0 + bx))):
        for v, ref in enumerate((vs0, vc0)):
            ref[x_far, H0 : H0 + by, :] = hx[side, v, 0:by, :]
            ref[x_near, H0 - 1 : H0, :] = hx[side, v, by : by + 1, :]
            ref[x_near, H0 + by : H0 + by + 1, :] = hx[side, v, by + 1 : by + 2, :]
    for side, col in enumerate((H0 - 2, H0 + by + 1)):
        for v, ref in enumerate((vs0, vc0)):
            ref[H0 : H0 + bx, col, :] = hy[side, v]
    narrow_r()
    unpack(gr, r2)

    ops2 = (cx2, cy2, cz2, rd2, None)
    ops3 = (cx3, cy3, cz3, rd3, None)
    ops4 = (cx4, cy4, cz4, rd4, None)

    def down(u, v, r, ops, pad, xc):
        def first(a):
            u[a] = ops[3][a] * r[a]

        slabs(pad, xc, 4, first)
        sweep((u,), (v,), (r,), ops, pad, xc, 8)

    down(u2, v2, r2, ops2, PAD2, x2)
    low2 = iota(v2.shape[1:], 1) < z2

    def coarsen2(g, carry):
        num, den = carry
        for k in range(2):
            pair = []
            for j in range(2):
                a = PAD2 + 2 * (2 * g + k) + j
                v, e = residual(v2, r2, a, ops2)
                both = jnp.where(low2, e + r2[a], 0.0)
                num = num + fold(both * shift(v, z2, 1))
                den = den + fold(both * v)
                pair.append(e)
            r3[PAD + 2 * g + k] = coarsen(pair[0] + pair[1])
        return num, den

    num2, den2 = lax.fori_loop(0, x3 // 2, coarsen2, (zero8, zero8))
    wide_p()
    total = gp[0]
    if nw <= 16:
        for w in range(1, nw):
            total = total + gp[w]
    else:
        total = lax.fori_loop(1, nw, lambda w, acc: acc + gp[w], total)
    pb[...] = total
    over_narrow(pb, lambda n: pbs.at[n], 5)
    down(u3, v3, r3, ops3, PAD, x3)
    coarsen_pairs(lambda a: residual(v3, r3, a, ops3)[1], x4, PAD, r4)
    down(u4, v4, r4, ops4, PAD, x4)

    def up3(g, _):
        for k in range(4):
            add = y_repeat(z_repeat(v4[PAD + 4 * g + k]))
            a = PAD + 2 * (4 * g + k)
            v3[a] = v3[a] + add
            v3[a + 1] = v3[a + 1] + add
        return 0

    lax.fori_loop(0, x4 // 4, up3, 0)
    sweep((v3,), (u3,), (r3,), ops3, PAD, x3, 8)
    sweep((u3,), (v3,), (r3,), ops3, PAD, x3, 8)
    low3 = iota(TILE, 1) < z2 // 2

    def dots(i, carry):
        num, den = carry
        for k in range(4):
            a = PAD + 4 * i + k
            both = jnp.where(low3, v3[a], 0.0)
            den = den + both * r3[a]
            num = num + both * shift(r3[a], -(z2 // 2), 1)
        return num, den

    num3, den3 = lax.fori_loop(0, x3 // 4, dots, (zero8, zero8))
    base = PAD2 + iw * b2x
    for i in range(b2x // 2 + 4):
        wide_tile = z_repeat(v3[PAD + iw * (b2x // 2) - 2 + i])
        for j in range(2):
            a = base - 4 + 2 * i + j
            v2[a, 0:8, :] = v2[a, 0:8, :] + y_repeat(wide_tile)
            v2[a, 8:16, :] = v2[a, 8:16, :] + y_repeat(wide_tile, 4)
    sweep((v2,), (u2,), (r2,), ops2, base - 3, b2x + 6, b2x + 6)
    sweep((u2,), (v2,), (r2,), ops2, base - 2, b2x + 4, b2x + 4)

    narrow_p()
    whole = total
    for j in range(1, nn):
        whole = whole + pbs[lax.rem(ino + j, nn)]
    num = jnp.sum(jnp.where(row8 == 0, whole, 0.0) + 64.0 * num2 + 512.0 * num3)
    den = jnp.sum(jnp.where(row8 == 1, whole, 0.0) + 64.0 * den2 + 512.0 * den3)
    ratio = (jnp.full(TILE, num) / (1.0 + jnp.full(TILE, den)))[0:1, :]

    def v1_landed(side):
        pltpu.make_async_copy(h1.at[side], h1.at[side], v1r.at[side]).wait()

    each(v1_landed, range(2))
    rows2 = v2.shape[1]
    full_y = 2 * rows2
    for i in range(b2x + 4):
        f1p[i, 0:b1y, :] = jnp.zeros((b1y, z1), F32)
        f1p[i, b1y + full_y : 2 * b1y + full_y, :] = jnp.zeros((b1y, z1), F32)
        for j in range(rows2 // 8):
            e = v2[base - 2 + i, 8 * j : 8 * j + 8, :]
            part = z_repeat(shift(e, z2, 1) - ratio * e)
            f1p[i, pl.ds(b1y + 16 * j, 8, stride=2), :] = part
            f1p[i, pl.ds(b1y + 16 * j + 1, 8, stride=2), :] = part
    window = pl.ds(pl.multiple_of(ino * b1y, 8), 3 * b1y)
    for x in range(-3, b1x + 3):
        a = H1 + x
        side, at = (0, x + 3) if x < 0 else (1, x - b1x)
        far = x < 0 or x >= b1x
        vs, vc = (h1[side, at], h1[side, 3 + at]) if far else (v1[0, a], v1[1, a])
        u1[0, a] = vc - ratio * vs + f1p[x // 2 + 2, window, :]
        if -2 <= x < b1x + 2:
            at = x + 2 if x < 0 else x - b1x
            rs, rc = (h1[side, 6 + at], h1[side, 8 + at]) if far else (r1[0, a], r1[1, a])
            w1[a] = rc - ratio * rs
    sweep((u1.at[0],), (u1.at[1],), (w1,), ops1, H1 - 2, b1x + 4, 2)
    sweep((u1.at[1],), (u1.at[0],), (w1,), ops1, H1 - 1, b1x + 2, 2)

    ratio0 = jnp.concatenate([ratio] * (nz // 128), axis=1)

    def up0(i, _):
        tiles = [u1[0, H1 - 1 + i, 8 * j : 8 * j + 8, :] for j in range(3)]
        rows = [top_bottom(y_repeat(tiles[0], 6), y_repeat(tiles[1], -2)),
                y_repeat(tiles[1], 2),
                top_bottom(y_repeat(tiles[1], 6), y_repeat(tiles[2], -2))]
        add = jnp.concatenate([jnp.concatenate([z_repeat(t), z_repeat(t, 64)], axis=1) for t in rows], axis=0)
        for k in range(2):
            a = H0 - 2 + 2 * i + k
            us0[a] = vc0[a] - ratio0 * vs0[a] + add
            rc0[a] = rc0[a] - ratio0 * rs0[a]
        return 0

    lax.fori_loop(0, b1x + 2, up0, 0)
    sweep((us0,), (uc0,), (rc0,), ops0, H0 - 1, bx + 2, 2)

    def last(a):
        own, t = neighbours(uc0, a, cx0, cy0, cz0)
        out_ref[a - H0] = (KEEP * own + rd0[a] * (rc0[a] + t))[H0 : H0 + by]

    slabs(H0, bx, 2, last)

    def sent(side):
        dx, dy = SIDES[side]
        if dy == 0:
            tiles = 7 * by * nz // 1024 + 3 + 4 + 2 * (by + 8) * nz // 1024 + 30
        elif dx == 0:
            tiles = 7 * bx * nz // 1024 + b1x + 2 * b1x + 2 * bx * nz // 1024
        else:
            tiles = 2 + 3 + 2
        view = tok.at[0:tiles]
        pltpu.make_async_copy(view, view, ss.at[side]).wait()

    each(sent)
    for kind, view in enumerate((gm.at[0, 0 : nw - 1], gm.at[0 : nn - 1], gr.at[0, 0 : nw - 1],
                                 gr.at[0 : nn - 1], gp.at[0 : nw - 1], pbs.at[0 : nn - 1])):
        pltpu.make_async_copy(view, view, gs.at[kind]).wait()


def solution(mesh):
    nw, nn = mesh.shape["wide"], mesh.shape["narrow"]

    def per_device(mobility, sav_vector, cotangent):
        bx, by, nz = mobility.shape
        b1x, b1y, z1 = bx // 2, by // 2, nz // 2
        x2, y2 = nw * bx // 4, nn * by // 4
        own = (bx, by, nz)
        l0 = (bx + 2 * H0, by + 2 * H0, nz)
        l1 = (b1x + 2 * H1, 3 * b1y, z1)
        l2 = (x2 + 2 * PAD2, y2, z1)
        l3 = (x2 // 2 + 2 * PAD, y2 // 2, z1)
        l4 = (x2 // 4 + 2 * PAD, 8, z1)
        own2 = (bx // 4 * (by // 4), z1)
        buffers = (
            [own] * 3 + [l0] * 12
            + [(2, 7, by, nz), (2, 7, bx, nz), (2, 7, bx, nz), (4, 8, nz), (4, 8, nz)]
            + [(2, 2, by + 8, nz)] * 2 + [(2, 2, bx, nz)] * 2
            + [(1, *l1)] + [l1] * 5 + [(2, *l1)] * 3 + [l1] + [(2, 10, 3 * b1y, z1)]
            + [l2] * 7 + [l3] * 7 + [l4] * 7
            + [(2, 2, b1x * l0[1], nz // 2)]
            + [own2, own2, TILE, (nn, nw, *own2), (nn, nw, *own2), (nw, *TILE), TILE, (nn, *TILE)]
            + [(bx // 4 + 4, 2 * y2 + 2 * b1y, z1), (128, *TILE)]
        )
        size = sum(4 * functools.reduce(lambda p, q: p * q, shape) for shape in buffers)
        dma = lambda n: pltpu.SemaphoreType.DMA((n,))
        scratch = [pltpu.VMEM(shape, F32) for shape in buffers]
        scratch += [dma(n) for n in (3, 8, 6, 6, 8, 8, 8, 4, 2)]
        return pl.pallas_call(
            functools.partial(kernel, nw, nn, bx, by, nz),
            out_shape=jax.ShapeDtypeStruct((bx, by, nz), F32),
            in_specs=[pl.BlockSpec(memory_space=pltpu.HBM)] * 3,
            out_specs=pl.BlockSpec(memory_space=pltpu.VMEM),
            scratch_shapes=scratch,
            compiler_params=pltpu.CompilerParams(
                collective_id=0, has_side_effects=True, vmem_limit_bytes=min(67043328, size + (8 << 20))
            ),
        )(mobility, sav_vector, cotangent)

    spec = P("wide", "narrow", None)
    return jax.shard_map(per_device, mesh=mesh, in_specs=(spec,) * 3, out_specs=spec, check_vma=False)
```

time: 47.5 us -> 41.5 us (0.87)
  Pallas kernels: 45.7 us -> 37.4 us
  local copies, waits for them, and re-layouts: 1.67 us -> 3.55 us
    pallas_call x1, Pallas kernels: 45.7 us -> 37.4 us  [per_device(): pl.pallas_call(functools.partial(kernel, nw, nn, bx, by, nz), out_shape=j...]
    unnamed x1 -> x7, local copies, waits for them, and re-layouts: 1.67 us -> 3.55 us
where the time goes in v1:
time: 41.5 us; the launch traced here: 41 us
  Pallas kernels  37.4 us (90%)
  local copies, waits for them, and re-layouts  3.55 us (9%)
    pallas_call x1, Pallas kernels, per_device(): pl.pallas_call(functools.partial(kernel, nw, nn, bx, by, nz), out_shape=j...  37.4 us
    unnamed x7, local copies, waits for them, and re-layouts  3.55 us

profile of v1, /device:TPU:1, one launch (start us, length us, event | category | flops | bytes accessed | tf_op | source)
XLA Modules:
  0.0 41.0 jit_solution(2497145056194659432)
XLA Ops:
  0.0 0.0 copy-start
  0.0 0.9 %copy-done = f32[16,16,256]{2,1,0:T(8,128)S(1)} copy-done((f32[16,16,256]{2,1,0:T(8,128)S(1)}, f32[16,16,256]{2,1,0:T(8,128)}, u32[]{:S(2)}) %copy-start) | copy-done | bytes 262168
  1.0 0.0 copy-start.1
  1.0 0.9 %copy-done.1 = f32[16,16,256]{2,1,0:T(8,128)S(1)} copy-done((f32[16,16,256]{2,1,0:T(8,128)S(1)}, f32[16,16,256]{2,1,0:T(8,128)}, u32[]{:S(2)}) %copy-start.1) | copy-done | bytes 262168
  1.9 0.0 copy-start.2
  1.9 0.9 %copy-done.2 = f32[16,16,256]{2,1,0:T(8,128)S(1)} copy-done((f32[16,16,256]{2,1,0:T(8,128)S(1)}, f32[16,16,256]{2,1,0:T(8,128)}, u32[]{:S(2)}) %copy-start.2) | copy-done | bytes 262168
  2.9 37.4 %shard_map.37 = f32[16,16,256]{2,1,0:T(8,128)S(1)} custom-call(f32[16,16,256]{2,1,0:T(8,128)S(1)} %copy-done, f32[16,16,256]{2,1,0:T(8,128)S(1)} %copy-done.1, f32[16,16,256]{2,1,0:T(8,128)S(1)} %copy-done.2), custom_call_target="tpu_custom_call" | custom-call | tf_op jit(solution)/shard_map/pallas_call | solution.py:722
  40.2 0.7 %copy.5 = f32[16,16,256]{2,1,0:T(8,128)} copy(f32[16,16,256]{2,1,0:T(8,128)S(1)} %shard_map.37) | data formatting | bytes 524288
Async XLA Ops:
  0.0 0.9 %copy-start = (f32[16,16,256]{2,1,0:T(8,128)S(1)}, f32[16,16,256]{2,1,0:T(8,128)}, u32[]{:S(2)}) copy-start(f32[16,16,256]{2,1,0:T(8,128)} %m_hbm.1) | copy-start | bytes 786436
  1.0 0.9 %copy-start.1 = (f32[16,16,256]{2,1,0:T(8,128)S(1)}, f32[16,16,256]{2,1,0:T(8,128)}, u32[]{:S(2)}) copy-start(f32[16,16,256]{2,1,0:T(8,128)} %s_hbm.1) | copy-start | bytes 786436
  1.9 0.9 %copy-start.2 = (f32[16,16,256]{2,1,0:T(8,128)S(1)}, f32[16,16,256]{2,1,0:T(8,128)}, u32[]{:S(2)}) copy-start(f32[16,16,256]{2,1,0:T(8,128)} %c_hbm.1) | copy-start | bytes 786436

commit v2 on v1

--- a/solution.py
+++ b/solution.py
@@ -13,6 +13,7 @@
 H1 = 4
 PAD = 2
 PAD2 = 4
+GRANT = 56200000
 MESH = pl.DeviceIdType.MESH
 F32 = jnp.float32
 SIDES = [(-1, 0), (1, 0), (0, -1), (0, 1), (-1, -1), (-1, 1), (1, -1), (1, 1)]
@@ -162,7 +163,7 @@
            m_ref, s_ref, c_ref,
            m0, cx0, cy0, cz0, rd0, d0, rs0, rc0, us0, uc0, vs0, vc0,
            rx, yp, ry, cp, rcn, xv, hx, yv, hy,
-           m1, cx1, cy1, cz1, rd1, d1, r1, u1, v1, w1, h1,
+           m1, cx1, cy1, cz1, rd1, d1, r1, u1, v1, w1, h1, hc,
            cx2, cy2, cz2, rd2, r2, u2, v2,
            cx3, cy3, cz3, rd3, r3, u3, v3,
            cx4, cy4, cz4, rd4, r4, u4, v4,
@@ -200,6 +201,8 @@
     for k in range(2):
         for i in range(h1.shape[1]):
             clear(h1, (k, i))
+        for i in range(2):
+            clear(hc, (k, i))
     side_rows = (slice(0, b1y), slice(2 * b1y, 3 * b1y))
     for a in (0, 1, 2, 3, H1 + b1x, H1 + b1x + 1, H1 + b1x + 2, H1 + b1x + 3):
         clear(m1, (0, a))
@@ -214,18 +217,62 @@
 
     barrier = pltpu.get_barrier_semaphore()
 
+    nb = nn // 2 * nw
+    me, odd = ino // 2 * nw + iw, lax.rem(ino, 2)
+    twin = ino + 1 - 2 * odd
+
+    def fellow(j):
+        to = lax.rem(me + j, nb)
+        return lax.rem(to, nw), 2 * (to // nw) + odd
+
     def greet(j, _):
-        pl.semaphore_signal(barrier, inc=1, device_id=(lax.rem(iw + j, nw), ino), device_id_type=MESH)
+        pl.semaphore_signal(barrier, inc=1, device_id=fellow(j), device_id_type=MESH)
         return 0
 
-    lax.fori_loop(1, nw, greet, 0)
-    for j in range(1, nn):
+    lax.fori_loop(1, nb, greet, 0)
+    for j in range(1, nn, 2):
         pl.semaphore_signal(barrier, inc=1, device_id=(iw, lax.rem(ino + j, nn)), device_id_type=MESH)
     for k in range(4, 8):
         @pl.when(there[k])
         def _():
             pl.semaphore_signal(barrier, inc=1, device_id=peer(k), device_id_type=MESH)
 
+    beside_x = jnp.minimum(iw, 1) + jnp.minimum(nw - 1 - iw, 1)
+    beside_y = jnp.minimum(ino, 1) + jnp.minimum(nn - 1 - ino, 1)
+    pl.semaphore_wait(barrier, nb - 1 + nn // 2 + beside_x * beside_y)
+
+    def remote(src, dst, ssem, rsem, dev):
+        return pltpu.make_async_remote_copy(src_ref=src, dst_ref=dst, send_sem=ssem, recv_sem=rsem,
+                                            device_id=dev, device_id_type=MESH)
+
+    def to_side(side, pairs, rsem):
+        return [remote(src, dst, ss.at[side], rsem.at[OPPOSITE[side]], peer(side)) for src, dst in pairs]
+
+    def e0_sends(side):
+        land = OPPOSITE[side]
+        if side < 2:
+            pairs = []
+            at = 0
+            for ref, width in ((m_hbm, 3), (s_hbm, 2), (c_hbm, 2)):
+                lo = 0 if side == 0 else bx - width
+                pairs.append((ref.at[lo : lo + width], rx.at[land, at : at + width]))
+                at += width
+            return to_side(side, pairs, e0r)
+        if side < 4:
+            return to_side(side, [(yp.at[side - 2], ry.at[land - 2])], e0r)
+        return to_side(side, [(cp.at[side - 4], rcn.at[land - 4])], e0r)
+
+    def each(fn, sides=range(8)):
+        for side in sides:
+            @pl.when(there[side])
+            def _():
+                fn(side)
+
+    def start(copies):
+        for copy in copies:
+            copy.start()
+
+    each(lambda k: start(e0_sends(k)), (0, 1))
     for copy in inputs:
         copy.wait()
     for side, (m_lo, r_lo) in enumerate(((0, 0), (by - 3, by - 2))):
@@ -242,30 +289,7 @@
                                          (s_ref, xa, ya), (c_ref, xa, ya))):
             cp[k - 4, i : i + 1, :] = ref[x, y : y + 1, :]
 
-    beside_x = jnp.minimum(iw, 1) + jnp.minimum(nw - 1 - iw, 1)
-    beside_y = jnp.minimum(ino, 1) + jnp.minimum(nn - 1 - ino, 1)
-    pl.semaphore_wait(barrier, nw + nn - 2 + beside_x * beside_y)
-
-    def remote(src, dst, ssem, rsem, dev):
-        return pltpu.make_async_remote_copy(src_ref=src, dst_ref=dst, send_sem=ssem, recv_sem=rsem,
-                                            device_id=dev, device_id_type=MESH)
-
-    def to_side(side, pairs, rsem):
-        return [remote(src, dst, ss.at[side], rsem.at[OPPOSITE[side]], peer(side)) for src, dst in pairs]
-
-    def e0_sends(side):
-        land = OPPOSITE[side]
-        if side < 2:
-            pairs = []
-            at = 0
-            for ref, width in ((m_ref, 3), (s_ref, 2), (c_ref, 2)):
-                lo = 0 if side == 0 else bx - width
-                pairs.append((ref.at[lo : lo + width], rx.at[land, at : at + width]))
-                at += width
-            return to_side(side, pairs, e0r)
-        if side < 4:
-            return to_side(side, [(yp.at[side - 2], ry.at[land - 2])], e0r)
-        return to_side(side, [(cp.at[side - 4], rcn.at[land - 4])], e0r)
+    each(lambda k: start(e0_sends(k)), (2, 3, 4, 5, 6, 7))
 
     def box1(side, sending, width, corner):
         dx, dy = SIDES[side]
@@ -290,21 +314,9 @@
             pltpu.make_async_copy(view, view, rsem.at[side]).wait()
         return fn
 
-    def each(fn, sides=range(8)):
-        for side in sides:
-            @pl.when(there[side])
-            def _():
-                fn(side)
-
-    def start(copies):
-        for copy in copies:
-            copy.start()
-
     def e0_landed(side):
         view = rx.at[side] if side < 2 else (ry.at[side - 2] if side < 4 else rcn.at[side - 4])
         pltpu.make_async_copy(view, view, e0r.at[side]).wait()
-
-    each(lambda k: start(e0_sends(k)), (0, 1, 2, 3, 4, 5, 6, 7))
 
     own_y = slice(b1y, 2 * b1y)
     for i in range(b1x):
@@ -315,30 +327,20 @@
         quads = [y_pairs(m1[0, H1 + 2 * k, own_y, :] + m1[0, H1 + 2 * k + 1, own_y, :]) for k in (i, i + 1)]
         mob2 = 0.125 * z_pairs(top_bottom(quads[0], quads[1]))
         sm2[i * b2y : (i + 2) * b2y, :] = mob2
-        gm[ino, iw, i * b2y : (i + 2) * b2y, :] = mob2
-
-    def over_wide(src, dst, kind):
+        gm[odd, me, i * b2y : (i + 2) * b2y, :] = mob2
+
+    def to_fellows(src, dst, kind):
         def step(j, _):
-            to = lax.rem(iw + j, nw)
-            remote(src, dst(iw), gs.at[kind], gq.at[kind], (to, ino)).start()
+            remote(src, dst, gs.at[kind], gq.at[kind], fellow(j)).start()
             return 0
 
-        lax.fori_loop(1, nw, step, 0)
-
-    def over_narrow(src, dst, kind):
-        for j in range(1, nn):
-            to = lax.rem(ino + j, nn)
-            remote(src, dst(ino), gs.at[kind], gq.at[kind], (iw, to)).start()
+        lax.fori_loop(1, nb, step, 0)
+
+    def to_twin(src, dst, kind):
+        remote(src, dst, gs.at[kind], gq.at[kind], (iw, twin)).start()
 
     def landed(view, kind):
         pltpu.make_async_copy(view, view, gq.at[kind]).wait()
-
-    wide_m = lambda: landed(gm.at[0, 0 : nw - 1], 0)
-    narrow_m = lambda: landed(gm.at[0 : nn - 1], 1)
-    wide_r = lambda: landed(gr.at[0, 0 : nw - 1], 2)
-    narrow_r = lambda: landed(gr.at[0 : nn - 1], 3)
-    wide_p = lambda: landed(gp.at[0 : nw - 1], 4)
-    narrow_p = lambda: landed(pbs.at[0 : nn - 1], 5)
 
     for ref, src, width in ((m0, m_ref, 3), (rs0, s_ref, 2), (rc0, c_ref, 2)):
         blank = jnp.zeros(m0.shape[1:], F32)
@@ -375,8 +377,6 @@
 
     build(m0, cx0, cy0, cz0, rd0, d0, H0 + 1, bx - 2, BASE_TAU, nz, 2, firsts0)
     sweep((us0, uc0), (vs0, vc0), (rs0, rc0), ops0, H0 + 2, bx - 4, 2)
-    each(lambda k: start(level1_sends(m1, m1r, k, 3, 3)))
-    over_wide(sm2, lambda w: gm.at[ino, w], 0)
 
     def down0(i, carry):
         num, den = carry
@@ -398,6 +398,7 @@
     part0 = lax.fori_loop(2, b1x - 2, down0, (zero8, zero8))
 
     each(e0_landed, (0, 1, 4, 5, 6, 7))
+    each(lambda k: start(level1_sends(m1, m1r, k, 3, 3)))
     for ref, at, width in fields:
         for i in range(width):
             ref[H0 - width + i, H0 : H0 + by, :] = rx[0, at + i]
@@ -409,16 +410,15 @@
         for i, (ref, x, y) in enumerate(((m0, xa, ya), (m0, xa, yb), (m0, xb, ya), (rs0, xa, ya), (rc0, xa, ya))):
             ref[x, y : y + 1, :] = rcn[k, i : i + 1, :]
     for lo, v_lo in ((H0 - 2, H0 - 1), (H0 + bx - 1, H0 + bx - 2)):
-        build(m0, cx0, cy0, cz0, rd0, d0, lo, 3, BASE_TAU, nz, 1, firsts0)
-        sweep((us0, uc0), (vs0, vc0), (rs0, rc0), ops0, v_lo, 3, 1)
+        build(m0, cx0, cy0, cz0, rd0, d0, lo, 3, BASE_TAU, nz, 3, firsts0)
+        sweep((us0, uc0), (vs0, vc0), (rs0, rc0), ops0, v_lo, 3, 3)
     part0 = lax.fori_loop(0, 2, down0, part0)
     num0, den0 = lax.fori_loop(b1x - 2, b1x, down0, part0)
     for v in range(2):
         for i in range(b1x):
             r1[v, H1 + i, own_y, :] = 0.125 * yz_pairs(t0, v, i * m0.shape[1] + H0)
     each(lambda k: start(level1_sends(r1, r1r, k, 2, 1)))
-    wide_m()
-    over_narrow(gm.at[ino], lambda n: gm.at[n], 1)
+    to_fellows(sm2, gm.at[odd, me], 0)
     for side, (x_far, x_near) in enumerate(((H0 + 1, H0), (H0 + bx - 2, H0 + bx - 1))):
         for v, ref in enumerate((vs0, vc0)):
             xv[side, v, 0:by, :] = ref[x_far, H0 : H0 + by, :]
@@ -433,10 +433,9 @@
         src, dst = (xv.at[side], hx.at[land]) if side < 2 else (yv.at[side - 2], hy.at[land - 2])
         return to_side(side, [(src, dst)], v0r)
 
-    each(lambda k: start(v0_sends(k)), range(4))
     each(level1_landed(m1, m1r, 3, 3))
     ops1 = (cx1, cy1, cz1, rd1, d1)
-    build(m1.at[0], cx1, cy1, cz1, rd1, d1, H1 - 3, b1x + 6, BASE_TAU / 4, z1, 2)
+    build(m1.at[0], cx1, cy1, cz1, rd1, d1, H1 - 3, b1x + 6, BASE_TAU / 4, z1, b1x // 2 + 3)
     each(level1_landed(r1, r1r, 2, 1))
     rr1 = (r1.at[0], r1.at[1])
     uu1 = (u1.at[0], u1.at[1])
@@ -446,8 +445,8 @@
         for v in range(2):
             u1[v, a] = rd1[a] * r1[v, a]
 
-    slabs(H1 - 2, b1x + 4, 2, first1)
-    sweep(uu1, vv1, rr1, ops1, H1 - 1, b1x + 2, 2)
+    slabs(H1 - 2, b1x + 4, b1x + 4, first1)
+    sweep(uu1, vv1, rr1, ops1, H1 - 1, b1x + 2, b1x // 2 + 1)
     num1, den1 = zero8, zero8
     quads = []
     for i in range(b2x):
@@ -465,23 +464,25 @@
             packed = [z_pairs(top_bottom(quads[i - 1][v], quads[i][v])) for v in range(2)]
             own2 = 0.125 * jnp.where(iota(TILE, 1) < z2, packed[0], packed[1])
             sr2[(i - 1) * b2y : (i + 1) * b2y, :] = own2
-            gr[ino, iw, (i - 1) * b2y : (i + 1) * b2y, :] = own2
-    over_wide(sr2, lambda w: gr.at[ino, w], 2)
+            gr[odd, me, (i - 1) * b2y : (i + 1) * b2y, :] = own2
+    to_fellows(sr2, gr.at[odd, me], 2)
     num_row = jnp.sum(num0 + 8.0 * num1, axis=0, keepdims=True)
     den_row = jnp.sum(den0 + 8.0 * den1, axis=0, keepdims=True)
     row8 = iota(TILE, 0)
     part = jnp.where(row8 == 0, num_row, jnp.where(row8 == 1, den_row, 0.0))
     sp2[...] = part
-    gp[iw] = part
-    over_wide(sp2, lambda w: gp.at[w], 4)
-
-    narrow_m()
+    gp[me] = part
+    to_fellows(sp2, gp.at[me], 4)
+
+    landed(gm.at[0, 0 : nb - 1], 0)
+    to_twin(gm.at[odd], gm.at[odd], 1)
+    landed(gm.at[0], 1)
 
     def unpack(src, dst):
         def step(w, _):
             for n in range(nn):
                 for i in range(b2x):
-                    dst[PAD2 + w * b2x + i, n * b2y : (n + 1) * b2y, :] = src[n, w, i * b2y : (i + 1) * b2y, :]
+                    dst[PAD2 + w * b2x + i, n * b2y : (n + 1) * b2y, :] = src[n % 2, n // 2 * nw + w, i * b2y : (i + 1) * b2y, :]
             return 0
 
         lax.fori_loop(0, nw, step, 0)
@@ -508,8 +509,8 @@
     coarsen_pairs(lambda a: v3[a], x4, PAD, v4)
     build(v4, cx4, cy4, cz4, rd4, None, PAD, x4, BASE_TAU / 256, z2 // 4, 4)
 
-    wide_r()
-    over_narrow(gr.at[ino], lambda n: gr.at[n], 3)
+    landed(gr.at[0, 0 : nb - 1], 2)
+    to_twin(gr.at[odd], gr.at[odd], 3)
 
     def v1_sends(side):
         land = OPPOSITE[side]
@@ -517,27 +518,19 @@
         for v in range(2):
             lo = H1 if side == 0 else H1 + b1x - 3
             pairs.append((v1.at[v, lo : lo + 3], h1.at[land, 3 * v : 3 * v + 3]))
-        for v in range(2):
-            lo = H1 if side == 0 else H1 + b1x - 2
-            pairs.append((r1.at[v, lo : lo + 2], h1.at[land, 6 + 2 * v : 8 + 2 * v]))
+        far = H1 + 1 if side == 0 else H1 + b1x - 2
+        for i, rows in enumerate(side_rows):
+            pairs.append((r1.at[:, far, rows], hc.at[land, i]))
         return to_side(side, pairs, v1r)
 
     each(lambda k: start(v1_sends(k)), range(2))
+    each(lambda k: start(v0_sends(k)), range(4))
 
     def v0_landed(side):
         view = hx.at[side] if side < 2 else hy.at[side - 2]
         pltpu.make_async_copy(view, view, v0r.at[side]).wait()
 
-    each(v0_landed, range(4))
-    for side, (x_far, x_near) in enumerate(((H0 - 2, H0 - 1), (H0 + bx + 1, H0 + bx))):
-        for v, ref in enumerate((vs0, vc0)):
-            ref[x_far, H0 : H0 + by, :] = hx[side, v, 0:by, :]
-            ref[x_near, H0 - 1 : H0, :] = hx[side, v, by : by + 1, :]
-            ref[x_near, H0 + by : H0 + by + 1, :] = hx[side, v, by + 1 : by + 2, :]
-    for side, col in enumerate((H0 - 2, H0 + by + 1)):
-        for v, ref in enumerate((vs0, vc0)):
-            ref[H0 : H0 + bx, col, :] = hy[side, v]
-    narrow_r()
+    landed(gr.at[0], 3)
     unpack(gr, r2)
 
     ops2 = (cx2, cy2, cz2, rd2, None)
@@ -548,36 +541,36 @@
         def first(a):
             u[a] = ops[3][a] * r[a]
 
-        slabs(pad, xc, 4, first)
-        sweep((u,), (v,), (r,), ops, pad, xc, 8)
+        slabs(pad, xc, 8, first)
+        sweep((u,), (v,), (r,), ops, pad, xc, min(xc, 16) if u.shape[1] == 8 else 8)
 
     down(u2, v2, r2, ops2, PAD2, x2)
     low2 = iota(v2.shape[1:], 1) < z2
 
     def coarsen2(g, carry):
         num, den = carry
-        for k in range(2):
+        for k in range(4):
             pair = []
             for j in range(2):
-                a = PAD2 + 2 * (2 * g + k) + j
+                a = PAD2 + 2 * (4 * g + k) + j
                 v, e = residual(v2, r2, a, ops2)
                 both = jnp.where(low2, e + r2[a], 0.0)
                 num = num + fold(both * shift(v, z2, 1))
                 den = den + fold(both * v)
                 pair.append(e)
-            r3[PAD + 2 * g + k] = coarsen(pair[0] + pair[1])
+            r3[PAD + 4 * g + k] = coarsen(pair[0] + pair[1])
         return num, den
 
-    num2, den2 = lax.fori_loop(0, x3 // 2, coarsen2, (zero8, zero8))
-    wide_p()
+    num2, den2 = lax.fori_loop(0, x3 // 4, coarsen2, (zero8, zero8))
+    landed(gp.at[0 : nb - 1], 4)
     total = gp[0]
-    if nw <= 16:
-        for w in range(1, nw):
+    if nb <= 32:
+        for w in range(1, nb):
             total = total + gp[w]
     else:
-        total = lax.fori_loop(1, nw, lambda w, acc: acc + gp[w], total)
+        total = lax.fori_loop(1, nb, lambda w, acc: acc + gp[w], total)
     pb[...] = total
-    over_narrow(pb, lambda n: pbs.at[n], 5)
+    to_twin(pb, pbs, 5)
     down(u3, v3, r3, ops3, PAD, x3)
     coarsen_pairs(lambda a: residual(v3, r3, a, ops3)[1], x4, PAD, r4)
     down(u4, v4, r4, ops4, PAD, x4)
@@ -591,8 +584,8 @@
         return 0
 
     lax.fori_loop(0, x4 // 4, up3, 0)
-    sweep((v3,), (u3,), (r3,), ops3, PAD, x3, 8)
-    sweep((u3,), (v3,), (r3,), ops3, PAD, x3, 8)
+    sweep((v3,), (u3,), (r3,), ops3, PAD, x3, 16)
+    sweep((u3,), (v3,), (r3,), ops3, PAD, x3, 16)
     low3 = iota(TILE, 1) < z2 // 2
 
     def dots(i, carry):
@@ -615,18 +608,20 @@
     sweep((v2,), (u2,), (r2,), ops2, base - 3, b2x + 6, b2x + 6)
     sweep((u2,), (v2,), (r2,), ops2, base - 2, b2x + 4, b2x + 4)
 
-    narrow_p()
-    whole = total
-    for j in range(1, nn):
-        whole = whole + pbs[lax.rem(ino + j, nn)]
+    landed(pbs, 5)
+    whole = total + pbs[...]
     num = jnp.sum(jnp.where(row8 == 0, whole, 0.0) + 64.0 * num2 + 512.0 * num3)
     den = jnp.sum(jnp.where(row8 == 1, whole, 0.0) + 64.0 * den2 + 512.0 * den3)
     ratio = (jnp.full(TILE, num) / (1.0 + jnp.full(TILE, den)))[0:1, :]
 
     def v1_landed(side):
-        pltpu.make_async_copy(h1.at[side], h1.at[side], v1r.at[side]).wait()
+        view = tok.at[0 : 6 * 3 * b1y // 8 + 4 * b1y // 8]
+        pltpu.make_async_copy(view, view, v1r.at[side]).wait()
 
     each(v1_landed, range(2))
+    for side, a in enumerate((H1 - 2, H1 + b1x + 1)):
+        for i, rows in enumerate(side_rows):
+            r1[:, a, rows] = hc[side, i]
     rows2 = v2.shape[1]
     full_y = 2 * rows2
     for i in range(b2x + 4):
@@ -645,15 +640,22 @@
         vs, vc = (h1[side, at], h1[side, 3 + at]) if far else (v1[0, a], v1[1, a])
         u1[0, a] = vc - ratio * vs + f1p[x // 2 + 2, window, :]
         if -2 <= x < b1x + 2:
-            at = x + 2 if x < 0 else x - b1x
-            rs, rc = (h1[side, 6 + at], h1[side, 8 + at]) if far else (r1[0, a], r1[1, a])
-            w1[a] = rc - ratio * rs
-    sweep((u1.at[0],), (u1.at[1],), (w1,), ops1, H1 - 2, b1x + 4, 2)
-    sweep((u1.at[1],), (u1.at[0],), (w1,), ops1, H1 - 1, b1x + 2, 2)
-
+            w1[a] = r1[1, a] - ratio * r1[0, a]
+    sweep((u1.at[0],), (u1.at[1],), (w1,), ops1, H1 - 2, b1x + 4, b1x // 2 + 2)
+    sweep((u1.at[1],), (u1.at[0],), (w1,), ops1, H1 - 1, b1x + 2, b1x // 2 + 1)
+
+    each(v0_landed, range(4))
+    for side, (x_far, x_near) in enumerate(((H0 - 2, H0 - 1), (H0 + bx + 1, H0 + bx))):
+        for v, ref in enumerate((vs0, vc0)):
+            ref[x_far, H0 : H0 + by, :] = hx[side, v, 0:by, :]
+            ref[x_near, H0 - 1 : H0, :] = hx[side, v, by : by + 1, :]
+            ref[x_near, H0 + by : H0 + by + 1, :] = hx[side, v, by + 1 : by + 2, :]
+    for side, col in enumerate((H0 - 2, H0 + by + 1)):
+        for v, ref in enumerate((vs0, vc0)):
+            ref[H0 : H0 + bx, col, :] = hy[side, v]
     ratio0 = jnp.concatenate([ratio] * (nz // 128), axis=1)
 
-    def up0(i, _):
+    def up0(i):
         tiles = [u1[0, H1 - 1 + i, 8 * j : 8 * j + 8, :] for j in range(3)]
         rows = [top_bottom(y_repeat(tiles[0], 6), y_repeat(tiles[1], -2)),
                 y_repeat(tiles[1], 2),
@@ -663,21 +665,20 @@
             a = H0 - 2 + 2 * i + k
             us0[a] = vc0[a] - ratio0 * vs0[a] + add
             rc0[a] = rc0[a] - ratio0 * rs0[a]
-        return 0
-
-    lax.fori_loop(0, b1x + 2, up0, 0)
-    sweep((us0,), (uc0,), (rc0,), ops0, H0 - 1, bx + 2, 2)
+
+    slabs(0, b1x + 2, 2, up0)
+    sweep((us0,), (uc0,), (rc0,), ops0, H0 - 1, bx + 2, 3)
 
     def last(a):
         own, t = neighbours(uc0, a, cx0, cy0, cz0)
         out_ref[a - H0] = (KEEP * own + rd0[a] * (rc0[a] + t))[H0 : H0 + by]
 
-    slabs(H0, bx, 2, last)
+    slabs(H0, bx, 4, last)
 
     def sent(side):
         dx, dy = SIDES[side]
         if dy == 0:
-            tiles = 7 * by * nz // 1024 + 3 + 4 + 2 * (by + 8) * nz // 1024 + 30
+            tiles = 7 * by * nz // 1024 + 3 + 4 + 2 * (by + 8) * nz // 1024 + 18 + 4
         elif dx == 0:
             tiles = 7 * bx * nz // 1024 + b1x + 2 * b1x + 2 * bx * nz // 1024
         else:
@@ -686,8 +687,8 @@
         pltpu.make_async_copy(view, view, ss.at[side]).wait()
 
     each(sent)
-    for kind, view in enumerate((gm.at[0, 0 : nw - 1], gm.at[0 : nn - 1], gr.at[0, 0 : nw - 1],
-                                 gr.at[0 : nn - 1], gp.at[0 : nw - 1], pbs.at[0 : nn - 1])):
+    for kind, view in enumerate((gm.at[0, 0 : nb - 1], gm.at[0], gr.at[0, 0 : nb - 1], gr.at[0],
+                                 gp.at[0 : nb - 1], pbs)):
         pltpu.make_async_copy(view, view, gs.at[kind]).wait()
 
 
@@ -709,10 +710,10 @@
             [own] * 3 + [l0] * 12
             + [(2, 7, by, nz), (2, 7, bx, nz), (2, 7, bx, nz), (4, 8, nz), (4, 8, nz)]
             + [(2, 2, by + 8, nz)] * 2 + [(2, 2, bx, nz)] * 2
-            + [(1, *l1)] + [l1] * 5 + [(2, *l1)] * 3 + [l1] + [(2, 10, 3 * b1y, z1)]
+            + [(1, *l1)] + [l1] * 5 + [(2, *l1)] * 3 + [l1] + [(2, 6, 3 * b1y, z1), (2, 2, 2, b1y, z1)]
             + [l2] * 7 + [l3] * 7 + [l4] * 7
             + [(2, 2, b1x * l0[1], nz // 2)]
-            + [own2, own2, TILE, (nn, nw, *own2), (nn, nw, *own2), (nw, *TILE), TILE, (nn, *TILE)]
+            + [own2, own2, TILE, (2, nn // 2 * nw, *own2), (2, nn // 2 * nw, *own2), (nn // 2 * nw, *TILE), TILE, TILE]
             + [(bx // 4 + 4, 2 * y2 + 2 * b1y, z1), (128, *TILE)]
         )
         size = sum(4 * functools.reduce(lambda p, q: p * q, shape) for shape in buffers)
@@ -726,7 +727,7 @@
             out_specs=pl.BlockSpec(memory_space=pltpu.VMEM),
             scratch_shapes=scratch,
             compiler_params=pltpu.CompilerParams(
-                collective_id=0, has_side_effects=True, vmem_limit_bytes=min(67043328, size + (8 << 20))
+                collective_id=0, has_side_effects=True, vmem_limit_bytes=GRANT if size < GRANT else 67043328
             ),
         )(mobility, sav_vector, cotangent)
 

time: 41.5 us -> 33.8 us (0.81)
  the two profiles are of different devices: /device:TPU:1 before, /device:TPU:8 now
where the time goes in v2:
time: 33.8 us; the launch traced here: 33.7 us
  Pallas kernels  33 us (98%)
  local copies, waits for them, and re-layouts  0.71 us (2%)
    pallas_call x1, Pallas kernels, per_device(): pl.pallas_call(functools.partial(kernel, nw, nn, bx, by, nz), out_shape=j...  33 us
    unnamed x1, local copies, waits for them, and re-layouts  0.71 us

profile of v2, /device:TPU:8, one launch (start us, length us, event | category | flops | bytes accessed | tf_op | source)
XLA Modules:
  0.0 33.7 jit_solution(16217641189559953805)
XLA Ops:
  0.0 33.0 %shard_map.37 = f32[16,16,256]{2,1,0:T(8,128)S(1)} custom-call(f32[16,16,256]{2,1,0:T(8,128)} %m_hbm.1, f32[16,16,256]{2,1,0:T(8,128)} %s_hbm.1, f32[16,16,256]{2,1,0:T(8,128)} %c_hbm.1), custom_call_target="tpu_custom_call" | custom-call | tf_op jit(solution)/shard_map/pallas_call | solution.py:723
  33.0 0.7 %copy.5 = f32[16,16,256]{2,1,0:T(8,128)} copy(f32[16,16,256]{2,1,0:T(8,128)S(1)} %shard_map.37) | data formatting | bytes 524288

commit v3 on v2

--- a/solution.py
+++ b/solution.py
@@ -162,13 +162,13 @@
 def kernel(nw, nn, bx, by, nz, m_hbm, s_hbm, c_hbm, out_ref,
            m_ref, s_ref, c_ref,
            m0, cx0, cy0, cz0, rd0, d0, rs0, rc0, us0, uc0, vs0, vc0,
-           rx, yp, ry, cp, rcn, xv, hx, yv, hy,
-           m1, cx1, cy1, cz1, rd1, d1, r1, u1, v1, w1, h1, hc,
+           rx, yp, ry, cp, rcn, xv, hx, yv, hy, xu, hu,
+           m1, cx1, cy1, cz1, rd1, d1, r1, u1, v1, w1, h1, hc, cv1, cs1, cr1,
            cx2, cy2, cz2, rd2, r2, u2, v2,
            cx3, cy3, cz3, rd3, r3, u3, v3,
            cx4, cy4, cz4, rd4, r4, u4, v4,
            t0, sm2, sr2, sp2, gm, gr, gp, pb, pbs, f1p, tok,
-           ins, ss, gs, gq, e0r, m1r, r1r, v0r, v1r):
+           ins, ss, gs, gq, e0r, m1r, r1r, v0r, v1r, u0r):
     iw, ino = lax.axis_index("wide"), lax.axis_index("narrow")
     b1x, b1y, z1 = bx // 2, by // 2, nz // 2
     b2x, b2y, z2 = bx // 4, by // 4, nz // 4
@@ -193,16 +193,15 @@
         ref[index] = jnp.zeros(ref[index].shape, F32)
 
     for k in range(2):
-        for ref in (rx, ry, hx, hy):
+        for ref in (rx, ry, hx, hy, hu):
             for i in range(ref.shape[1]):
                 clear(ref, (k, i))
     for k in range(4):
         clear(rcn, k)
     for k in range(2):
-        for i in range(h1.shape[1]):
-            clear(h1, (k, i))
-        for i in range(2):
-            clear(hc, (k, i))
+        clear(h1, k)
+        clear(hc, k)
+        clear(cr1, k)
     side_rows = (slice(0, b1y), slice(2 * b1y, 3 * b1y))
     for a in (0, 1, 2, 3, H1 + b1x, H1 + b1x + 1, H1 + b1x + 2, H1 + b1x + 3):
         clear(m1, (0, a))
@@ -222,14 +221,23 @@
     twin = ino + 1 - 2 * odd
 
     def fellow(j):
-        to = lax.rem(me + j, nb)
-        return lax.rem(to, nw), 2 * (to // nw) + odd
-
-    def greet(j, _):
-        pl.semaphore_signal(barrier, inc=1, device_id=fellow(j), device_id_type=MESH)
-        return 0
-
-    lax.fori_loop(1, nb, greet, 0)
+        to = me + j
+        to = jnp.where(to >= nb, to - nb, to)
+        row = to // nw
+        return to - row * nw, 2 * row + odd
+
+    def over_fellows(fn):
+        if nb <= 16:
+            for j in range(1, nb):
+                fn(j)
+        else:
+            def step(j, _):
+                fn(j)
+                return 0
+
+            lax.fori_loop(1, nb, step, 0)
+
+    over_fellows(lambda j: pl.semaphore_signal(barrier, inc=1, device_id=fellow(j), device_id_type=MESH))
     for j in range(1, nn, 2):
         pl.semaphore_signal(barrier, inc=1, device_id=(iw, lax.rem(ino + j, nn)), device_id_type=MESH)
     for k in range(4, 8):
@@ -253,7 +261,7 @@
         if side < 2:
             pairs = []
             at = 0
-            for ref, width in ((m_hbm, 3), (s_hbm, 2), (c_hbm, 2)):
+            for ref, width in ((m_hbm, 2), (s_hbm, 1), (c_hbm, 1)):
                 lo = 0 if side == 0 else bx - width
                 pairs.append((ref.at[lo : lo + width], rx.at[land, at : at + width]))
                 at += width
@@ -291,9 +299,20 @@
 
     each(lambda k: start(e0_sends(k)), (2, 3, 4, 5, 6, 7))
 
-    def box1(side, sending, width, corner):
+    near1 = ((1, 1), (1, 2), (1, 3), (2, 1), (2, 2), (3, 1))
+    near_m1 = near1 + ((2, 3), (1, 4))
+
+    def inside1(side, i, j):
         dx, dy = SIDES[side]
-        w = corner if dx and dy else width
+        return H1 + i - 1 if dx < 0 else H1 + b1x - i, b1y + j - 1 if dy < 0 else 2 * b1y - j
+
+    def outside1(side, i, j):
+        dx, dy = SIDES[side]
+        return H1 - i if dx < 0 else H1 + b1x + i - 1, b1y - j if dy < 0 else 2 * b1y + j - 1
+
+    def box1(side, sending, width):
+        dx, dy = SIDES[side]
+        w = width
         if sending:
             xlo, w = (H1, w) if dx < 0 else ((H1 + b1x - w, w) if dx > 0 else (H1, b1x))
             ylo = b1y
@@ -302,15 +321,20 @@
             ylo = b1y * (1 + dy)
         return xlo, w, ylo
 
-    def level1_sends(ref, rsem, side, width, corner):
-        sx, w, sy = box1(side, True, width, corner)
-        tx, _, ty = box1(OPPOSITE[side], False, width, corner)
+    def level1_sends(ref, rsem, side, width, kc):
+        if side > 3:
+            return to_side(side, [(cs1.at[kc, side - 4], cr1.at[kc, OPPOSITE[side] - 4])], rsem)
+        sx, w, sy = box1(side, True, width)
+        tx, _, ty = box1(OPPOSITE[side], False, width)
         return to_side(side, [(ref.at[:, sx : sx + w, sy : sy + b1y], ref.at[:, tx : tx + w, ty : ty + b1y])], rsem)
 
-    def level1_landed(ref, rsem, width, corner):
+    def level1_landed(ref, rsem, width, kc):
         def fn(side):
-            tx, w, ty = box1(side, False, width, corner)
-            view = ref.at[:, tx : tx + w, ty : ty + b1y]
+            if side > 3:
+                view = cr1.at[kc, side - 4]
+            else:
+                tx, w, ty = box1(side, False, width)
+                view = ref.at[:, tx : tx + w, ty : ty + b1y]
             pltpu.make_async_copy(view, view, rsem.at[side]).wait()
         return fn
 
@@ -323,6 +347,10 @@
         put_halves(t0, 0, slice(i * by, (i + 1) * by), m_ref[2 * i] + m_ref[2 * i + 1])
     for i in range(b1x):
         m1[0, H1 + i, own_y, :] = 0.125 * yz_pairs(t0, 0, i * by)
+    for k in range(4, 8):
+        for n, (i, j) in enumerate(near_m1):
+            x, y = inside1(k, i, j)
+            cs1[0, k - 4, n : n + 1, :] = m1[0, x, y : y + 1, :]
     for i in range(0, b2x, 2):
         quads = [y_pairs(m1[0, H1 + 2 * k, own_y, :] + m1[0, H1 + 2 * k + 1, own_y, :]) for k in (i, i + 1)]
         mob2 = 0.125 * z_pairs(top_bottom(quads[0], quads[1]))
@@ -330,11 +358,7 @@
         gm[odd, me, i * b2y : (i + 2) * b2y, :] = mob2
 
     def to_fellows(src, dst, kind):
-        def step(j, _):
-            remote(src, dst, gs.at[kind], gq.at[kind], fellow(j)).start()
-            return 0
-
-        lax.fori_loop(1, nb, step, 0)
+        over_fellows(lambda j: remote(src, dst, gs.at[kind], gq.at[kind], fellow(j)).start())
 
     def to_twin(src, dst, kind):
         remote(src, dst, gs.at[kind], gq.at[kind], (iw, twin)).start()
@@ -342,17 +366,22 @@
     def landed(view, kind):
         pltpu.make_async_copy(view, view, gq.at[kind]).wait()
 
-    for ref, src, width in ((m0, m_ref, 3), (rs0, s_ref, 2), (rc0, c_ref, 2)):
+    for ref, src, width in ((m0, m_ref, 2), (rs0, s_ref, 1), (rc0, c_ref, 1)):
         blank = jnp.zeros(m0.shape[1:], F32)
         for i in range(width):
             ref[H0 - 1 - i] = blank
             ref[H0 + bx + i] = blank
 
-        def put(i, _):
+        def put(i):
             ref[H0 + i, H0 : H0 + by, :] = src[i]
-            return 0
-
-        lax.fori_loop(0, bx, put, 0)
+
+        slabs(0, bx, 4, put)
+    for ref in (us0, uc0):
+        ref[H0 - 2] = jnp.zeros(m0.shape[1:], F32)
+        ref[H0 + bx + 1] = jnp.zeros(m0.shape[1:], F32)
+    for a in (0, 1, 2, 3, H1 + b1x, H1 + b1x + 1, H1 + b1x + 2, H1 + b1x + 3):
+        for v in range(2):
+            v1[v, a] = jnp.zeros(v1.shape[2:], F32)
     for ref in (u3, v3, u4, v4):
         zero = jnp.zeros(ref.shape[1:], F32)
         for a in (0, 1, ref.shape[0] - 2, ref.shape[0] - 1):
@@ -375,7 +404,13 @@
     ops0 = (cx0, cy0, cz0, rd0, d0)
     firsts0 = ((rs0, us0), (rc0, uc0))
 
-    build(m0, cx0, cy0, cz0, rd0, d0, H0 + 1, bx - 2, BASE_TAU, nz, 2, firsts0)
+    for side, a in enumerate((H0 + 1, H0 + bx - 2)):
+        build(m0, cx0, cy0, cz0, rd0, d0, a, 1, BASE_TAU, nz, 1, firsts0)
+        for v, ref in enumerate((us0, uc0)):
+            xu[side, v] = ref[a, H0 : H0 + by, :]
+    each(lambda k: start(to_side(k, [(xu.at[k], hu.at[OPPOSITE[k]])], u0r)), (0, 1))
+    each(lambda k: start(level1_sends(m1, m1r, k, 3, 0)))
+    build(m0, cx0, cy0, cz0, rd0, d0, H0 + 2, bx - 4, BASE_TAU, nz, 2, firsts0)
     sweep((us0, uc0), (vs0, vc0), (rs0, rc0), ops0, H0 + 2, bx - 4, 2)
 
     def down0(i, carry):
@@ -397,26 +432,39 @@
     zero8 = jnp.zeros(TILE, F32)
     part0 = lax.fori_loop(2, b1x - 2, down0, (zero8, zero8))
 
+    def u0_landed(side):
+        pltpu.make_async_copy(hu.at[side], hu.at[side], u0r.at[side]).wait()
+
     each(e0_landed, (0, 1, 4, 5, 6, 7))
-    each(lambda k: start(level1_sends(m1, m1r, k, 3, 3)))
-    for ref, at, width in fields:
+    each(u0_landed, (0, 1))
+    for ref, at, width in ((m0, 0, 2), (rs0, 2, 1), (rc0, 3, 1)):
         for i in range(width):
             ref[H0 - width + i, H0 : H0 + by, :] = rx[0, at + i]
             ref[H0 + bx + i, H0 : H0 + by, :] = rx[1, at + i]
+    for v, ref in enumerate((us0, uc0)):
+        ref[H0 - 2, H0 : H0 + by, :] = hu[0, v]
+        ref[H0 + bx + 1, H0 : H0 + by, :] = hu[1, v]
     for k in range(4):
         dx, dy = SIDES[4 + k]
         xa, xb = (H0 - 1, H0 - 2) if dx < 0 else (H0 + bx, H0 + bx + 1)
         ya, yb = (H0 - 1, H0 - 2) if dy < 0 else (H0 + by, H0 + by + 1)
         for i, (ref, x, y) in enumerate(((m0, xa, ya), (m0, xa, yb), (m0, xb, ya), (rs0, xa, ya), (rc0, xa, ya))):
             ref[x, y : y + 1, :] = rcn[k, i : i + 1, :]
-    for lo, v_lo in ((H0 - 2, H0 - 1), (H0 + bx - 1, H0 + bx - 2)):
-        build(m0, cx0, cy0, cz0, rd0, d0, lo, 3, BASE_TAU, nz, 3, firsts0)
+    beyond = m0[H0 - 2]
+    own = m0[H0 - 1]
+    cx0[H0 - 2] = jnp.where(jnp.minimum(own, beyond) > 0.0, rounded(0.5 * BASE_TAU * (own + beyond)), 0.0)
+    for lo, v_lo in ((H0 - 1, H0 - 1), (H0 + bx - 1, H0 + bx - 2)):
+        build(m0, cx0, cy0, cz0, rd0, d0, lo, 2, BASE_TAU, nz, 2, firsts0)
         sweep((us0, uc0), (vs0, vc0), (rs0, rc0), ops0, v_lo, 3, 3)
     part0 = lax.fori_loop(0, 2, down0, part0)
     num0, den0 = lax.fori_loop(b1x - 2, b1x, down0, part0)
     for v in range(2):
         for i in range(b1x):
             r1[v, H1 + i, own_y, :] = 0.125 * yz_pairs(t0, v, i * m0.shape[1] + H0)
+    for k in range(4, 8):
+        for n in range(6):
+            x, y = inside1(k, 1, 1 + n // 2)
+            cs1[1, k - 4, n : n + 1, :] = r1[n % 2, x, y : y + 1, :]
     each(lambda k: start(level1_sends(r1, r1r, k, 2, 1)))
     to_fellows(sm2, gm.at[odd, me], 0)
     for side, (x_far, x_near) in enumerate(((H0 + 1, H0), (H0 + bx - 2, H0 + bx - 1))):
@@ -433,10 +481,18 @@
         src, dst = (xv.at[side], hx.at[land]) if side < 2 else (yv.at[side - 2], hy.at[land - 2])
         return to_side(side, [(src, dst)], v0r)
 
-    each(level1_landed(m1, m1r, 3, 3))
+    each(level1_landed(m1, m1r, 3, 0))
+    for k in range(4, 8):
+        for n, (i, j) in enumerate(near_m1):
+            x, y = outside1(k, i, j)
+            m1[0, x, y : y + 1, :] = cr1[0, k - 4, n : n + 1, :]
     ops1 = (cx1, cy1, cz1, rd1, d1)
     build(m1.at[0], cx1, cy1, cz1, rd1, d1, H1 - 3, b1x + 6, BASE_TAU / 4, z1, b1x // 2 + 3)
     each(level1_landed(r1, r1r, 2, 1))
+    for k in range(4, 8):
+        for n in range(6):
+            x, y = outside1(k, 1, 1 + n // 2)
+            r1[n % 2, x, y : y + 1, :] = cr1[1, k - 4, n : n + 1, :]
     rr1 = (r1.at[0], r1.at[1])
     uu1 = (u1.at[0], u1.at[1])
     vv1 = (v1.at[0], v1.at[1])
@@ -474,6 +530,21 @@
     gp[me] = part
     to_fellows(sp2, gp.at[me], 4)
 
+    def v1_corners(side, ref_v, ref_r, tiles, outward):
+        for d in range(2):
+            corner = 4 + 2 * side + d
+            for n, (i, j) in enumerate(near1 + ((1, 2), (2, 1))):
+                x = (outside1 if outward else inside1)(corner, i, j)[0]
+                y = outside1(corner, i, j)[1]
+                ref = ref_v if n < 6 else ref_r
+                for v in range(2):
+                    if outward:
+                        ref[v, x, y : y + 1, :] = tiles[side, v, d, n : n + 1, :]
+                    else:
+                        tiles[side, v, d, n : n + 1, :] = ref[v, x, y : y + 1, :]
+
+    for side in range(2):
+        v1_corners(side, v1, r1, cv1, False)
     landed(gm.at[0, 0 : nb - 1], 0)
     to_twin(gm.at[odd], gm.at[odd], 1)
     landed(gm.at[0], 1)
@@ -514,14 +585,8 @@
 
     def v1_sends(side):
         land = OPPOSITE[side]
-        pairs = []
-        for v in range(2):
-            lo = H1 if side == 0 else H1 + b1x - 3
-            pairs.append((v1.at[v, lo : lo + 3], h1.at[land, 3 * v : 3 * v + 3]))
-        far = H1 + 1 if side == 0 else H1 + b1x - 2
-        for i, rows in enumerate(side_rows):
-            pairs.append((r1.at[:, far, rows], hc.at[land, i]))
-        return to_side(side, pairs, v1r)
+        lo = H1 if side == 0 else H1 + b1x - 3
+        return to_side(side, [(v1.at[:, lo : lo + 3, own_y], h1.at[land]), (cv1.at[side], hc.at[land])], v1r)
 
     each(lambda k: start(v1_sends(k)), range(2))
     each(lambda k: start(v0_sends(k)), range(4))
@@ -615,13 +680,13 @@
     ratio = (jnp.full(TILE, num) / (1.0 + jnp.full(TILE, den)))[0:1, :]
 
     def v1_landed(side):
-        view = tok.at[0 : 6 * 3 * b1y // 8 + 4 * b1y // 8]
+        view = tok.at[0 : 10]
         pltpu.make_async_copy(view, view, v1r.at[side]).wait()
 
     each(v1_landed, range(2))
-    for side, a in enumerate((H1 - 2, H1 + b1x + 1)):
-        for i, rows in enumerate(side_rows):
-            r1[:, a, rows] = hc[side, i]
+    for side, a in enumerate((H1 - 3, H1 + b1x)):
+        v1[:, a : a + 3, own_y] = h1[side]
+        v1_corners(side, v1, r1, hc, True)
     rows2 = v2.shape[1]
     full_y = 2 * rows2
     for i in range(b2x + 4):
@@ -635,10 +700,7 @@
     window = pl.ds(pl.multiple_of(ino * b1y, 8), 3 * b1y)
     for x in range(-3, b1x + 3):
         a = H1 + x
-        side, at = (0, x + 3) if x < 0 else (1, x - b1x)
-        far = x < 0 or x >= b1x
-        vs, vc = (h1[side, at], h1[side, 3 + at]) if far else (v1[0, a], v1[1, a])
-        u1[0, a] = vc - ratio * vs + f1p[x // 2 + 2, window, :]
+        u1[0, a] = v1[1, a] - ratio * v1[0, a] + f1p[x // 2 + 2, window, :]
         if -2 <= x < b1x + 2:
             w1[a] = r1[1, a] - ratio * r1[0, a]
     sweep((u1.at[0],), (u1.at[1],), (w1,), ops1, H1 - 2, b1x + 4, b1x // 2 + 2)
@@ -678,11 +740,11 @@
     def sent(side):
         dx, dy = SIDES[side]
         if dy == 0:
-            tiles = 7 * by * nz // 1024 + 3 + 4 + 2 * (by + 8) * nz // 1024 + 18 + 4
+            tiles = 6 * by * nz // 1024 + 3 + 4 + 2 * (by + 8) * nz // 1024 + 10
         elif dx == 0:
             tiles = 7 * bx * nz // 1024 + b1x + 2 * b1x + 2 * bx * nz // 1024
         else:
-            tiles = 2 + 3 + 2
+            tiles = 2 + 1 + 1
         view = tok.at[0:tiles]
         pltpu.make_async_copy(view, view, ss.at[side]).wait()
 
@@ -708,9 +770,9 @@
         own2 = (bx // 4 * (by // 4), z1)
         buffers = (
             [own] * 3 + [l0] * 12
-            + [(2, 7, by, nz), (2, 7, bx, nz), (2, 7, bx, nz), (4, 8, nz), (4, 8, nz)]
-            + [(2, 2, by + 8, nz)] * 2 + [(2, 2, bx, nz)] * 2
-            + [(1, *l1)] + [l1] * 5 + [(2, *l1)] * 3 + [l1] + [(2, 6, 3 * b1y, z1), (2, 2, 2, b1y, z1)]
+            + [(2, 4, by, nz), (2, 7, bx, nz), (2, 7, bx, nz), (4, 8, nz), (4, 8, nz)]
+            + [(2, 2, by + 8, nz)] * 2 + [(2, 2, bx, nz)] * 2 + [(2, 2, by, nz)] * 2
+            + [(1, *l1)] + [l1] * 5 + [(2, *l1)] * 3 + [l1] + [(2, 2, 3, b1y, z1), (2, 2, 2, b1y, z1), (2, 2, 2, b1y, z1), (2, 4, *TILE), (2, 4, *TILE)]
             + [l2] * 7 + [l3] * 7 + [l4] * 7
             + [(2, 2, b1x * l0[1], nz // 2)]
             + [own2, own2, TILE, (2, nn // 2 * nw, *own2), (2, nn // 2 * nw, *own2), (nn // 2 * nw, *TILE), TILE, TILE]
@@ -719,7 +781,7 @@
         size = sum(4 * functools.reduce(lambda p, q: p * q, shape) for shape in buffers)
         dma = lambda n: pltpu.SemaphoreType.DMA((n,))
         scratch = [pltpu.VMEM(shape, F32) for shape in buffers]
-        scratch += [dma(n) for n in (3, 8, 6, 6, 8, 8, 8, 4, 2)]
+        scratch += [dma(n) for n in (3, 8, 6, 6, 8, 8, 8, 4, 2, 2)]
         return pl.pallas_call(
             functools.partial(kernel, nw, nn, bx, by, nz),
             out_shape=jax.ShapeDtypeStruct((bx, by, nz), F32),

time: 33.8 us -> 32.2 us (0.953)
  the two profiles are of different devices: /device:TPU:8 before, /device:TPU:1 now
where the time goes in v3:
time: 32.2 us; the launch traced here: 32 us
  Pallas kernels  31.3 us (97%)
  local copies, waits for them, and re-layouts  0.71 us (2%)
    pallas_call x1, Pallas kernels, per_device(): pl.pallas_call(functools.partial(kernel, nw, nn, bx, by, nz), out_shape=j...  31.3 us
    unnamed x1, local copies, waits for them, and re-layouts  0.71 us

profile of v3, /device:TPU:1, one launch (start us, length us, event | category | flops | bytes accessed | tf_op | source)
XLA Modules:
  0.0 32.0 jit_solution(10131122201133836292)
XLA Ops:
  0.0 31.3 %shard_map.37 = f32[16,16,256]{2,1,0:T(8,128)S(1)} custom-call(f32[16,16,256]{2,1,0:T(8,128)} %m_hbm.1, f32[16,16,256]{2,1,0:T(8,128)} %s_hbm.1, f32[16,16,256]{2,1,0:T(8,128)} %c_hbm.1), custom_call_target="tpu_custom_call" | custom-call | tf_op jit(solution)/shard_map/pallas_call | solution.py:785
  31.3 0.7 %copy.5 = f32[16,16,256]{2,1,0:T(8,128)} copy(f32[16,16,256]{2,1,0:T(8,128)S(1)} %shard_map.37) | data formatting | bytes 524288

commit v4 on v3

--- a/solution.py
+++ b/solution.py
@@ -30,7 +30,7 @@
 
 
 def take(value, index, axis):
-    return jnp.take_along_axis(value, index, axis=axis)
+    return jnp.take_along_axis(value, index, axis=axis, mode="promise_in_bounds")
 
 
 def z_pairs(tile):
@@ -69,9 +69,23 @@
     return x.astype(jnp.bfloat16).astype(F32)
 
 
+def loop(count, chunk, body, carry):
+    if count <= chunk:
+        for i in range(count):
+            carry = body(i, carry)
+        return carry
+
+    def step(g, carry):
+        for k in range(chunk):
+            carry = body(g * chunk + k, carry)
+        return carry
+
+    return lax.fori_loop(0, count // chunk, step, carry)
+
+
 def slabs(lo, count, chunk, body):
-    if count == chunk:
-        for k in range(chunk):
+    if count <= chunk:
+        for k in range(count):
             body(lo + k)
         return
 
@@ -164,8 +178,8 @@
            m0, cx0, cy0, cz0, rd0, d0, rs0, rc0, us0, uc0, vs0, vc0,
            rx, yp, ry, cp, rcn, xv, hx, yv, hy, xu, hu,
            m1, cx1, cy1, cz1, rd1, d1, r1, u1, v1, w1, h1, hc, cv1, cs1, cr1,
-           cx2, cy2, cz2, rd2, r2, u2, v2,
-           cx3, cy3, cz3, rd3, r3, u3, v3,
+           cx2, cy2, cz2, rd2, r2, u2, v2, d2,
+           cx3, cy3, cz3, rd3, r3, u3, v3, d3,
            cx4, cy4, cz4, rd4, r4, u4, v4,
            t0, sm2, sr2, sp2, gm, gr, gp, pb, pbs, f1p, tok,
            ins, ss, gs, gq, e0r, m1r, r1r, v0r, v1r, u0r):
@@ -184,35 +198,13 @@
     def peer(side):
         return (iw + SIDES[side][0], ino + SIDES[side][1])
 
-    inputs = [pltpu.make_async_copy(src, dst, ins.at[i])
-              for i, (src, dst) in enumerate(((m_hbm, m_ref), (s_hbm, s_ref), (c_hbm, c_ref)))]
+    inputs = [pltpu.make_async_copy(src, dst, ins.at[0])
+              for src, dst in ((m_hbm, m_ref), (s_hbm, s_ref), (c_hbm, c_ref))]
     for copy in inputs:
         copy.start()
 
     def clear(ref, index):
         ref[index] = jnp.zeros(ref[index].shape, F32)
-
-    for k in range(2):
-        for ref in (rx, ry, hx, hy, hu):
-            for i in range(ref.shape[1]):
-                clear(ref, (k, i))
-    for k in range(4):
-        clear(rcn, k)
-    for k in range(2):
-        clear(h1, k)
-        clear(hc, k)
-        clear(cr1, k)
-    side_rows = (slice(0, b1y), slice(2 * b1y, 3 * b1y))
-    for a in (0, 1, 2, 3, H1 + b1x, H1 + b1x + 1, H1 + b1x + 2, H1 + b1x + 3):
-        clear(m1, (0, a))
-    for a in (H1 - 2, H1 - 1, H1 + b1x, H1 + b1x + 1):
-        for v in range(2):
-            clear(r1, (v, a))
-    for a in range(H1, H1 + b1x):
-        for rows in side_rows:
-            clear(m1, (0, a, rows))
-            for v in range(2):
-                clear(r1, (v, a, rows))
 
     barrier = pltpu.get_barrier_semaphore()
 
@@ -281,8 +273,8 @@
             copy.start()
 
     each(lambda k: start(e0_sends(k)), (0, 1))
-    for copy in inputs:
-        copy.wait()
+    view = tok.at[0 : 3 * bx * by * nz // 1024]
+    pltpu.make_async_copy(view, view, ins.at[0]).wait()
     for side, (m_lo, r_lo) in enumerate(((0, 0), (by - 3, by - 2))):
         for k in range(3):
             yp[side, k] = m_ref[:, m_lo + k, :]
@@ -358,10 +350,10 @@
         gm[odd, me, i * b2y : (i + 2) * b2y, :] = mob2
 
     def to_fellows(src, dst, kind):
-        over_fellows(lambda j: remote(src, dst, gs.at[kind], gq.at[kind], fellow(j)).start())
+        over_fellows(lambda j: remote(src, dst, gs.at[2 if kind > 3 else kind % 2], gq.at[kind], fellow(j)).start())
 
     def to_twin(src, dst, kind):
-        remote(src, dst, gs.at[kind], gq.at[kind], (iw, twin)).start()
+        remote(src, dst, gs.at[2 if kind > 3 else kind % 2], gq.at[kind], (iw, twin)).start()
 
     def landed(view, kind):
         pltpu.make_async_copy(view, view, gq.at[kind]).wait()
@@ -375,24 +367,45 @@
         def put(i):
             ref[H0 + i, H0 : H0 + by, :] = src[i]
 
-        slabs(0, bx, 4, put)
+        slabs(0, bx, bx, put)
+    side_rows = (slice(0, b1y), slice(2 * b1y, 3 * b1y))
+    for k in range(8):
+        @pl.when(jnp.logical_not(there[k]))
+        def _():
+            if k > 3:
+                clear(rcn, k - 4)
+                clear(cr1, (0, k - 4))
+                clear(cr1, (1, k - 4))
+                return
+            lands = ((rx, hx, hu, h1, hc) if k < 2 else (ry, hy))
+            for ref in lands:
+                clear(ref, k % 2)
+            for ref, width in ((m1, 3), (r1, 2)):
+                xlo, w, ylo = box1(k, False, width)
+                clear(ref, (slice(None), slice(xlo, xlo + w), slice(ylo, ylo + b1y)))
+    for a in (0, H1 + b1x + 3):
+        clear(m1, (0, a))
+    for a in (1, 2, 3, H1 + b1x, H1 + b1x + 1, H1 + b1x + 2):
+        for rows in side_rows:
+            clear(m1, (0, a, rows))
+            for v in range(2):
+                clear(r1, (v, a, rows))
     for ref in (us0, uc0):
         ref[H0 - 2] = jnp.zeros(m0.shape[1:], F32)
         ref[H0 + bx + 1] = jnp.zeros(m0.shape[1:], F32)
     for a in (0, 1, 2, 3, H1 + b1x, H1 + b1x + 1, H1 + b1x + 2, H1 + b1x + 3):
         for v in range(2):
             v1[v, a] = jnp.zeros(v1.shape[2:], F32)
-    for ref in (u3, v3, u4, v4):
+    for ref in (u4, v4):
         zero = jnp.zeros(ref.shape[1:], F32)
         for a in (0, 1, ref.shape[0] - 2, ref.shape[0] - 1):
             ref[a] = zero
-    for ref in (u2, v2, r2, cx2, cy2, cz2, rd2):
+    for ref in (u2, v2, r2, cx2, cy2, cz2, rd2, u3, v3, r3, cx3, cy3, cz3, rd3):
         zero = jnp.zeros(ref.shape[1:], F32)
         for a in range(PAD2):
             ref[a] = zero
             ref[ref.shape[0] - 1 - a] = zero
-    for ref in (cx3, cx4):
-        ref[PAD - 1] = jnp.zeros(ref.shape[1:], F32)
+    cx4[PAD - 1] = jnp.zeros(cx4.shape[1:], F32)
 
     each(e0_landed, (2, 3))
     fields = ((m0, 0, 3), (rs0, 3, 2), (rc0, 5, 2))
@@ -410,8 +423,8 @@
             xu[side, v] = ref[a, H0 : H0 + by, :]
     each(lambda k: start(to_side(k, [(xu.at[k], hu.at[OPPOSITE[k]])], u0r)), (0, 1))
     each(lambda k: start(level1_sends(m1, m1r, k, 3, 0)))
-    build(m0, cx0, cy0, cz0, rd0, d0, H0 + 2, bx - 4, BASE_TAU, nz, 2, firsts0)
-    sweep((us0, uc0), (vs0, vc0), (rs0, rc0), ops0, H0 + 2, bx - 4, 2)
+    build(m0, cx0, cy0, cz0, rd0, d0, H0 + 2, bx - 4, BASE_TAU, nz, bx - 4, firsts0)
+    sweep((us0, uc0), (vs0, vc0), (rs0, rc0), ops0, H0 + 2, bx - 4, bx - 4)
 
     def down0(i, carry):
         num, den = carry
@@ -424,13 +437,13 @@
             num = num + fold_own(both * vc)
             den = den + fold_own(both * vs)
             sums.append((es, ec))
-        at = pl.ds(pl.multiple_of(i * m0.shape[1], 8), m0.shape[1])
+        at = slice(i * m0.shape[1], (i + 1) * m0.shape[1])
         put_halves(t0, 0, at, sums[0][0] + sums[1][0])
         put_halves(t0, 1, at, sums[0][1] + sums[1][1])
         return num, den
 
     zero8 = jnp.zeros(TILE, F32)
-    part0 = lax.fori_loop(2, b1x - 2, down0, (zero8, zero8))
+    part0 = loop(b1x - 4, b1x - 4, lambda i, c: down0(2 + i, c), (zero8, zero8))
 
     def u0_landed(side):
         pltpu.make_async_copy(hu.at[side], hu.at[side], u0r.at[side]).wait()
@@ -456,8 +469,7 @@
     for lo, v_lo in ((H0 - 1, H0 - 1), (H0 + bx - 1, H0 + bx - 2)):
         build(m0, cx0, cy0, cz0, rd0, d0, lo, 2, BASE_TAU, nz, 2, firsts0)
         sweep((us0, uc0), (vs0, vc0), (rs0, rc0), ops0, v_lo, 3, 3)
-    part0 = lax.fori_loop(0, 2, down0, part0)
-    num0, den0 = lax.fori_loop(b1x - 2, b1x, down0, part0)
+    num0, den0 = loop(2, 2, lambda i, c: down0(b1x - 2 + i, down0(i, c)), part0)
     for v in range(2):
         for i in range(b1x):
             r1[v, H1 + i, own_y, :] = 0.125 * yz_pairs(t0, v, i * m0.shape[1] + H0)
@@ -487,7 +499,7 @@
             x, y = outside1(k, i, j)
             m1[0, x, y : y + 1, :] = cr1[0, k - 4, n : n + 1, :]
     ops1 = (cx1, cy1, cz1, rd1, d1)
-    build(m1.at[0], cx1, cy1, cz1, rd1, d1, H1 - 3, b1x + 6, BASE_TAU / 4, z1, b1x // 2 + 3)
+    build(m1.at[0], cx1, cy1, cz1, rd1, d1, H1 - 3, b1x + 6, BASE_TAU / 4, z1, b1x + 6)
     each(level1_landed(r1, r1r, 2, 1))
     for k in range(4, 8):
         for n in range(6):
@@ -502,7 +514,7 @@
             u1[v, a] = rd1[a] * r1[v, a]
 
     slabs(H1 - 2, b1x + 4, b1x + 4, first1)
-    sweep(uu1, vv1, rr1, ops1, H1 - 1, b1x + 2, b1x // 2 + 1)
+    sweep(uu1, vv1, rr1, ops1, H1 - 1, b1x + 2, b1x + 2)
     num1, den1 = zero8, zero8
     quads = []
     for i in range(b2x):
@@ -524,8 +536,8 @@
     to_fellows(sr2, gr.at[odd, me], 2)
     num_row = jnp.sum(num0 + 8.0 * num1, axis=0, keepdims=True)
     den_row = jnp.sum(den0 + 8.0 * den1, axis=0, keepdims=True)
-    row8 = iota(TILE, 0)
-    part = jnp.where(row8 == 0, num_row, jnp.where(row8 == 1, den_row, 0.0))
+    low1 = iota((1, 128), 1) < 64
+    part = jnp.where(low1, num_row + shift(num_row, 64, 1), den_row + shift(den_row, 64, 1))
     sp2[...] = part
     gp[me] = part
     to_fellows(sp2, gp.at[me], 4)
@@ -548,47 +560,57 @@
     landed(gm.at[0, 0 : nb - 1], 0)
     to_twin(gm.at[odd], gm.at[odd], 1)
     landed(gm.at[0], 1)
-
-    def unpack(src, dst):
-        def step(w, _):
-            for n in range(nn):
-                for i in range(b2x):
-                    dst[PAD2 + w * b2x + i, n * b2y : (n + 1) * b2y, :] = src[n % 2, n // 2 * nw + w, i * b2y : (i + 1) * b2y, :]
-            return 0
-
-        lax.fori_loop(0, nw, step, 0)
-
-    unpack(gm, v2)
-    build(v2, cx2, cy2, cz2, rd2, None, PAD2, x2, BASE_TAU / 16, z2, 8)
-
-    def coarsen(x):
-        if x.shape[0] == 16:
-            return 0.125 * z_pairs(top_bottom(y_pairs(x[0:8]), y_pairs(x[8:16])))
-        return 0.125 * z_pairs(top_bottom(y_pairs(x), 0.0))
-
-    def coarsen_pairs(get, xc, pad, dst):
-        def step(g, _):
-            for k in range(4):
-                a = pad + 2 * (4 * g + k)
-                dst[PAD + 4 * g + k] = coarsen(get(a) + get(a + 1))
-            return 0
-
-        lax.fori_loop(0, xc // 4, step, 0)
-
-    coarsen_pairs(lambda a: v2[a], x3, PAD2, v3)
-    build(v3, cx3, cy3, cz3, rd3, None, PAD, x3, BASE_TAU / 64, z2 // 2, 4)
-    coarsen_pairs(lambda a: v3[a], x4, PAD, v4)
-    build(v4, cx4, cy4, cz4, rd4, None, PAD, x4, BASE_TAU / 256, z2 // 4, 4)
-
-    landed(gr.at[0, 0 : nb - 1], 2)
-    to_twin(gr.at[odd], gr.at[odd], 3)
-
     def v1_sends(side):
         land = OPPOSITE[side]
         lo = H1 if side == 0 else H1 + b1x - 3
         return to_side(side, [(v1.at[:, lo : lo + 3, own_y], h1.at[land]), (cv1.at[side], hc.at[land])], v1r)
 
     each(lambda k: start(v1_sends(k)), range(2))
+
+    def unpack(src, dst, u=None):
+        def step(w, carry):
+            for i in range(b2x):
+                a = PAD2 + w * b2x + i
+                for n in range(nn):
+                    dst[a, n * b2y : (n + 1) * b2y, :] = src[n % 2, n // 2 * nw + w, i * b2y : (i + 1) * b2y, :]
+                if u is not None:
+                    u[a] = rd2[a] * dst[a]
+            return carry
+
+        loop(nw, 8, step, 0)
+
+    unpack(gm, v2)
+    kept2 = d2 if d2.shape == v2.shape else None
+    build(v2, cx2, cy2, cz2, rd2, kept2, PAD2, x2, BASE_TAU / 16, z2, 16)
+
+    def coarsen_y(x):
+        if x.shape[0] == 16:
+            return top_bottom(y_pairs(x[0:8]), y_pairs(x[8:16]))
+        return top_bottom(y_pairs(x), 0.0)
+
+    def coarsen_z(dst, lo, count):
+        def body(a):
+            dst[a] = 0.125 * z_pairs(dst[a])
+
+        slabs(lo, count, min(count, 16), body)
+
+    def coarsen_pairs(src, dst, xc, pad):
+        def body(i, carry):
+            a = PAD2 + 2 * i
+            dst[pad + i] = coarsen_y(src[a] + src[a + 1])
+            return carry
+
+        loop(xc, 16, body, 0)
+        coarsen_z(dst, pad, xc)
+
+    coarsen_pairs(v2, v3, x3, PAD2)
+    build(v3, cx3, cy3, cz3, rd3, d3, PAD2, x3, BASE_TAU / 64, z2 // 2, 16)
+    coarsen_pairs(v3, v4, x4, PAD)
+    build(v4, cx4, cy4, cz4, rd4, None, PAD, x4, BASE_TAU / 256, z2 // 4, 8)
+
+    landed(gr.at[0, 0 : nb - 1], 2)
+    to_twin(gr.at[odd], gr.at[odd], 3)
+
     each(lambda k: start(v0_sends(k)), range(4))
 
     def v0_landed(side):
@@ -596,37 +618,33 @@
         pltpu.make_async_copy(view, view, v0r.at[side]).wait()
 
     landed(gr.at[0], 3)
-    unpack(gr, r2)
-
-    ops2 = (cx2, cy2, cz2, rd2, None)
-    ops3 = (cx3, cy3, cz3, rd3, None)
+    unpack(gr, r2, u2)
+
+    ops2 = (cx2, cy2, cz2, rd2, kept2)
+    ops3 = (cx3, cy3, cz3, rd3, d3)
     ops4 = (cx4, cy4, cz4, rd4, None)
 
-    def down(u, v, r, ops, pad, xc):
-        def first(a):
-            u[a] = ops[3][a] * r[a]
-
-        slabs(pad, xc, 8, first)
-        sweep((u,), (v,), (r,), ops, pad, xc, min(xc, 16) if u.shape[1] == 8 else 8)
-
-    down(u2, v2, r2, ops2, PAD2, x2)
-    low2 = iota(v2.shape[1:], 1) < z2
-
-    def coarsen2(g, carry):
-        num, den = carry
-        for k in range(4):
+    def coarsen_residual(v, r, ops, dst, xc, pad, seg):
+        low = iota(v.shape[1:], 1) < seg
+
+        def step(i, carry):
+            num, den = carry
             pair = []
             for j in range(2):
-                a = PAD2 + 2 * (4 * g + k) + j
-                v, e = residual(v2, r2, a, ops2)
-                both = jnp.where(low2, e + r2[a], 0.0)
-                num = num + fold(both * shift(v, z2, 1))
-                den = den + fold(both * v)
+                a = PAD2 + 2 * i + j
+                own, e = residual(v, r, a, ops)
+                both = jnp.where(low, e + r[a], 0.0)
+                num = num + fold(both * shift(own, -seg, 1))
+                den = den + fold(both * own)
                 pair.append(e)
-            r3[PAD + 4 * g + k] = coarsen(pair[0] + pair[1])
-        return num, den
-
-    num2, den2 = lax.fori_loop(0, x3 // 4, coarsen2, (zero8, zero8))
+            dst[pad + i] = coarsen_y(pair[0] + pair[1])
+            return num, den
+
+        sums = loop(xc, 16, step, (zero8, zero8))
+        coarsen_z(dst, pad, xc)
+        return sums
+
+    sweep((u2,), (v2,), (r2,), ops2, PAD2, x2, 32)
     landed(gp.at[0 : nb - 1], 4)
     total = gp[0]
     if nb <= 32:
@@ -636,48 +654,58 @@
         total = lax.fori_loop(1, nb, lambda w, acc: acc + gp[w], total)
     pb[...] = total
     to_twin(pb, pbs, 5)
-    down(u3, v3, r3, ops3, PAD, x3)
-    coarsen_pairs(lambda a: residual(v3, r3, a, ops3)[1], x4, PAD, r4)
-    down(u4, v4, r4, ops4, PAD, x4)
-
-    def up3(g, _):
-        for k in range(4):
-            add = y_repeat(z_repeat(v4[PAD + 4 * g + k]))
-            a = PAD + 2 * (4 * g + k)
-            v3[a] = v3[a] + add
-            v3[a + 1] = v3[a + 1] + add
-        return 0
-
-    lax.fori_loop(0, x4 // 4, up3, 0)
-    sweep((v3,), (u3,), (r3,), ops3, PAD, x3, 16)
-    sweep((u3,), (v3,), (r3,), ops3, PAD, x3, 16)
-    low3 = iota(TILE, 1) < z2 // 2
+    num2, den2 = coarsen_residual(v2, r2, ops2, r3, x3, PAD2, z2)
+    def first3(a):
+        u3[a] = rd3[a] * r3[a]
+
+    slabs(PAD2, x3, 16, first3)
+    sweep((u3,), (v3,), (r3,), ops3, PAD2, x3, 16)
+    num3, den3 = coarsen_residual(v3, r3, ops3, r4, x4, PAD, z2 // 2)
+
+    def first4(a):
+        u4[a] = rd4[a] * r4[a]
+
+    slabs(PAD, x4, 8, first4)
+    sweep((u4,), (v4,), (r4,), ops4, PAD, x4, 8)
+    low4 = iota(TILE, 1) < z2 // 4
 
     def dots(i, carry):
         num, den = carry
-        for k in range(4):
-            a = PAD + 4 * i + k
-            both = jnp.where(low3, v3[a], 0.0)
-            den = den + both * r3[a]
-            num = num + both * shift(r3[a], -(z2 // 2), 1)
+        for k in range(8):
+            a = PAD + 8 * i + k
+            both = jnp.where(low4, r4[a], 0.0)
+            den = den + both * v4[a]
+            num = num + both * shift(v4[a], -(z2 // 4), 1)
         return num, den
 
-    num3, den3 = lax.fori_loop(0, x3 // 4, dots, (zero8, zero8))
+    num4, den4 = dots(0, (zero8, zero8)) if x4 == 8 else lax.fori_loop(0, x4 // 8, dots, (zero8, zero8))
+    b3x = b2x // 2
+    base3 = PAD2 + iw * b3x
+    for i in range(b3x // 2 + 4):
+        add = y_repeat(z_repeat(v4[PAD + iw * (b3x // 2) - 2 + i]))
+        for j in range(2):
+            a = base3 - 4 + 2 * i + j
+            v3[a] = v3[a] + add
+    sweep((v3,), (u3,), (r3,), ops3, base3 - 3, b3x + 6, b3x + 6)
+    sweep((u3,), (v3,), (r3,), ops3, base3 - 2, b3x + 4, b3x + 4)
+    landed(pbs, 5)
+    whole = total + pbs[...]
+
+    def total_of(mask, n2, n3, n4):
+        x = jnp.sum(64.0 * n2 + 512.0 * n3 + 4096.0 * n4, axis=0, keepdims=True)
+        return jnp.sum(x + jnp.where(mask, whole, 0.0), axis=1, keepdims=True)
+
+    ratio = total_of(low1, num2, num3, num4) / (1.0 + total_of(jnp.logical_not(low1), den2, den3, den4))
+    ratio = jnp.broadcast_to(ratio, (1, 128))
     base = PAD2 + iw * b2x
     for i in range(b2x // 2 + 4):
-        wide_tile = z_repeat(v3[PAD + iw * (b2x // 2) - 2 + i])
+        wide_tile = z_repeat(v3[base3 - 2 + i])
         for j in range(2):
             a = base - 4 + 2 * i + j
             v2[a, 0:8, :] = v2[a, 0:8, :] + y_repeat(wide_tile)
             v2[a, 8:16, :] = v2[a, 8:16, :] + y_repeat(wide_tile, 4)
     sweep((v2,), (u2,), (r2,), ops2, base - 3, b2x + 6, b2x + 6)
     sweep((u2,), (v2,), (r2,), ops2, base - 2, b2x + 4, b2x + 4)
-
-    landed(pbs, 5)
-    whole = total + pbs[...]
-    num = jnp.sum(jnp.where(row8 == 0, whole, 0.0) + 64.0 * num2 + 512.0 * num3)
-    den = jnp.sum(jnp.where(row8 == 1, whole, 0.0) + 64.0 * den2 + 512.0 * den3)
-    ratio = (jnp.full(TILE, num) / (1.0 + jnp.full(TILE, den)))[0:1, :]
 
     def v1_landed(side):
         view = tok.at[0 : 10]
@@ -703,8 +731,8 @@
         u1[0, a] = v1[1, a] - ratio * v1[0, a] + f1p[x // 2 + 2, window, :]
         if -2 <= x < b1x + 2:
             w1[a] = r1[1, a] - ratio * r1[0, a]
-    sweep((u1.at[0],), (u1.at[1],), (w1,), ops1, H1 - 2, b1x + 4, b1x // 2 + 2)
-    sweep((u1.at[1],), (u1.at[0],), (w1,), ops1, H1 - 1, b1x + 2, b1x // 2 + 1)
+    sweep((u1.at[0],), (u1.at[1],), (w1,), ops1, H1 - 2, b1x + 4, b1x + 4)
+    sweep((u1.at[1],), (u1.at[0],), (w1,), ops1, H1 - 1, b1x + 2, b1x + 2)
 
     each(v0_landed, range(4))
     for side, (x_far, x_near) in enumerate(((H0 - 2, H0 - 1), (H0 + bx + 1, H0 + bx))):
@@ -717,25 +745,32 @@
             ref[H0 : H0 + bx, col, :] = hy[side, v]
     ratio0 = jnp.concatenate([ratio] * (nz // 128), axis=1)
 
-    def up0(i):
-        tiles = [u1[0, H1 - 1 + i, 8 * j : 8 * j + 8, :] for j in range(3)]
-        rows = [top_bottom(y_repeat(tiles[0], 6), y_repeat(tiles[1], -2)),
-                y_repeat(tiles[1], 2),
-                top_bottom(y_repeat(tiles[1], 6), y_repeat(tiles[2], -2))]
-        add = jnp.concatenate([jnp.concatenate([z_repeat(t), z_repeat(t, 64)], axis=1) for t in rows], axis=0)
+    def up0(g):
+        tiles = [[u1[0, H1 - 1 + 2 * g + k, 8 * j : 8 * j + 8, :] for j in range(3)] for k in range(2)]
+        sub = iota(TILE, 0)
+        ends = [top_bottom(jnp.where(sub < 2, shift(t[0], 2, 0), shift(t[2], 2, 0)), 0.0) for t in tiles]
+        ends = top_bottom(ends[0], shift(ends[1], 4, 0))
+        halves = [[z_repeat(t, start) for t in (ends, tiles[0][1], tiles[1][1])] for start in (0, 64)]
         for k in range(2):
-            a = H0 - 2 + 2 * i + k
-            us0[a] = vc0[a] - ratio0 * vs0[a] + add
-            rc0[a] = rc0[a] - ratio0 * rs0[a]
-
-    slabs(0, b1x + 2, 2, up0)
-    sweep((us0,), (uc0,), (rc0,), ops0, H0 - 1, bx + 2, 3)
+            adds = []
+            for end, mid in ((h[0], h[1 + k]) for h in halves):
+                end = shift(end, -4 * k, 0) if k else end
+                adds.append((top_bottom(y_repeat(end), y_repeat(mid, -2)), y_repeat(mid, 2),
+                             top_bottom(y_repeat(mid, 6), y_repeat(end))))
+            add = jnp.concatenate([jnp.concatenate([adds[0][j], adds[1][j]], axis=1) for j in range(3)], axis=0)
+            for i in range(2):
+                a = H0 - 2 + 4 * g + 2 * k + i
+                us0[a] = vc0[a] - ratio0 * vs0[a] + add
+                rc0[a] = rc0[a] - ratio0 * rs0[a]
+
+    slabs(0, b1x // 2 + 1, b1x // 2 + 1, up0)
+    sweep((us0,), (uc0,), (rc0,), ops0, H0 - 1, bx + 2, bx + 2)
 
     def last(a):
         own, t = neighbours(uc0, a, cx0, cy0, cz0)
         out_ref[a - H0] = (KEEP * own + rd0[a] * (rc0[a] + t))[H0 : H0 + by]
 
-    slabs(H0, bx, 4, last)
+    slabs(H0, bx, bx, last)
 
     def sent(side):
         dx, dy = SIDES[side]
@@ -749,9 +784,8 @@
         pltpu.make_async_copy(view, view, ss.at[side]).wait()
 
     each(sent)
-    for kind, view in enumerate((gm.at[0, 0 : nb - 1], gm.at[0], gr.at[0, 0 : nb - 1], gr.at[0],
-                                 gp.at[0 : nb - 1], pbs)):
-        pltpu.make_async_copy(view, view, gs.at[kind]).wait()
+    for i, view in enumerate((gr.at[:, 0 : nb - 1], gr, gp)):
+        pltpu.make_async_copy(view, view, gs.at[i]).wait()
 
 
 def solution(mesh):
@@ -765,7 +799,7 @@
         l0 = (bx + 2 * H0, by + 2 * H0, nz)
         l1 = (b1x + 2 * H1, 3 * b1y, z1)
         l2 = (x2 + 2 * PAD2, y2, z1)
-        l3 = (x2 // 2 + 2 * PAD, y2 // 2, z1)
+        l3 = (x2 // 2 + 2 * PAD2, y2 // 2, z1)
         l4 = (x2 // 4 + 2 * PAD, 8, z1)
         own2 = (bx // 4 * (by // 4), z1)
         buffers = (
@@ -773,15 +807,15 @@
             + [(2, 4, by, nz), (2, 7, bx, nz), (2, 7, bx, nz), (4, 8, nz), (4, 8, nz)]
             + [(2, 2, by + 8, nz)] * 2 + [(2, 2, bx, nz)] * 2 + [(2, 2, by, nz)] * 2
             + [(1, *l1)] + [l1] * 5 + [(2, *l1)] * 3 + [l1] + [(2, 2, 3, b1y, z1), (2, 2, 2, b1y, z1), (2, 2, 2, b1y, z1), (2, 4, *TILE), (2, 4, *TILE)]
-            + [l2] * 7 + [l3] * 7 + [l4] * 7
+            + [l2] * 7 + [l2 if nw <= 16 else (1, *TILE)] + [l3] * 8 + [l4] * 7
             + [(2, 2, b1x * l0[1], nz // 2)]
-            + [own2, own2, TILE, (2, nn // 2 * nw, *own2), (2, nn // 2 * nw, *own2), (nn // 2 * nw, *TILE), TILE, TILE]
-            + [(bx // 4 + 4, 2 * y2 + 2 * b1y, z1), (128, *TILE)]
+            + [own2, own2, (1, 128), (2, nn // 2 * nw, *own2), (2, nn // 2 * nw, *own2), (nn // 2 * nw, 1, 128), (1, 128), (1, 128)]
+            + [(bx // 4 + 4, 2 * y2 + 2 * b1y, z1), (3 * bx * by * nz // 1024, *TILE)]
         )
         size = sum(4 * functools.reduce(lambda p, q: p * q, shape) for shape in buffers)
         dma = lambda n: pltpu.SemaphoreType.DMA((n,))
         scratch = [pltpu.VMEM(shape, F32) for shape in buffers]
-        scratch += [dma(n) for n in (3, 8, 6, 6, 8, 8, 8, 4, 2, 2)]
+        scratch += [dma(n) for n in (1, 8, 3, 6, 8, 8, 8, 4, 2, 2)]
         return pl.pallas_call(
             functools.partial(kernel, nw, nn, bx, by, nz),
             out_shape=jax.ShapeDtypeStruct((bx, by, nz), F32),

time: 32.2 us -> 28.8 us (0.89)
  the two profiles are of different devices: /device:TPU:1 before, /device:TPU:0 now
where the time goes in v4:
time: 28.8 us; the launch traced here: 28.6 us
  Pallas kernels  27.9 us (97%)
  local copies, waits for them, and re-layouts  0.71 us (2%)
    pallas_call x1, Pallas kernels, per_device(): pl.pallas_call(functools.partial(kernel, nw, nn, bx, by, nz), out_shape=j...  27.9 us
    unnamed x1, local copies, waits for them, and re-layouts  0.71 us

profile of v4, /device:TPU:0, one launch (start us, length us, event | category | flops | bytes accessed | tf_op | source)
XLA Modules:
  0.0 28.6 jit_solution(12037519503521869859)
XLA Ops:
  0.0 27.9 %shard_map.37 = f32[16,16,256]{2,1,0:T(8,128)S(1)} custom-call(f32[16,16,256]{2,1,0:T(8,128)} %m_hbm.1, f32[16,16,256]{2,1,0:T(8,128)} %s_hbm.1, f32[16,16,256]{2,1,0:T(8,128)} %c_hbm.1), custom_call_target="tpu_custom_call" | custom-call | tf_op jit(solution)/shard_map/pallas_call | solution.py:819
  27.9 0.7 %copy.5 = f32[16,16,256]{2,1,0:T(8,128)} copy(f32[16,16,256]{2,1,0:T(8,128)S(1)} %shard_map.37) | data formatting | bytes 524288

commit v5 on v4

--- a/solution.py
+++ b/solution.py
@@ -177,12 +177,12 @@
            m_ref, s_ref, c_ref,
            m0, cx0, cy0, cz0, rd0, d0, rs0, rc0, us0, uc0, vs0, vc0,
            rx, yp, ry, cp, rcn, xv, hx, yv, hy, xu, hu,
-           m1, cx1, cy1, cz1, rd1, d1, r1, u1, v1, w1, h1, hc, cv1, cs1, cr1,
+           m1, cx1, cy1, cz1, rd1, d1, r1, u1, v1, w1, h1, hc, cv1, cs1, cr1, cs2, cr2,
            cx2, cy2, cz2, rd2, r2, u2, v2, d2,
            cx3, cy3, cz3, rd3, r3, u3, v3, d3,
            cx4, cy4, cz4, rd4, r4, u4, v4,
            t0, sm2, sr2, sp2, gm, gr, gp, pb, pbs, f1p, tok,
-           ins, ss, gs, gq, e0r, m1r, r1r, v0r, v1r, u0r):
+           ins, ss, gs, gq, e0r, y0r, m1r, r1r, v0r, v1r, u0r):
     iw, ino = lax.axis_index("wide"), lax.axis_index("narrow")
     b1x, b1y, z1 = bx // 2, by // 2, nz // 2
     b2x, b2y, z2 = bx // 4, by // 4, nz // 4
@@ -246,7 +246,10 @@
                                             device_id=dev, device_id_type=MESH)
 
     def to_side(side, pairs, rsem):
-        return [remote(src, dst, ss.at[side], rsem.at[OPPOSITE[side]], peer(side)) for src, dst in pairs]
+        land = OPPOSITE[side]
+        if rsem is e0r and land > 3:
+            land -= 2
+        return [remote(src, dst, ss.at[side], rsem.at[land], peer(side)) for src, dst in pairs]
 
     def e0_sends(side):
         land = OPPOSITE[side]
@@ -258,9 +261,11 @@
                 pairs.append((ref.at[lo : lo + width], rx.at[land, at : at + width]))
                 at += width
             return to_side(side, pairs, e0r)
-        if side < 4:
-            return to_side(side, [(yp.at[side - 2], ry.at[land - 2])], e0r)
         return to_side(side, [(cp.at[side - 4], rcn.at[land - 4])], e0r)
+
+    def y0_sends(side, lo, hi, sem):
+        land = OPPOSITE[side] - 2
+        return [remote(yp.at[side - 2, lo:hi], ry.at[land, lo:hi], ss.at[side], y0r.at[sem + land], peer(side))]
 
     def each(fn, sides=range(8)):
         for side in sides:
@@ -275,21 +280,25 @@
     each(lambda k: start(e0_sends(k)), (0, 1))
     view = tok.at[0 : 3 * bx * by * nz // 1024]
     pltpu.make_async_copy(view, view, ins.at[0]).wait()
-    for side, (m_lo, r_lo) in enumerate(((0, 0), (by - 3, by - 2))):
-        for k in range(3):
-            yp[side, k] = m_ref[:, m_lo + k, :]
-        for k in range(2):
-            yp[side, 3 + k] = s_ref[:, r_lo + k, :]
-            yp[side, 5 + k] = c_ref[:, r_lo + k, :]
+    def yp_fill(side, at, ref, k):
+        yp[side, at] = ref[:, by - 1 - k if side else k, :]
+
+    for side in range(2):
+        yp_fill(side, 0, m_ref, 0)
+    each(lambda k: start(y0_sends(k, 0, 1, 0)), (2, 3))
+    for side in range(2):
+        for at, (ref, k) in enumerate(((m_ref, 1), (m_ref, 2), (s_ref, 0), (s_ref, 1), (c_ref, 0), (c_ref, 1))):
+            yp_fill(side, 1 + at, ref, k)
+    each(lambda k: start(y0_sends(k, 1, 7, 2)), (2, 3))
     for k in range(4, 8):
         dx, dy = SIDES[k]
         xa, xb = (0, 1) if dx < 0 else (bx - 1, bx - 2)
         ya, yb = (0, 1) if dy < 0 else (by - 1, by - 2)
         for i, (ref, x, y) in enumerate(((m_ref, xa, ya), (m_ref, xa, yb), (m_ref, xb, ya),
                                          (s_ref, xa, ya), (c_ref, xa, ya))):
-            cp[k - 4, i : i + 1, :] = ref[x, y : y + 1, :]
-
-    each(lambda k: start(e0_sends(k)), (2, 3, 4, 5, 6, 7))
+            cp[k - 4, i] = ref[x, y : y + 1, :]
+
+    each(lambda k: start(e0_sends(k)), (4, 5, 6, 7))
 
     near1 = ((1, 1), (1, 2), (1, 3), (2, 1), (2, 2), (3, 1))
     near_m1 = near1 + ((2, 3), (1, 4))
@@ -315,7 +324,8 @@
 
     def level1_sends(ref, rsem, side, width, kc):
         if side > 3:
-            return to_side(side, [(cs1.at[kc, side - 4], cr1.at[kc, OPPOSITE[side] - 4])], rsem)
+            src, dst = (cs2, cr2) if kc else (cs1, cr1)
+            return to_side(side, [(src.at[side - 4], dst.at[OPPOSITE[side] - 4])], rsem)
         sx, w, sy = box1(side, True, width)
         tx, _, ty = box1(OPPOSITE[side], False, width)
         return to_side(side, [(ref.at[:, sx : sx + w, sy : sy + b1y], ref.at[:, tx : tx + w, ty : ty + b1y])], rsem)
@@ -323,7 +333,7 @@
     def level1_landed(ref, rsem, width, kc):
         def fn(side):
             if side > 3:
-                view = cr1.at[kc, side - 4]
+                view = (cr2 if kc else cr1).at[side - 4]
             else:
                 tx, w, ty = box1(side, False, width)
                 view = ref.at[:, tx : tx + w, ty : ty + b1y]
@@ -331,8 +341,16 @@
         return fn
 
     def e0_landed(side):
-        view = rx.at[side] if side < 2 else (ry.at[side - 2] if side < 4 else rcn.at[side - 4])
-        pltpu.make_async_copy(view, view, e0r.at[side]).wait()
+        if side in (2, 3):
+            view = ry.at[side - 2, 1:7]
+            pltpu.make_async_copy(view, view, y0r.at[side]).wait()
+        else:
+            view = rx.at[side] if side < 2 else rcn.at[side - 4]
+            pltpu.make_async_copy(view, view, e0r.at[side if side < 2 else side - 2]).wait()
+
+    def near_landed(side):
+        view = ry.at[side - 2, 0:1]
+        pltpu.make_async_copy(view, view, y0r.at[side - 2]).wait()
 
     own_y = slice(b1y, 2 * b1y)
     for i in range(b1x):
@@ -342,7 +360,7 @@
     for k in range(4, 8):
         for n, (i, j) in enumerate(near_m1):
             x, y = inside1(k, i, j)
-            cs1[0, k - 4, n : n + 1, :] = m1[0, x, y : y + 1, :]
+            cs1[k - 4, n : n + 1, :] = m1[0, x, y : y + 1, :]
     for i in range(0, b2x, 2):
         quads = [y_pairs(m1[0, H1 + 2 * k, own_y, :] + m1[0, H1 + 2 * k + 1, own_y, :]) for k in (i, i + 1)]
         mob2 = 0.125 * z_pairs(top_bottom(quads[0], quads[1]))
@@ -374,8 +392,8 @@
         def _():
             if k > 3:
                 clear(rcn, k - 4)
-                clear(cr1, (0, k - 4))
-                clear(cr1, (1, k - 4))
+                clear(cr1, k - 4)
+                clear(cr2, k - 4)
                 return
             lands = ((rx, hx, hu, h1, hc) if k < 2 else (ry, hy))
             for ref in lands:
@@ -407,23 +425,24 @@
             ref[ref.shape[0] - 1 - a] = zero
     cx4[PAD - 1] = jnp.zeros(cx4.shape[1:], F32)
 
-    each(e0_landed, (2, 3))
-    fields = ((m0, 0, 3), (rs0, 3, 2), (rc0, 5, 2))
-    for ref, at, width in fields:
-        for i in range(width):
-            ref[H0 : H0 + bx, H0 - width + i, :] = ry[0, at + i]
-            ref[H0 : H0 + bx, H0 + by + i, :] = ry[1, at + i]
-
     ops0 = (cx0, cy0, cz0, rd0, d0)
     firsts0 = ((rs0, us0), (rc0, uc0))
-
+    each(near_landed, (2, 3))
+    m0[H0 : H0 + bx, H0 - 1, :] = ry[0, 0]
+    m0[H0 : H0 + bx, H0 + by, :] = ry[1, 0]
     for side, a in enumerate((H0 + 1, H0 + bx - 2)):
         build(m0, cx0, cy0, cz0, rd0, d0, a, 1, BASE_TAU, nz, 1, firsts0)
         for v, ref in enumerate((us0, uc0)):
             xu[side, v] = ref[a, H0 : H0 + by, :]
     each(lambda k: start(to_side(k, [(xu.at[k], hu.at[OPPOSITE[k]])], u0r)), (0, 1))
     each(lambda k: start(level1_sends(m1, m1r, k, 3, 0)))
-    build(m0, cx0, cy0, cz0, rd0, d0, H0 + 2, bx - 4, BASE_TAU, nz, bx - 4, firsts0)
+    each(e0_landed, (2, 3))
+    for ref, at, lo, width in ((m0, 1, 1, 2), (rs0, 3, 0, 2), (rc0, 5, 0, 2)):
+        for i in range(width):
+            ref[H0 : H0 + bx, H0 - 1 - lo - i, :] = ry[0, at + i]
+            ref[H0 : H0 + bx, H0 + by + lo + i, :] = ry[1, at + i]
+
+    build(m0, cx0, cy0, cz0, rd0, d0, H0 + 1, bx - 2, BASE_TAU, nz, bx - 2, firsts0)
     sweep((us0, uc0), (vs0, vc0), (rs0, rc0), ops0, H0 + 2, bx - 4, bx - 4)
 
     def down0(i, carry):
@@ -445,38 +464,44 @@
     zero8 = jnp.zeros(TILE, F32)
     part0 = loop(b1x - 4, b1x - 4, lambda i, c: down0(2 + i, c), (zero8, zero8))
 
+
+    def coarse0(i):
+        for v in range(2):
+            r1[v, H1 + i, own_y, :] = 0.125 * yz_pairs(t0, v, i * m0.shape[1] + H0)
+
+    slabs(2, b1x - 4, b1x - 4, coarse0)
     def u0_landed(side):
         pltpu.make_async_copy(hu.at[side], hu.at[side], u0r.at[side]).wait()
 
     each(e0_landed, (0, 1, 4, 5, 6, 7))
-    each(u0_landed, (0, 1))
     for ref, at, width in ((m0, 0, 2), (rs0, 2, 1), (rc0, 3, 1)):
         for i in range(width):
             ref[H0 - width + i, H0 : H0 + by, :] = rx[0, at + i]
             ref[H0 + bx + i, H0 : H0 + by, :] = rx[1, at + i]
-    for v, ref in enumerate((us0, uc0)):
-        ref[H0 - 2, H0 : H0 + by, :] = hu[0, v]
-        ref[H0 + bx + 1, H0 : H0 + by, :] = hu[1, v]
     for k in range(4):
         dx, dy = SIDES[4 + k]
         xa, xb = (H0 - 1, H0 - 2) if dx < 0 else (H0 + bx, H0 + bx + 1)
         ya, yb = (H0 - 1, H0 - 2) if dy < 0 else (H0 + by, H0 + by + 1)
         for i, (ref, x, y) in enumerate(((m0, xa, ya), (m0, xa, yb), (m0, xb, ya), (rs0, xa, ya), (rc0, xa, ya))):
-            ref[x, y : y + 1, :] = rcn[k, i : i + 1, :]
+            ref[x, y : y + 1, :] = rcn[k, i]
     beyond = m0[H0 - 2]
     own = m0[H0 - 1]
     cx0[H0 - 2] = jnp.where(jnp.minimum(own, beyond) > 0.0, rounded(0.5 * BASE_TAU * (own + beyond)), 0.0)
-    for lo, v_lo in ((H0 - 1, H0 - 1), (H0 + bx - 1, H0 + bx - 2)):
+    for lo in (H0 - 1, H0 + bx - 1):
         build(m0, cx0, cy0, cz0, rd0, d0, lo, 2, BASE_TAU, nz, 2, firsts0)
+    each(u0_landed, (0, 1))
+    for v, ref in enumerate((us0, uc0)):
+        ref[H0 - 2, H0 : H0 + by, :] = hu[0, v]
+        ref[H0 + bx + 1, H0 : H0 + by, :] = hu[1, v]
+    for v_lo in (H0 - 1, H0 + bx - 2):
         sweep((us0, uc0), (vs0, vc0), (rs0, rc0), ops0, v_lo, 3, 3)
     num0, den0 = loop(2, 2, lambda i, c: down0(b1x - 2 + i, down0(i, c)), part0)
-    for v in range(2):
-        for i in range(b1x):
-            r1[v, H1 + i, own_y, :] = 0.125 * yz_pairs(t0, v, i * m0.shape[1] + H0)
+    for i in (0, 1, b1x - 2, b1x - 1):
+        coarse0(i)
     for k in range(4, 8):
         for n in range(6):
             x, y = inside1(k, 1, 1 + n // 2)
-            cs1[1, k - 4, n : n + 1, :] = r1[n % 2, x, y : y + 1, :]
+            cs2[k - 4, n] = r1[n % 2, x, y : y + 1, :]
     each(lambda k: start(level1_sends(r1, r1r, k, 2, 1)))
     to_fellows(sm2, gm.at[odd, me], 0)
     for side, (x_far, x_near) in enumerate(((H0 + 1, H0), (H0 + bx - 2, H0 + bx - 1))):
@@ -497,42 +522,52 @@
     for k in range(4, 8):
         for n, (i, j) in enumerate(near_m1):
             x, y = outside1(k, i, j)
-            m1[0, x, y : y + 1, :] = cr1[0, k - 4, n : n + 1, :]
+            m1[0, x, y : y + 1, :] = cr1[k - 4, n : n + 1, :]
     ops1 = (cx1, cy1, cz1, rd1, d1)
     build(m1.at[0], cx1, cy1, cz1, rd1, d1, H1 - 3, b1x + 6, BASE_TAU / 4, z1, b1x + 6)
-    each(level1_landed(r1, r1r, 2, 1))
-    for k in range(4, 8):
-        for n in range(6):
-            x, y = outside1(k, 1, 1 + n // 2)
-            r1[n % 2, x, y : y + 1, :] = cr1[1, k - 4, n : n + 1, :]
     rr1 = (r1.at[0], r1.at[1])
     uu1 = (u1.at[0], u1.at[1])
     vv1 = (v1.at[0], v1.at[1])
+    halves1 = {}
 
     def first1(a):
         for v in range(2):
             u1[v, a] = rd1[a] * r1[v, a]
 
-    slabs(H1 - 2, b1x + 4, b1x + 4, first1)
-    sweep(uu1, vv1, rr1, ops1, H1 - 1, b1x + 2, b1x + 2)
-    num1, den1 = zero8, zero8
-    quads = []
-    for i in range(b2x):
+    def down1(i, carry):
+        num, den = carry
         pair = []
         for k in range(2):
             a = H1 + 2 * i + k
             vs, es = residual(vv1[0], rr1[0], a, ops1)
             vc, ec = residual(vv1[1], rr1[1], a, ops1)
             both = (es + r1[0, a])[own_y]
-            num1 = num1 + both * vc[own_y]
-            den1 = den1 + both * vs[own_y]
+            num = num + both * vc[own_y]
+            den = den + both * vs[own_y]
             pair.append((es[own_y], ec[own_y]))
-        quads.append([y_pairs(pair[0][v] + pair[1][v]) for v in range(2)])
-        if i % 2:
-            packed = [z_pairs(top_bottom(quads[i - 1][v], quads[i][v])) for v in range(2)]
-            own2 = 0.125 * jnp.where(iota(TILE, 1) < z2, packed[0], packed[1])
-            sr2[(i - 1) * b2y : (i + 1) * b2y, :] = own2
-            gr[odd, me, (i - 1) * b2y : (i + 1) * b2y, :] = own2
+        halves1[i] = [y_pairs(pair[0][v] + pair[1][v]) for v in range(2)]
+        return num, den
+
+    landed1 = level1_landed(r1, r1r, 2, 1)
+    each(landed1, (2, 3))
+    slabs(H1, b1x, b1x, first1)
+    sweep(uu1, vv1, rr1, ops1, H1 + 1, b1x - 2, b1x - 2)
+    sums1 = loop(b2x - 2, b2x - 2, lambda i, c: down1(1 + i, c), (zero8, zero8))
+    each(landed1, (0, 1, 4, 5, 6, 7))
+    for k in range(4, 8):
+        for n in range(6):
+            x, y = outside1(k, 1, 1 + n // 2)
+            r1[n % 2, x, y : y + 1, :] = cr2[k - 4, n]
+    for a in (H1 - 2, H1 + b1x):
+        slabs(a, 2, 2, first1)
+    for a in (H1 - 1, H1 + b1x - 1):
+        sweep(uu1, vv1, rr1, ops1, a, 2, 2)
+    num1, den1 = down1(b2x - 1, down1(0, sums1))
+    for i in range(0, b2x, 2):
+        packed = [z_pairs(top_bottom(halves1[i][v], halves1[i + 1][v])) for v in range(2)]
+        own2 = 0.125 * jnp.where(iota(TILE, 1) < z2, packed[0], packed[1])
+        sr2[i * b2y : (i + 2) * b2y, :] = own2
+        gr[odd, me, i * b2y : (i + 2) * b2y, :] = own2
     to_fellows(sr2, gr.at[odd, me], 2)
     num_row = jnp.sum(num0 + 8.0 * num1, axis=0, keepdims=True)
     den_row = jnp.sum(den0 + 8.0 * den1, axis=0, keepdims=True)
@@ -566,6 +601,7 @@
         return to_side(side, [(v1.at[:, lo : lo + 3, own_y], h1.at[land]), (cv1.at[side], hc.at[land])], v1r)
 
     each(lambda k: start(v1_sends(k)), range(2))
+    each(lambda k: start(v0_sends(k)), range(4))
 
     def unpack(src, dst, u=None):
         def step(w, carry):
@@ -611,13 +647,21 @@
     landed(gr.at[0, 0 : nb - 1], 2)
     to_twin(gr.at[odd], gr.at[odd], 3)
 
-    each(lambda k: start(v0_sends(k)), range(4))
 
     def v0_landed(side):
         view = hx.at[side] if side < 2 else hy.at[side - 2]
         pltpu.make_async_copy(view, view, v0r.at[side]).wait()
 
     landed(gr.at[0], 3)
+    landed(gp.at[0 : nb - 1], 4)
+    total = gp[0]
+    if nb <= 32:
+        for w in range(1, nb):
+            total = total + gp[w]
+    else:
+        total = lax.fori_loop(1, nb, lambda w, acc: acc + gp[w], total)
+    pb[...] = total
+    to_twin(pb, pbs, 5)
     unpack(gr, r2, u2)
 
     ops2 = (cx2, cy2, cz2, rd2, kept2)
@@ -645,15 +689,6 @@
         return sums
 
     sweep((u2,), (v2,), (r2,), ops2, PAD2, x2, 32)
-    landed(gp.at[0 : nb - 1], 4)
-    total = gp[0]
-    if nb <= 32:
-        for w in range(1, nb):
-            total = total + gp[w]
-    else:
-        total = lax.fori_loop(1, nb, lambda w, acc: acc + gp[w], total)
-    pb[...] = total
-    to_twin(pb, pbs, 5)
     num2, den2 = coarsen_residual(v2, r2, ops2, r3, x3, PAD2, z2)
     def first3(a):
         u3[a] = rd3[a] * r3[a]
@@ -779,7 +814,7 @@
         elif dx == 0:
             tiles = 7 * bx * nz // 1024 + b1x + 2 * b1x + 2 * bx * nz // 1024
         else:
-            tiles = 2 + 1 + 1
+            tiles = 3
         view = tok.at[0:tiles]
         pltpu.make_async_copy(view, view, ss.at[side]).wait()
 
@@ -804,9 +839,9 @@
         own2 = (bx // 4 * (by // 4), z1)
         buffers = (
             [own] * 3 + [l0] * 12
-            + [(2, 4, by, nz), (2, 7, bx, nz), (2, 7, bx, nz), (4, 8, nz), (4, 8, nz)]
+            + [(2, 4, by, nz), (2, 7, bx, nz), (2, 7, bx, nz), (4, 5, 1, nz), (4, 5, 1, nz)]
             + [(2, 2, by + 8, nz)] * 2 + [(2, 2, bx, nz)] * 2 + [(2, 2, by, nz)] * 2
-            + [(1, *l1)] + [l1] * 5 + [(2, *l1)] * 3 + [l1] + [(2, 2, 3, b1y, z1), (2, 2, 2, b1y, z1), (2, 2, 2, b1y, z1), (2, 4, *TILE), (2, 4, *TILE)]
+            + [(1, *l1)] + [l1] * 5 + [(2, *l1)] * 3 + [l1] + [(2, 2, 3, b1y, z1), (2, 2, 2, b1y, z1), (2, 2, 2, b1y, z1), (4, *TILE), (4, *TILE), (4, 6, 1, z1), (4, 6, 1, z1)]
             + [l2] * 7 + [l2 if nw <= 16 else (1, *TILE)] + [l3] * 8 + [l4] * 7
             + [(2, 2, b1x * l0[1], nz // 2)]
             + [own2, own2, (1, 128), (2, nn // 2 * nw, *own2), (2, nn // 2 * nw, *own2), (nn // 2 * nw, 1, 128), (1, 128), (1, 128)]
@@ -815,7 +850,7 @@
         size = sum(4 * functools.reduce(lambda p, q: p * q, shape) for shape in buffers)
         dma = lambda n: pltpu.SemaphoreType.DMA((n,))
         scratch = [pltpu.VMEM(shape, F32) for shape in buffers]
-        scratch += [dma(n) for n in (1, 8, 3, 6, 8, 8, 8, 4, 2, 2)]
+        scratch += [dma(n) for n in (1, 8, 3, 6, 6, 4, 8, 8, 4, 2, 2)]
         return pl.pallas_call(
             functools.partial(kernel, nw, nn, bx, by, nz),
             out_shape=jax.ShapeDtypeStruct((bx, by, nz), F32),

time: 28.8 us -> 28 us (0.972)
  the two profiles are of different devices: /device:TPU:0 before, /device:TPU:1 now
where the time goes in v5:
time: 28 us; the launch traced here: 27.7 us
  Pallas kernels  27 us (96%)
  local copies, waits for them, and re-layouts  0.71 us (3%)
    pallas_call x1, Pallas kernels, per_device(): pl.pallas_call(functools.partial(kernel, nw, nn, bx, by, nz), out_shape=j...  27 us
    unnamed x1, local copies, waits for them, and re-layouts  0.71 us

profile of v5, /device:TPU:1, one launch (start us, length us, event | category | flops | bytes accessed | tf_op | source)
XLA Modules:
  0.0 27.7 jit_solution(6926213037340944517)
XLA Ops:
  0.0 27.0 %shard_map.37 = f32[16,16,256]{2,1,0:T(8,128)S(1)} custom-call(f32[16,16,256]{2,1,0:T(8,128)} %m_hbm.1, f32[16,16,256]{2,1,0:T(8,128)} %s_hbm.1, f32[16,16,256]{2,1,0:T(8,128)} %c_hbm.1), custom_call_target="tpu_custom_call" | custom-call | tf_op jit(solution)/shard_map/pallas_call | solution.py:854
  27.0 0.7 %copy.5 = f32[16,16,256]{2,1,0:T(8,128)} copy(f32[16,16,256]{2,1,0:T(8,128)S(1)} %shard_map.37) | data formatting | bytes 524288

commit v6 on v5

--- a/solution.py
+++ b/solution.py
@@ -177,12 +177,12 @@
            m_ref, s_ref, c_ref,
            m0, cx0, cy0, cz0, rd0, d0, rs0, rc0, us0, uc0, vs0, vc0,
            rx, yp, ry, cp, rcn, xv, hx, yv, hy, xu, hu,
-           m1, cx1, cy1, cz1, rd1, d1, r1, u1, v1, w1, h1, hc, cv1, cs1, cr1, cs2, cr2,
+           m1, cx1, cy1, cz1, rd1, d1, r1, u1, v1, w1, h1, hc, cv1, cs1, cr1, cs2, cr2, qs1, qr1,
            cx2, cy2, cz2, rd2, r2, u2, v2, d2,
            cx3, cy3, cz3, rd3, r3, u3, v3, d3,
            cx4, cy4, cz4, rd4, r4, u4, v4,
            t0, sm2, sr2, sp2, gm, gr, gp, pb, pbs, f1p, tok,
-           ins, ss, gs, gq, e0r, y0r, m1r, r1r, v0r, v1r, u0r):
+           ins, ss, gs, gq, e0r, y0r, m1r, r1r, v0r, v1r, u0r, mr):
     iw, ino = lax.axis_index("wide"), lax.axis_index("narrow")
     b1x, b1y, z1 = bx // 2, by // 2, nz // 2
     b2x, b2y, z2 = bx // 4, by // 4, nz // 4
@@ -229,17 +229,31 @@
 
             lax.fori_loop(1, nb, step, 0)
 
-    over_fellows(lambda j: pl.semaphore_signal(barrier, inc=1, device_id=fellow(j), device_id_type=MESH))
-    for j in range(1, nn, 2):
-        pl.semaphore_signal(barrier, inc=1, device_id=(iw, lax.rem(ino + j, nn)), device_id_type=MESH)
-    for k in range(4, 8):
+    rounds = []
+    while 1 << len(rounds) < nb:
+        rounds.append(1 << len(rounds))
+
+    def partner(d):
+        to = me + d - 2 * d * lax.rem(me // d, 2)
+        row = to // nw
+        return to - row * nw, 2 * row + odd
+
+    for d in rounds[1:]:
+        pl.semaphore_signal(barrier, inc=1, device_id=partner(d), device_id_type=MESH)
+    for k in range(8):
         @pl.when(there[k])
         def _():
             pl.semaphore_signal(barrier, inc=1, device_id=peer(k), device_id_type=MESH)
 
+    def meet(n):
+        if n > 0:
+            pl.semaphore_wait(mr.at[n - 1], 1)
+        if n < len(rounds):
+            pl.semaphore_signal(mr.at[n], inc=1, device_id=partner(rounds[n]), device_id_type=MESH)
+
     beside_x = jnp.minimum(iw, 1) + jnp.minimum(nw - 1 - iw, 1)
     beside_y = jnp.minimum(ino, 1) + jnp.minimum(nn - 1 - ino, 1)
-    pl.semaphore_wait(barrier, nb - 1 + nn // 2 + beside_x * beside_y)
+    pl.semaphore_wait(barrier, len(rounds) - 1 + beside_x + beside_y + beside_x * beside_y)
 
     def remote(src, dst, ssem, rsem, dev):
         return pltpu.make_async_remote_copy(src_ref=src, dst_ref=dst, send_sem=ssem, recv_sem=rsem,
@@ -278,6 +292,7 @@
             copy.start()
 
     each(lambda k: start(e0_sends(k)), (0, 1))
+    meet(0)
     view = tok.at[0 : 3 * bx * by * nz // 1024]
     pltpu.make_async_copy(view, view, ins.at[0]).wait()
     def yp_fill(side, at, ref, k):
@@ -326,14 +341,31 @@
         if side > 3:
             src, dst = (cs2, cr2) if kc else (cs1, cr1)
             return to_side(side, [(src.at[side - 4], dst.at[OPPOSITE[side] - 4])], rsem)
+        if kc and side > 1:
+            return to_side(side, [(qs1.at[side - 2], qr1.at[OPPOSITE[side] - 2])], rsem)
         sx, w, sy = box1(side, True, width)
         tx, _, ty = box1(OPPOSITE[side], False, width)
         return to_side(side, [(ref.at[:, sx : sx + w, sy : sy + b1y], ref.at[:, tx : tx + w, ty : ty + b1y])], rsem)
+
+    def r1_pack(side):
+        for x in range(b1x):
+            rs, rc = r1[0, H1 + x, own_y, :], r1[1, H1 + x, own_y, :]
+            qs1[side - 2, x] = top_bottom(rs, shift(rc, 4, 0)) if side == 2 else top_bottom(shift(rs, 4, 0), rc)
+
+    def r1_unpack(side):
+        rows = side_rows[side - 2]
+        for x in range(b1x):
+            tile = qr1[side - 2, x]
+            other = shift(tile, 4, 0)
+            r1[0, H1 + x, rows, :] = other if side == 2 else tile
+            r1[1, H1 + x, rows, :] = tile if side == 2 else other
 
     def level1_landed(ref, rsem, width, kc):
         def fn(side):
             if side > 3:
                 view = (cr2 if kc else cr1).at[side - 4]
+            elif kc and side > 1:
+                view = qr1.at[side - 2]
             else:
                 tx, w, ty = box1(side, False, width)
                 view = ref.at[:, tx : tx + w, ty : ty + b1y]
@@ -361,17 +393,21 @@
         for n, (i, j) in enumerate(near_m1):
             x, y = inside1(k, i, j)
             cs1[k - 4, n : n + 1, :] = m1[0, x, y : y + 1, :]
-    for i in range(0, b2x, 2):
-        quads = [y_pairs(m1[0, H1 + 2 * k, own_y, :] + m1[0, H1 + 2 * k + 1, own_y, :]) for k in (i, i + 1)]
-        mob2 = 0.125 * z_pairs(top_bottom(quads[0], quads[1]))
-        sm2[i * b2y : (i + 2) * b2y, :] = mob2
-        gm[odd, me, i * b2y : (i + 2) * b2y, :] = mob2
+    low2 = iota(TILE, 1) < z2
+    for i in range(0, b2x, 4):
+        tiles = []
+        for n in range(i, i + 4, 2):
+            quads = [y_pairs(m1[0, H1 + 2 * k, own_y, :] + m1[0, H1 + 2 * k + 1, own_y, :]) for k in (n, n + 1)]
+            tiles.append(0.125 * z_pairs(top_bottom(quads[0], quads[1])))
+        mob2 = jnp.where(low2, tiles[0], tiles[1])
+        sm2[2 * i : 2 * i + 8, :] = mob2
+        gm[odd, me, 2 * i : 2 * i + 8, :] = mob2
 
     def to_fellows(src, dst, kind):
-        over_fellows(lambda j: remote(src, dst, gs.at[2 if kind > 3 else kind % 2], gq.at[kind], fellow(j)).start())
+        over_fellows(lambda j: remote(src, dst, gs.at[kind if kind < 4 else 4], gq.at[kind], fellow(j)).start())
 
     def to_twin(src, dst, kind):
-        remote(src, dst, gs.at[2 if kind > 3 else kind % 2], gq.at[kind], (iw, twin)).start()
+        remote(src, dst, gs.at[kind if kind < 4 else 4], gq.at[kind], (iw, twin)).start()
 
     def landed(view, kind):
         pltpu.make_async_copy(view, view, gq.at[kind]).wait()
@@ -395,10 +431,10 @@
                 clear(cr1, k - 4)
                 clear(cr2, k - 4)
                 return
-            lands = ((rx, hx, hu, h1, hc) if k < 2 else (ry, hy))
+            lands = ((rx, hx, hu, h1, hc) if k < 2 else (ry, hy, qr1))
             for ref in lands:
                 clear(ref, k % 2)
-            for ref, width in ((m1, 3), (r1, 2)):
+            for ref, width in (((m1, 3), (r1, 2)) if k < 2 else ((m1, 3),)):
                 xlo, w, ylo = box1(k, False, width)
                 clear(ref, (slice(None), slice(xlo, xlo + w), slice(ylo, ylo + b1y)))
     for a in (0, H1 + b1x + 3):
@@ -427,6 +463,7 @@
 
     ops0 = (cx0, cy0, cz0, rd0, d0)
     firsts0 = ((rs0, us0), (rc0, uc0))
+    meet(1)
     each(near_landed, (2, 3))
     m0[H0 : H0 + bx, H0 - 1, :] = ry[0, 0]
     m0[H0 : H0 + bx, H0 + by, :] = ry[1, 0]
@@ -442,6 +479,7 @@
             ref[H0 : H0 + bx, H0 - 1 - lo - i, :] = ry[0, at + i]
             ref[H0 : H0 + bx, H0 + by + lo + i, :] = ry[1, at + i]
 
+    meet(2)
     build(m0, cx0, cy0, cz0, rd0, d0, H0 + 1, bx - 2, BASE_TAU, nz, bx - 2, firsts0)
     sweep((us0, uc0), (vs0, vc0), (rs0, rc0), ops0, H0 + 2, bx - 4, bx - 4)
 
@@ -470,6 +508,7 @@
             r1[v, H1 + i, own_y, :] = 0.125 * yz_pairs(t0, v, i * m0.shape[1] + H0)
 
     slabs(2, b1x - 4, b1x - 4, coarse0)
+    meet(3)
     def u0_landed(side):
         pltpu.make_async_copy(hu.at[side], hu.at[side], u0r.at[side]).wait()
 
@@ -502,8 +541,9 @@
         for n in range(6):
             x, y = inside1(k, 1, 1 + n // 2)
             cs2[k - 4, n] = r1[n % 2, x, y : y + 1, :]
+    for k in (2, 3):
+        r1_pack(k)
     each(lambda k: start(level1_sends(r1, r1r, k, 2, 1)))
-    to_fellows(sm2, gm.at[odd, me], 0)
     for side, (x_far, x_near) in enumerate(((H0 + 1, H0), (H0 + bx - 2, H0 + bx - 1))):
         for v, ref in enumerate((vs0, vc0)):
             xv[side, v, 0:by, :] = ref[x_far, H0 : H0 + by, :]
@@ -525,6 +565,9 @@
             m1[0, x, y : y + 1, :] = cr1[k - 4, n : n + 1, :]
     ops1 = (cx1, cy1, cz1, rd1, d1)
     build(m1.at[0], cx1, cy1, cz1, rd1, d1, H1 - 3, b1x + 6, BASE_TAU / 4, z1, b1x + 6)
+    for n in range(4, len(rounds) + 1):
+        meet(n)
+    to_fellows(sm2, gm.at[odd, me], 0)
     rr1 = (r1.at[0], r1.at[1])
     uu1 = (u1.at[0], u1.at[1])
     vv1 = (v1.at[0], v1.at[1])
@@ -550,6 +593,8 @@
 
     landed1 = level1_landed(r1, r1r, 2, 1)
     each(landed1, (2, 3))
+    for k in (2, 3):
+        r1_unpack(k)
     slabs(H1, b1x, b1x, first1)
     sweep(uu1, vv1, rr1, ops1, H1 + 1, b1x - 2, b1x - 2)
     sums1 = loop(b2x - 2, b2x - 2, lambda i, c: down1(1 + i, c), (zero8, zero8))
@@ -565,7 +610,7 @@
     num1, den1 = down1(b2x - 1, down1(0, sums1))
     for i in range(0, b2x, 2):
         packed = [z_pairs(top_bottom(halves1[i][v], halves1[i + 1][v])) for v in range(2)]
-        own2 = 0.125 * jnp.where(iota(TILE, 1) < z2, packed[0], packed[1])
+        own2 = 0.125 * jnp.where(low2, packed[0], packed[1])
         sr2[i * b2y : (i + 2) * b2y, :] = own2
         gr[odd, me, i * b2y : (i + 2) * b2y, :] = own2
     to_fellows(sr2, gr.at[odd, me], 2)
@@ -600,8 +645,6 @@
         lo = H1 if side == 0 else H1 + b1x - 3
         return to_side(side, [(v1.at[:, lo : lo + 3, own_y], h1.at[land]), (cv1.at[side], hc.at[land])], v1r)
 
-    each(lambda k: start(v1_sends(k)), range(2))
-    each(lambda k: start(v0_sends(k)), range(4))
 
     def unpack(src, dst, u=None):
         def step(w, carry):
@@ -615,7 +658,18 @@
 
         loop(nw, 8, step, 0)
 
-    unpack(gm, v2)
+    def unpack_m(w, carry):
+        for n in range(nn):
+            for i in range(0, b2x, 4):
+                tile = gm[n % 2, n // 2 * nw + w, 2 * i : 2 * i + 8, :]
+                other = shift(tile, z2, 1)
+                for k, part in enumerate((jnp.where(low2, tile, other), jnp.where(low2, other, tile))):
+                    for h in range(2):
+                        a = PAD2 + w * b2x + i + 2 * k + h
+                        v2[a, n * b2y : (n + 1) * b2y, :] = part[h * b2y : (h + 1) * b2y, :]
+        return carry
+
+    loop(nw, 8, unpack_m, 0)
     kept2 = d2 if d2.shape == v2.shape else None
     build(v2, cx2, cy2, cz2, rd2, kept2, PAD2, x2, BASE_TAU / 16, z2, 16)
 
@@ -644,6 +698,8 @@
     coarsen_pairs(v3, v4, x4, PAD)
     build(v4, cx4, cy4, cz4, rd4, None, PAD, x4, BASE_TAU / 256, z2 // 4, 8)
 
+    each(lambda k: start(v1_sends(k)), range(2))
+    each(lambda k: start(v0_sends(k)), range(4))
     landed(gr.at[0, 0 : nb - 1], 2)
     to_twin(gr.at[odd], gr.at[odd], 3)
 
@@ -812,14 +868,14 @@
         if dy == 0:
             tiles = 6 * by * nz // 1024 + 3 + 4 + 2 * (by + 8) * nz // 1024 + 10
         elif dx == 0:
-            tiles = 7 * bx * nz // 1024 + b1x + 2 * b1x + 2 * bx * nz // 1024
+            tiles = 7 * bx * nz // 1024 + b1x + b1x + 2 * bx * nz // 1024
         else:
             tiles = 3
         view = tok.at[0:tiles]
         pltpu.make_async_copy(view, view, ss.at[side]).wait()
 
     each(sent)
-    for i, view in enumerate((gr.at[:, 0 : nb - 1], gr, gp)):
+    for i, view in enumerate((gm.at[0, 0 : nb - 1], gm.at[0], gr.at[0, 0 : nb - 1], gr.at[0], gp)):
         pltpu.make_async_copy(view, view, gs.at[i]).wait()
 
 
@@ -837,20 +893,23 @@
         l3 = (x2 // 2 + 2 * PAD2, y2 // 2, z1)
         l4 = (x2 // 4 + 2 * PAD, 8, z1)
         own2 = (bx // 4 * (by // 4), z1)
+        half2 = (bx // 4 * (by // 4) // 2, z1)
         buffers = (
             [own] * 3 + [l0] * 12
             + [(2, 4, by, nz), (2, 7, bx, nz), (2, 7, bx, nz), (4, 5, 1, nz), (4, 5, 1, nz)]
             + [(2, 2, by + 8, nz)] * 2 + [(2, 2, bx, nz)] * 2 + [(2, 2, by, nz)] * 2
-            + [(1, *l1)] + [l1] * 5 + [(2, *l1)] * 3 + [l1] + [(2, 2, 3, b1y, z1), (2, 2, 2, b1y, z1), (2, 2, 2, b1y, z1), (4, *TILE), (4, *TILE), (4, 6, 1, z1), (4, 6, 1, z1)]
+            + [(1, *l1)] + [l1] * 5 + [(2, *l1)] * 3 + [l1] + [(2, 2, 3, b1y, z1), (2, 2, 2, b1y, z1), (2, 2, 2, b1y, z1), (4, *TILE), (4, *TILE), (4, 6, 1, z1), (4, 6, 1, z1), (2, b1x, *TILE), (2, b1x, *TILE)]
             + [l2] * 7 + [l2 if nw <= 16 else (1, *TILE)] + [l3] * 8 + [l4] * 7
             + [(2, 2, b1x * l0[1], nz // 2)]
-            + [own2, own2, (1, 128), (2, nn // 2 * nw, *own2), (2, nn // 2 * nw, *own2), (nn // 2 * nw, 1, 128), (1, 128), (1, 128)]
+            + [half2, own2, (1, 128), (2, nn // 2 * nw, *half2), (2, nn // 2 * nw, *own2), (nn // 2 * nw, 1, 128), (1, 128), (1, 128)]
             + [(bx // 4 + 4, 2 * y2 + 2 * b1y, z1), (3 * bx * by * nz // 1024, *TILE)]
         )
         size = sum(4 * functools.reduce(lambda p, q: p * q, shape) for shape in buffers)
         dma = lambda n: pltpu.SemaphoreType.DMA((n,))
         scratch = [pltpu.VMEM(shape, F32) for shape in buffers]
-        scratch += [dma(n) for n in (1, 8, 3, 6, 6, 4, 8, 8, 4, 2, 2)]
+        scratch += [dma(n) for n in (1, 8, 5, 6, 6, 4, 8, 8, 4, 2, 2)]
+        steps = (nn // 2 * nw - 1).bit_length()
+        scratch.append(pltpu.SemaphoreType.REGULAR((steps,)))
         return pl.pallas_call(
             functools.partial(kernel, nw, nn, bx, by, nz),
             out_shape=jax.ShapeDtypeStruct((bx, by, nz), F32),

time: 28 us -> 27.6 us (0.986)
  no operation moved by 1% of the time
where the time goes in v6:
time: 27.6 us; the launch traced here: 27.5 us
  Pallas kernels  26.8 us (97%)
  local copies, waits for them, and re-layouts  0.71 us (3%)
    pallas_call x1, Pallas kernels, per_device(): pl.pallas_call(functools.partial(kernel, nw, nn, bx, by, nz), out_shape=j...  26.8 us
    unnamed x1, local copies, waits for them, and re-layouts  0.71 us

profile of v6, /device:TPU:1, one launch (start us, length us, event | category | flops | bytes accessed | tf_op | source)
XLA Modules:
  0.0 27.5 jit_solution(14562601649207287701)
XLA Ops:
  0.0 26.8 %shard_map.37 = f32[16,16,256]{2,1,0:T(8,128)S(1)} custom-call(f32[16,16,256]{2,1,0:T(8,128)} %m_hbm.1, f32[16,16,256]{2,1,0:T(8,128)} %s_hbm.1, f32[16,16,256]{2,1,0:T(8,128)} %c_hbm.1), custom_call_target="tpu_custom_call" | custom-call | tf_op jit(solution)/shard_map/pallas_call | solution.py:913
  26.8 0.7 %copy.5 = f32[16,16,256]{2,1,0:T(8,128)} copy(f32[16,16,256]{2,1,0:T(8,128)S(1)} %shard_map.37) | data formatting | bytes 524288

commit v7 on v6

--- a/solution.py
+++ b/solution.py
@@ -181,8 +181,8 @@
            cx2, cy2, cz2, rd2, r2, u2, v2, d2,
            cx3, cy3, cz3, rd3, r3, u3, v3, d3,
            cx4, cy4, cz4, rd4, r4, u4, v4,
-           t0, sm2, sr2, sp2, gm, gr, gp, pb, pbs, f1p, tok,
-           ins, ss, gs, gq, e0r, y0r, m1r, r1r, v0r, v1r, u0r, mr):
+           t0, sm2, sr2, sp2, gm, gr, gp, f1p, tok,
+           ins, ss, gs, gq, e0r, y0r, m1r, r1r, u0r, mr):
     iw, ino = lax.axis_index("wide"), lax.axis_index("narrow")
     b1x, b1y, z1 = bx // 2, by // 2, nz // 2
     b2x, b2y, z2 = bx // 4, by // 4, nz // 4
@@ -248,8 +248,9 @@
     def meet(n):
         if n > 0:
             pl.semaphore_wait(mr.at[n - 1], 1)
-        if n < len(rounds):
-            pl.semaphore_signal(mr.at[n], inc=1, device_id=partner(rounds[n]), device_id_type=MESH)
+        if n <= len(rounds):
+            to = partner(rounds[n]) if n < len(rounds) else (iw, twin)
+            pl.semaphore_signal(mr.at[n], inc=1, device_id=to, device_id_type=MESH)
 
     beside_x = jnp.minimum(iw, 1) + jnp.minimum(nw - 1 - iw, 1)
     beside_y = jnp.minimum(ino, 1) + jnp.minimum(nn - 1 - ino, 1)
@@ -403,11 +404,31 @@
         sm2[2 * i : 2 * i + 8, :] = mob2
         gm[odd, me, 2 * i : 2 * i + 8, :] = mob2
 
+    def send_sem(kind):
+        return gs.at[gs.shape[0] - 1 if kind > 3 else min(kind, gs.shape[0] - 2)]
+
     def to_fellows(src, dst, kind):
-        over_fellows(lambda j: remote(src, dst, gs.at[kind if kind < 4 else 4], gq.at[kind], fellow(j)).start())
+        over_fellows(lambda j: remote(src, dst, send_sem(kind), gq.at[kind], fellow(j)).start())
 
     def to_twin(src, dst, kind):
-        remote(src, dst, gs.at[kind if kind < 4 else 4], gq.at[kind], (iw, twin)).start()
+        remote(src, dst, send_sem(kind), gq.at[kind], (iw, twin)).start()
+
+    def to_others(src, dst, kind):
+        def to_one(j):
+            to = me + j
+            to = jnp.where(to >= nb, to - nb, to)
+            row = to // nw
+            remote(src, dst, send_sem(kind), gq.at[kind], (to - row * nw, 2 * row + 1 - odd)).start()
+
+        if nb <= 16:
+            for j in range(nb):
+                to_one(j)
+        else:
+            def step(j, _):
+                to_one(j)
+                return 0
+
+            lax.fori_loop(0, nb, step, 0)
 
     def landed(view, kind):
         pltpu.make_async_copy(view, view, gq.at[kind]).wait()
@@ -513,6 +534,9 @@
         pltpu.make_async_copy(hu.at[side], hu.at[side], u0r.at[side]).wait()
 
     each(e0_landed, (0, 1, 4, 5, 6, 7))
+    for n in range(4, len(rounds) + 1):
+        meet(n)
+    to_fellows(sm2, gm.at[odd, me], 0)
     for ref, at, width in ((m0, 0, 2), (rs0, 2, 1), (rc0, 3, 1)):
         for i in range(width):
             ref[H0 - width + i, H0 : H0 + by, :] = rx[0, at + i]
@@ -543,7 +567,7 @@
             cs2[k - 4, n] = r1[n % 2, x, y : y + 1, :]
     for k in (2, 3):
         r1_pack(k)
-    each(lambda k: start(level1_sends(r1, r1r, k, 2, 1)))
+    each(lambda k: start(level1_sends(r1, r1r, k, 2, 1)), (4, 5, 6, 7, 0, 1, 2, 3))
     for side, (x_far, x_near) in enumerate(((H0 + 1, H0), (H0 + bx - 2, H0 + bx - 1))):
         for v, ref in enumerate((vs0, vc0)):
             xv[side, v, 0:by, :] = ref[x_far, H0 : H0 + by, :]
@@ -556,7 +580,9 @@
     def v0_sends(side):
         land = OPPOSITE[side]
         src, dst = (xv.at[side], hx.at[land]) if side < 2 else (yv.at[side - 2], hy.at[land - 2])
-        return to_side(side, [(src, dst)], v0r)
+        if side < 2:
+            return to_side(side, [(src, dst)], e0r)
+        return [remote(src, dst, ss.at[side], y0r.at[land], peer(side))]
 
     each(level1_landed(m1, m1r, 3, 0))
     for k in range(4, 8):
@@ -565,9 +591,6 @@
             m1[0, x, y : y + 1, :] = cr1[k - 4, n : n + 1, :]
     ops1 = (cx1, cy1, cz1, rd1, d1)
     build(m1.at[0], cx1, cy1, cz1, rd1, d1, H1 - 3, b1x + 6, BASE_TAU / 4, z1, b1x + 6)
-    for n in range(4, len(rounds) + 1):
-        meet(n)
-    to_fellows(sm2, gm.at[odd, me], 0)
     rr1 = (r1.at[0], r1.at[1])
     uu1 = (u1.at[0], u1.at[1])
     vv1 = (v1.at[0], v1.at[1])
@@ -613,14 +636,17 @@
         own2 = 0.125 * jnp.where(low2, packed[0], packed[1])
         sr2[i * b2y : (i + 2) * b2y, :] = own2
         gr[odd, me, i * b2y : (i + 2) * b2y, :] = own2
+    meet(len(rounds) + 1)
     to_fellows(sr2, gr.at[odd, me], 2)
     num_row = jnp.sum(num0 + 8.0 * num1, axis=0, keepdims=True)
     den_row = jnp.sum(den0 + 8.0 * den1, axis=0, keepdims=True)
     low1 = iota((1, 128), 1) < 64
     part = jnp.where(low1, num_row + shift(num_row, 64, 1), den_row + shift(den_row, 64, 1))
     sp2[...] = part
-    gp[me] = part
-    to_fellows(sp2, gp.at[me], 4)
+    mine = odd * nb + me
+    gp[mine] = part
+    to_fellows(sp2, gp.at[mine], 4)
+    to_others(sp2, gp.at[mine], 4)
 
     def v1_corners(side, ref_v, ref_r, tiles, outward):
         for d in range(2):
@@ -643,7 +669,7 @@
     def v1_sends(side):
         land = OPPOSITE[side]
         lo = H1 if side == 0 else H1 + b1x - 3
-        return to_side(side, [(v1.at[:, lo : lo + 3, own_y], h1.at[land]), (cv1.at[side], hc.at[land])], v1r)
+        return to_side(side, [(v1.at[:, lo : lo + 3, own_y], h1.at[land]), (cv1.at[side], hc.at[land])], u0r)
 
 
     def unpack(src, dst, u=None):
@@ -706,18 +732,9 @@
 
     def v0_landed(side):
         view = hx.at[side] if side < 2 else hy.at[side - 2]
-        pltpu.make_async_copy(view, view, v0r.at[side]).wait()
+        pltpu.make_async_copy(view, view, e0r.at[side] if side < 2 else y0r.at[side]).wait()
 
     landed(gr.at[0], 3)
-    landed(gp.at[0 : nb - 1], 4)
-    total = gp[0]
-    if nb <= 32:
-        for w in range(1, nb):
-            total = total + gp[w]
-    else:
-        total = lax.fori_loop(1, nb, lambda w, acc: acc + gp[w], total)
-    pb[...] = total
-    to_twin(pb, pbs, 5)
     unpack(gr, r2, u2)
 
     ops2 = (cx2, cy2, cz2, rd2, kept2)
@@ -745,6 +762,8 @@
         return sums
 
     sweep((u2,), (v2,), (r2,), ops2, PAD2, x2, 32)
+    landed(gp.at[0 : 2 * nb - 1], 4)
+    whole = loop(2 * nb, 32, lambda i, acc: acc + gp[i], jnp.zeros((1, 128), F32))
     num2, den2 = coarsen_residual(v2, r2, ops2, r3, x3, PAD2, z2)
     def first3(a):
         u3[a] = rd3[a] * r3[a]
@@ -779,8 +798,6 @@
             v3[a] = v3[a] + add
     sweep((v3,), (u3,), (r3,), ops3, base3 - 3, b3x + 6, b3x + 6)
     sweep((u3,), (v3,), (r3,), ops3, base3 - 2, b3x + 4, b3x + 4)
-    landed(pbs, 5)
-    whole = total + pbs[...]
 
     def total_of(mask, n2, n3, n4):
         x = jnp.sum(64.0 * n2 + 512.0 * n3 + 4096.0 * n4, axis=0, keepdims=True)
@@ -800,7 +817,7 @@
 
     def v1_landed(side):
         view = tok.at[0 : 10]
-        pltpu.make_async_copy(view, view, v1r.at[side]).wait()
+        pltpu.make_async_copy(view, view, u0r.at[side]).wait()
 
     each(v1_landed, range(2))
     for side, a in enumerate((H1 - 3, H1 + b1x)):
@@ -875,7 +892,12 @@
         pltpu.make_async_copy(view, view, ss.at[side]).wait()
 
     each(sent)
-    for i, view in enumerate((gm.at[0, 0 : nb - 1], gm.at[0], gr.at[0, 0 : nb - 1], gr.at[0], gp)):
+    if gs.shape[0] == 2:
+        views = (tok.at[0 : 3 * (nb - 1) + 3 * nb],)
+    else:
+        views = (gm.at[0, 0 : nb - 1], gm.at[0], gr.at[0, 0 : nb - 1], gr.at[0])
+    views += (gp.at[0 : 2 * nb - 1],)
+    for i, view in enumerate(views):
         pltpu.make_async_copy(view, view, gs.at[i]).wait()
 
 
@@ -901,14 +923,14 @@
             + [(1, *l1)] + [l1] * 5 + [(2, *l1)] * 3 + [l1] + [(2, 2, 3, b1y, z1), (2, 2, 2, b1y, z1), (2, 2, 2, b1y, z1), (4, *TILE), (4, *TILE), (4, 6, 1, z1), (4, 6, 1, z1), (2, b1x, *TILE), (2, b1x, *TILE)]
             + [l2] * 7 + [l2 if nw <= 16 else (1, *TILE)] + [l3] * 8 + [l4] * 7
             + [(2, 2, b1x * l0[1], nz // 2)]
-            + [half2, own2, (1, 128), (2, nn // 2 * nw, *half2), (2, nn // 2 * nw, *own2), (nn // 2 * nw, 1, 128), (1, 128), (1, 128)]
+            + [half2, own2, (1, 128), (2, nn // 2 * nw, *half2), (2, nn // 2 * nw, *own2), (nn * nw, 1, 128)]
             + [(bx // 4 + 4, 2 * y2 + 2 * b1y, z1), (3 * bx * by * nz // 1024, *TILE)]
         )
         size = sum(4 * functools.reduce(lambda p, q: p * q, shape) for shape in buffers)
         dma = lambda n: pltpu.SemaphoreType.DMA((n,))
         scratch = [pltpu.VMEM(shape, F32) for shape in buffers]
-        scratch += [dma(n) for n in (1, 8, 5, 6, 6, 4, 8, 8, 4, 2, 2)]
-        steps = (nn // 2 * nw - 1).bit_length()
+        scratch += [dma(n) for n in (1, 8, 2 if nn // 2 * nw <= 16 else 5, 5, 6, 4, 8, 8, 2)]
+        steps = (nn // 2 * nw - 1).bit_length() + 1
         scratch.append(pltpu.SemaphoreType.REGULAR((steps,)))
         return pl.pallas_call(
             functools.partial(kernel, nw, nn, bx, by, nz),

time: 27.6 us -> 27.2 us (0.986)
  Pallas kernels: 26.8 us -> 26.3 us
    pallas_call x1, Pallas kernels: 26.8 us -> 26.3 us  [per_device(): pl.pallas_call(functools.partial(kernel, nw, nn, bx, by, nz), out_shape=j...]
where the time goes in v7:
time: 27.2 us; the launch traced here: 27 us
  Pallas kernels  26.3 us (97%)
  local copies, waits for them, and re-layouts  0.71 us (3%)
    pallas_call x1, Pallas kernels, per_device(): pl.pallas_call(functools.partial(kernel, nw, nn, bx, by, nz), out_shape=j...  26.3 us
    unnamed x1, local copies, waits for them, and re-layouts  0.71 us

profile of v7, /device:TPU:1, one launch (start us, length us, event | category | flops | bytes accessed | tf_op | source)
XLA Modules:
  0.0 27.0 jit_solution(13955493856826275410)
XLA Ops:
  0.0 26.3 %shard_map.37 = f32[16,16,256]{2,1,0:T(8,128)S(1)} custom-call(f32[16,16,256]{2,1,0:T(8,128)} %m_hbm.1, f32[16,16,256]{2,1,0:T(8,128)} %s_hbm.1, f32[16,16,256]{2,1,0:T(8,128)} %c_hbm.1), custom_call_target="tpu_custom_call" | custom-call | tf_op jit(solution)/shard_map/pallas_call | solution.py:935
  26.3 0.7 %copy.5 = f32[16,16,256]{2,1,0:T(8,128)} copy(f32[16,16,256]{2,1,0:T(8,128)S(1)} %shard_map.37) | data formatting | bytes 524288

commit v8 on v7

--- a/solution.py
+++ b/solution.py
@@ -137,6 +137,17 @@
     return own, total
 
 
+class Scaled:
+    def __init__(self, rd, r, lo, hi):
+        self.rd, self.r, self.lo, self.hi, self.seen = rd, r, lo, hi, {}
+
+    def __getitem__(self, a):
+        if a not in self.seen:
+            inside = self.lo <= a < self.hi
+            self.seen[a] = self.rd[a] * self.r[a] if inside else jnp.zeros(self.r.shape[1:], F32)
+        return self.seen[a]
+
+
 def sweep(vin, vout, r, ops, lo, count, chunk):
     cx, cy, cz, rd, d = ops
 
@@ -176,7 +187,7 @@
 def kernel(nw, nn, bx, by, nz, m_hbm, s_hbm, c_hbm, out_ref,
            m_ref, s_ref, c_ref,
            m0, cx0, cy0, cz0, rd0, d0, rs0, rc0, us0, uc0, vs0, vc0,
-           rx, yp, ry, cp, rcn, xv, hx, yv, hy, xu, hu,
+           rx, yp, ry, cp, rcn, xv, hx, xc, hxc, yv, hy, xu, hu,
            m1, cx1, cy1, cz1, rd1, d1, r1, u1, v1, w1, h1, hc, cv1, cs1, cr1, cs2, cr2, qs1, qr1,
            cx2, cy2, cz2, rd2, r2, u2, v2, d2,
            cx3, cy3, cz3, rd3, r3, u3, v3, d3,
@@ -452,7 +463,7 @@
                 clear(cr1, k - 4)
                 clear(cr2, k - 4)
                 return
-            lands = ((rx, hx, hu, h1, hc) if k < 2 else (ry, hy, qr1))
+            lands = ((rx, hx, hxc, hu, h1, hc) if k < 2 else (ry, hy, qr1))
             for ref in lands:
                 clear(ref, k % 2)
             for ref, width in (((m1, 3), (r1, 2)) if k < 2 else ((m1, 3),)):
@@ -484,7 +495,6 @@
 
     ops0 = (cx0, cy0, cz0, rd0, d0)
     firsts0 = ((rs0, us0), (rc0, uc0))
-    meet(1)
     each(near_landed, (2, 3))
     m0[H0 : H0 + bx, H0 - 1, :] = ry[0, 0]
     m0[H0 : H0 + bx, H0 + by, :] = ry[1, 0]
@@ -494,6 +504,7 @@
             xu[side, v] = ref[a, H0 : H0 + by, :]
     each(lambda k: start(to_side(k, [(xu.at[k], hu.at[OPPOSITE[k]])], u0r)), (0, 1))
     each(lambda k: start(level1_sends(m1, m1r, k, 3, 0)))
+    meet(1)
     each(e0_landed, (2, 3))
     for ref, at, lo, width in ((m0, 1, 1, 2), (rs0, 3, 0, 2), (rc0, 5, 0, 2)):
         for i in range(width):
@@ -570,19 +581,18 @@
     each(lambda k: start(level1_sends(r1, r1r, k, 2, 1)), (4, 5, 6, 7, 0, 1, 2, 3))
     for side, (x_far, x_near) in enumerate(((H0 + 1, H0), (H0 + bx - 2, H0 + bx - 1))):
         for v, ref in enumerate((vs0, vc0)):
-            xv[side, v, 0:by, :] = ref[x_far, H0 : H0 + by, :]
-            xv[side, v, by : by + 1, :] = ref[x_near, H0 - 1 : H0, :]
-            xv[side, v, by + 1 : by + 2, :] = ref[x_near, H0 + by : H0 + by + 1, :]
+            xv[side, v] = ref[x_far, H0 : H0 + by, :]
+            xc[side, 2 * v] = ref[x_near, H0 - 1 : H0, :]
+            xc[side, 2 * v + 1] = ref[x_near, H0 + by : H0 + by + 1, :]
     for side, col in enumerate((H0 + 1, H0 + by - 2)):
         for v, ref in enumerate((vs0, vc0)):
             yv[side, v] = ref[H0 : H0 + bx, col, :]
 
     def v0_sends(side):
         land = OPPOSITE[side]
-        src, dst = (xv.at[side], hx.at[land]) if side < 2 else (yv.at[side - 2], hy.at[land - 2])
         if side < 2:
-            return to_side(side, [(src, dst)], e0r)
-        return [remote(src, dst, ss.at[side], y0r.at[land], peer(side))]
+            return to_side(side, [(xv.at[side], hx.at[land]), (xc.at[side], hxc.at[land])], e0r)
+        return [remote(yv.at[side - 2], hy.at[land - 2], ss.at[side], y0r.at[land], peer(side))]
 
     each(level1_landed(m1, m1r, 3, 0))
     for k in range(4, 8):
@@ -731,7 +741,7 @@
 
 
     def v0_landed(side):
-        view = hx.at[side] if side < 2 else hy.at[side - 2]
+        view = tok.at[0 : (2 * by + 4) * nz // 1024] if side < 2 else hy.at[side - 2]
         pltpu.make_async_copy(view, view, e0r.at[side] if side < 2 else y0r.at[side]).wait()
 
     landed(gr.at[0], 3)
@@ -768,15 +778,21 @@
     def first3(a):
         u3[a] = rd3[a] * r3[a]
 
-    slabs(PAD2, x3, 16, first3)
-    sweep((u3,), (v3,), (r3,), ops3, PAD2, x3, 16)
+    if x3 <= 16:
+        sweep((Scaled(rd3, r3, PAD2, PAD2 + x3),), (v3,), (r3,), ops3, PAD2, x3, 16)
+    else:
+        slabs(PAD2, x3, 16, first3)
+        sweep((u3,), (v3,), (r3,), ops3, PAD2, x3, 16)
     num3, den3 = coarsen_residual(v3, r3, ops3, r4, x4, PAD, z2 // 2)
 
     def first4(a):
         u4[a] = rd4[a] * r4[a]
 
-    slabs(PAD, x4, 8, first4)
-    sweep((u4,), (v4,), (r4,), ops4, PAD, x4, 8)
+    if x4 <= 8:
+        sweep((Scaled(rd4, r4, PAD, PAD + x4),), (v4,), (r4,), ops4, PAD, x4, 8)
+    else:
+        slabs(PAD, x4, 8, first4)
+        sweep((u4,), (v4,), (r4,), ops4, PAD, x4, 8)
     low4 = iota(TILE, 1) < z2 // 4
 
     def dots(i, carry):
@@ -845,9 +861,9 @@
     each(v0_landed, range(4))
     for side, (x_far, x_near) in enumerate(((H0 - 2, H0 - 1), (H0 + bx + 1, H0 + bx))):
         for v, ref in enumerate((vs0, vc0)):
-            ref[x_far, H0 : H0 + by, :] = hx[side, v, 0:by, :]
-            ref[x_near, H0 - 1 : H0, :] = hx[side, v, by : by + 1, :]
-            ref[x_near, H0 + by : H0 + by + 1, :] = hx[side, v, by + 1 : by + 2, :]
+            ref[x_far, H0 : H0 + by, :] = hx[side, v]
+            ref[x_near, H0 - 1 : H0, :] = hxc[side, 2 * v]
+            ref[x_near, H0 + by : H0 + by + 1, :] = hxc[side, 2 * v + 1]
     for side, col in enumerate((H0 - 2, H0 + by + 1)):
         for v, ref in enumerate((vs0, vc0)):
             ref[H0 : H0 + bx, col, :] = hy[side, v]
@@ -883,7 +899,7 @@
     def sent(side):
         dx, dy = SIDES[side]
         if dy == 0:
-            tiles = 6 * by * nz // 1024 + 3 + 4 + 2 * (by + 8) * nz // 1024 + 10
+            tiles = 6 * by * nz // 1024 + 3 + 4 + (2 * by + 4) * nz // 1024 + 10
         elif dx == 0:
             tiles = 7 * bx * nz // 1024 + b1x + b1x + 2 * bx * nz // 1024
         else:
@@ -919,7 +935,7 @@
         buffers = (
             [own] * 3 + [l0] * 12
             + [(2, 4, by, nz), (2, 7, bx, nz), (2, 7, bx, nz), (4, 5, 1, nz), (4, 5, 1, nz)]
-            + [(2, 2, by + 8, nz)] * 2 + [(2, 2, bx, nz)] * 2 + [(2, 2, by, nz)] * 2
+            + [(2, 2, by, nz)] * 2 + [(2, 4, 1, nz)] * 2 + [(2, 2, bx, nz)] * 2 + [(2, 2, by, nz)] * 2
             + [(1, *l1)] + [l1] * 5 + [(2, *l1)] * 3 + [l1] + [(2, 2, 3, b1y, z1), (2, 2, 2, b1y, z1), (2, 2, 2, b1y, z1), (4, *TILE), (4, *TILE), (4, 6, 1, z1), (4, 6, 1, z1), (2, b1x, *TILE), (2, b1x, *TILE)]
             + [l2] * 7 + [l2 if nw <= 16 else (1, *TILE)] + [l3] * 8 + [l4] * 7
             + [(2, 2, b1x * l0[1], nz // 2)]

time: 27.2 us -> 27.1 us (level)
  no operation moved by 1% of the time
where the time goes in v8:
time: 27.1 us; the launch traced here: 27 us
  Pallas kernels  26.3 us (97%)
  local copies, waits for them, and re-layouts  0.71 us (3%)
    pallas_call x1, Pallas kernels, per_device(): pl.pallas_call(functools.partial(kernel, nw, nn, bx, by, nz), out_shape=j...  26.3 us
    unnamed x1, local copies, waits for them, and re-layouts  0.71 us

profile of v8, /device:TPU:1, one launch (start us, length us, event | category | flops | bytes accessed | tf_op | source)
XLA Modules:
  0.0 27.0 jit_solution(7687627322296890074)
XLA Ops:
  0.0 26.3 %shard_map.37 = f32[16,16,256]{2,1,0:T(8,128)S(1)} custom-call(f32[16,16,256]{2,1,0:T(8,128)} %m_hbm.1, f32[16,16,256]{2,1,0:T(8,128)} %s_hbm.1, f32[16,16,256]{2,1,0:T(8,128)} %c_hbm.1), custom_call_target="tpu_custom_call" | custom-call | tf_op jit(solution)/shard_map/pallas_call | solution.py:951
  26.3 0.7 %copy.5 = f32[16,16,256]{2,1,0:T(8,128)} copy(f32[16,16,256]{2,1,0:T(8,128)S(1)} %shard_map.37) | data formatting | bytes 524288

commit v9 on v8

--- a/solution.py
+++ b/solution.py
@@ -495,6 +495,7 @@
 
     ops0 = (cx0, cy0, cz0, rd0, d0)
     firsts0 = ((rs0, us0), (rc0, uc0))
+    meet(1)
     each(near_landed, (2, 3))
     m0[H0 : H0 + bx, H0 - 1, :] = ry[0, 0]
     m0[H0 : H0 + bx, H0 + by, :] = ry[1, 0]
@@ -504,7 +505,6 @@
             xu[side, v] = ref[a, H0 : H0 + by, :]
     each(lambda k: start(to_side(k, [(xu.at[k], hu.at[OPPOSITE[k]])], u0r)), (0, 1))
     each(lambda k: start(level1_sends(m1, m1r, k, 3, 0)))
-    meet(1)
     each(e0_landed, (2, 3))
     for ref, at, lo, width in ((m0, 1, 1, 2), (rs0, 3, 0, 2), (rc0, 5, 0, 2)):
         for i in range(width):

time: 27.1 us -> 27.2 us (level)
  no operation moved by 1% of the time
where the time goes in v9:
time: 27.2 us; the launch traced here: 27 us
  Pallas kernels  26.3 us (97%)
  local copies, waits for them, and re-layouts  0.71 us (3%)
    pallas_call x1, Pallas kernels, per_device(): pl.pallas_call(functools.partial(kernel, nw, nn, bx, by, nz), out_shape=j...  26.3 us
    unnamed x1, local copies, waits for them, and re-layouts  0.71 us

profile of v9, /device:TPU:1, one launch (start us, length us, event | category | flops | bytes accessed | tf_op | source)
XLA Modules:
  0.0 27.0 jit_solution(3631411843307490432)
XLA Ops:
  0.0 26.3 %shard_map.37 = f32[16,16,256]{2,1,0:T(8,128)S(1)} custom-call(f32[16,16,256]{2,1,0:T(8,128)} %m_hbm.1, f32[16,16,256]{2,1,0:T(8,128)} %s_hbm.1, f32[16,16,256]{2,1,0:T(8,128)} %c_hbm.1), custom_call_target="tpu_custom_call" | custom-call | tf_op jit(solution)/shard_map/pallas_call | solution.py:951
  26.3 0.7 %copy.5 = f32[16,16,256]{2,1,0:T(8,128)} copy(f32[16,16,256]{2,1,0:T(8,128)S(1)} %shard_map.37) | data formatting | bytes 524288
